TPU v7x, 32 devices: a whole 2x2x4 slice. The times are simulated.
32 devices in a mesh: rep: 2 (over core), exp: 16 (over z, y, x).
Axes of the slice: x: 2, y: 2, z: 4, core: 2. Of those that a mesh axis runs over, the one named last changes fastest.
Arguments:
- tokens: bfloat16 [4096, 4096], P(('rep', 'exp')), may hold values from -6 to 6
- expert_ids: int32 [4096, 8], P(('rep', 'exp')), may hold values from 0 to 15, all different within a row; in each aligned block of 128 rows (0 to 127, 128 to 255, ...) at most 72 rows name the same one
- route_weights: bfloat16 [4096, 8], P(('rep', 'exp')), may hold values from 0.099609375 to 1
- cotangent: bfloat16 [4096, 4096], P(('rep', 'exp')), may hold values from -0.3984375 to 0.3984375
- w_gate: bfloat16 [16, 4096, 768], P('exp'), may hold values from -0.09375 to 0.09375
- w_up: bfloat16 [16, 4096, 768], P('exp'), may hold values from -0.09375 to 0.09375
- w_down: bfloat16 [16, 768, 4096], P('exp'), may hold values from -0.21875 to 0.21875
- ia3_scale: float32 [16, 768], P('exp'), may hold values from 0.25 to 1.75
Outputs:
- mixed: bfloat16 [4096, 4096], P(('rep', 'exp'))
- ia3_grad: float32 [16, 768], P('exp')
Inputs may be any that keep to these rules, and one draw needn't show every extreme that they name: `expert_ids`: among the choices of one device's 128 tokens, no expert is named more than 72 times, a bound that some block reaches; a token names 8 different experts.
All inputs are finite; a program needn't handle non-finite values.
Results may differ from a plain program's by a relative error of at most 0.0057.
Values may be sent and summed in bfloat16 or wider, within the bound.
No kernel may reach another device: no remote copies, remote signals or barrier semaphores. Data moves between devices by JAX's collectives and lax.ppermute only.
A program may use at most 192 MiB of HBM per device.

v0:
```python
import jax
import jax.numpy as jnp
from jax import lax
from jax.sharding import PartitionSpec as P


def shards(tokens, expert_ids, route_weights, cotangent, w_gate, w_up, w_down, ia3_scale):
    owners = lax.axis_size("exp")
    tok_rows, model_width = tokens.shape
    per_token = expert_ids.shape[1]
    capacity = tok_rows * per_token // owners + tok_rows * per_token // (8 * owners)
    flat_ids = expert_ids.reshape(-1)
    one_hot = (flat_ids[:, None] == jnp.arange(owners, dtype=jnp.int32)[None, :]).astype(jnp.int32)
    before = jnp.cumsum(one_hot, axis=0) - one_hot
    slot_index = jnp.sum(before * one_hot, axis=1)
    source_row = jnp.arange(tok_rows * per_token, dtype=jnp.int32) // per_token

    def into_slots(values):
        empty = jnp.zeros((owners, capacity) + values.shape[1:], values.dtype)
        return empty.at[flat_ids, slot_index].set(values)

    token_send = into_slots(tokens[source_row])
    weight_send = into_slots(route_weights.reshape(-1))
    token_recv, weight_recv = (
        lax.all_to_all(token_send, "exp", split_axis=0, concat_axis=0, tiled=True),
        lax.all_to_all(weight_send, "exp", split_axis=0, concat_axis=0, tiled=True),
    )
    received_rows = token_recv.reshape(-1, model_width)
    gate_pre = jnp.dot(received_rows, w_gate[0], preferred_element_type=jnp.float32)
    up_pre = jnp.dot(received_rows, w_up[0], preferred_element_type=jnp.float32)
    activated = jax.nn.silu(gate_pre) * up_pre
    hidden = (ia3_scale[0][None, :] * activated).astype(jnp.bfloat16)
    expert_out = jnp.dot(hidden, w_down[0], preferred_element_type=jnp.float32).astype(jnp.bfloat16)
    returned = lax.all_to_all(
        expert_out.reshape(owners, capacity, model_width),
        "exp",
        split_axis=0,
        concat_axis=0,
        tiled=True,
    )
    picked = returned[flat_ids, slot_index].reshape(tok_rows, per_token, model_width)
    mixed = jnp.einsum(
        "tkd,tk->td", picked, route_weights, preferred_element_type=jnp.float32
    ).astype(jnp.bfloat16)
    grad_send = into_slots(cotangent[source_row])
    grad_recv = lax.all_to_all(grad_send, "exp", split_axis=0, concat_axis=0, tiled=True)
    back_proj = lax.dot_general(
        grad_recv.reshape(-1, model_width),
        w_down[0],
        (((1,), (1,)), ((), ())),
        preferred_element_type=jnp.float32,
    )
    weight_rows = weight_recv.reshape(-1).astype(jnp.float32)
    local_grad = jnp.sum(weight_rows[:, None] * activated * back_proj, axis=0)
    summed = lax.psum(local_grad, "rep")
    return (mixed, summed[None, :])


def solution(mesh):
    in_specs = (
        P(("rep", "exp"), None),
        P(("rep", "exp"), None),
        P(("rep", "exp"), None),
        P(("rep", "exp"), None),
        P("exp", None, None),
        P("exp", None, None),
        P("exp", None, None),
        P("exp", None),
    )
    out_specs = (P(("rep", "exp"), None), P("exp", None))
    return jax.shard_map(shards, mesh=mesh, in_specs=in_specs, out_specs=out_specs, check_vma=False)
```

profile of v0, /device:TPU:12, one launch (start us, length us, event | category | flops | bytes accessed | tf_op | source)
XLA Modules:
  0.0 740.8 jit_solution(9610862103730349479)
XLA Ops:
  0.6 0.9 copy.18
  1.5 0.1 eq.29
  1.7 0.1 reshape.134
  1.8 4.5 reduce-window.6
  6.4 0.1 copy.21
  6.8 0.7 multiply_reduce_fusion
  7.6 0.8 and_reduce_fusion
  8.3 0.8 copy.23
  9.1 0.1 reshape.185
  9.2 7.6 %scatter_custom_fusion.1 = bf16[1152]{0:T(1024)(128)(2,1)S(1)} fusion(s32[1024]{0:T(1024)S(1)} %broadcast_select_fusion, bf16[1024]{0:T(1024)(128)(2,1)S(1)} %reshape.185, bf16[]{:T(256)} %constant.27.clone.1), kind=kCustom, calls=%fused_computation.47 | custom fusion | bytes 2306
  16.8 0.7 all_to_all.20
  17.5 7.4 %all-to-all-start.2 = ((bf16[16,1,72]{2,1,0:T(2,128)(2,1)}), bf16[16,1,72]{2,1,0:T(2,128)(2,1)S(1)}, u32[]{:S(2)}, u32[]{:S(2)}) async-start(bf16[16,1,72]{2,1,0:T(2,128)(2,1)} %all_to_all.20), calls=%async_computation.2 | async-start | bytes 16384 | tf_op jit(solution)/shard_map/all_to_all | solution.py:26
  25.0 7.7 %gather_fusion = bf16[1024,4096]{1,0:T(8,128)(2,1)} fusion(bf16[128,4096]{1,0:T(8,128)(2,1)S(1)} %copy-done, s32[1024]{0:T(1024)S(1)} %broadcast_clamp_fusion), kind=kCustom, calls=%fused_computation | custom fusion | bytes 16781312 | tf_op jit(solution)/shard_map/gather | solution.py:22
  32.7 18.3 %scatter_custom_fusion = bf16[1152,4096]{1,0:T(8,128)(2,1)} fusion(s32[1024]{0:T(1024)S(1)} %broadcast_select_fusion, bf16[1024,4096]{1,0:T(8,128)(2,1)} %gather_fusion, bf16[]{:T(256)} %constant.27.clone.1), kind=kCustom, calls=%fused_computation.18 | custom fusion | bytes 9437696
  51.1 7.4 all-to-all-start
  58.5 7.7 %gather_fusion.2 = bf16[1024,4096]{1,0:T(8,128)(2,1)} fusion(bf16[128,4096]{1,0:T(8,128)(2,1)S(1)} %copy-done.2, s32[1024]{0:T(1024)S(1)} %broadcast_clamp_fusion), kind=kCustom, calls=%fused_computation.2 | custom fusion | bytes 16781312 | tf_op jit(solution)/shard_map/gather | solution.py:45
  66.2 18.2 %scatter_custom_fusion.2 = bf16[1152,4096]{1,0:T(8,128)(2,1)} fusion(s32[1024]{0:T(1024)S(1)} %broadcast_select_fusion, bf16[1024,4096]{1,0:T(8,128)(2,1)} %gather_fusion.2, bf16[]{:T(256)} %constant.27.clone.1), kind=kCustom, calls=%fused_computation.16 | custom fusion | bytes 9437696
  84.4 185.3 %all-to-all-done = bf16[16,72,4096]{2,1,0:T(8,128)(2,1)} async-done(((bf16[16,72,4096]{2,1,0:T(8,128)(2,1)}), bf16[16,72,4096]{2,1,0:T(8,128)(2,1)}, u32[]{:S(2)}, u32[]{:S(2)}) %all-to-all-start) | async-done | bytes 9437216 | tf_op jit(solution)/shard_map/all_to_all | solution.py:25
  269.7 8.2 %all-to-all-start.3 = ((bf16[16,72,4096]{2,1,0:T(8,128)(2,1)}), bf16[16,72,4096]{2,1,0:T(8,128)(2,1)}, u32[]{:S(2)}, u32[]{:S(2)}) async-start(bf16[16,72,4096]{2,1,0:T(8,128)(2,1)} %bitcast.55), calls=%async_computation.3 | async-start | bytes 18874368 | tf_op jit(solution)/shard_map/all_to_all | solution.py:46
  277.9 12.0 %fusion.7 = f32[1152,768]{1,0:T(8,128)S(1)} fusion(bf16[1152,4096]{1,0:T(8,128)(2,1)} %bitcast.5, bf16[1,4096,768]{2,1,0:T(8,128)(2,1)} %param.12), kind=kOutput, calls=%fused_computation.14 | convolution fusion | flops 7247757312 | bytes 19267584 | tf_op jit(solution)/shard_map/dot_general | solution.py:29
  290.0 12.2 %fusion.13 = f32[1152,768]{1,0:T(8,128)S(1)} fusion(bf16[1152,4096]{1,0:T(8,128)(2,1)} %bitcast.5, bf16[1,4096,768]{2,1,0:T(8,128)(2,1)} %param.13, f32[1152,768]{1,0:T(8,128)S(1)} %fusion.7), kind=kOutput, calls=%fused_computation.20 | convolution fusion | flops 7252180992 | bytes 22806528 | tf_op jit(solution)/shard_map/dot_general | solution.py:30
  302.2 1.9 copy-done.5
  304.1 9.6 %convolution_convert_fusion = bf16[1152,4096]{1,0:T(8,128)(2,1)} fusion(bf16[1,768,4096]{2,1,0:T(8,128)(2,1)S(1)} %bitcast.65, f32[1152,768]{1,0:T(8,128)S(1)} %fusion.13, f32[768]{0:T(1024)S(1)} %reduce.6), kind=kOutput, calls=%fused_computation.6 | convolution fusion | flops 7254245376 | bytes 19270656 | tf_op jit(solution)/shard_map/dot_general | solution.py:33
  313.7 171.5 %all-to-all-done.3 = bf16[16,72,4096]{2,1,0:T(8,128)(2,1)} async-done(((bf16[16,72,4096]{2,1,0:T(8,128)(2,1)}), bf16[16,72,4096]{2,1,0:T(8,128)(2,1)}, u32[]{:S(2)}, u32[]{:S(2)}) %all-to-all-start.3) | async-done | bytes 9437216 | tf_op jit(solution)/shard_map/all_to_all | solution.py:46
  485.2 8.6 %all-to-all-start.1 = ((bf16[16,72,4096]{2,1,0:T(8,128)(2,1)}), bf16[16,72,4096]{2,1,0:T(8,128)(2,1)}, u32[]{:S(2)}, u32[]{:S(2)}) async-start(bf16[16,72,4096]{2,1,0:T(8,128)(2,1)} %bitcast.57), calls=%async_computation.1 | async-start | bytes 18874368 | tf_op jit(solution)/shard_map/all_to_all | solution.py:34
  493.7 0.1 copy.25
  494.0 12.5 %fusion.20 = f32[768]{0:T(1024)S(1)} fusion(bf16[1152,4096]{1,0:T(8,128)(2,1)} %bitcast.15, bf16[1,768,4096]{2,1,0:T(8,128)(2,1)} %param.14, f32[1152,768]{1,0:T(8,128)} %copy-done.5, f32[1152]{0:T(1024)S(1)} %reshape.154), kind=kOutput, calls=%fused_computation.25 | convolution fusion | flops 7250410496 | bytes 19275264 | tf_op jit(solution)/shard_map/dot_general | solution.py:47
  506.5 3.2 psum.7
  509.7 188.7 %all-to-all-done.1 = bf16[16,72,4096]{2,1,0:T(8,128)(2,1)} async-done(((bf16[16,72,4096]{2,1,0:T(8,128)(2,1)}), bf16[16,72,4096]{2,1,0:T(8,128)(2,1)}, u32[]{:S(2)}, u32[]{:S(2)}) %all-to-all-start.1) | async-done | bytes 9437216 | tf_op jit(solution)/shard_map/all_to_all | solution.py:34
  698.5 34.4 %gather_fusion.1 = bf16[1024,4096]{1,0:T(8,128)(2,1)} fusion(bf16[16,72,4096]{2,1,0:T(8,128)(2,1)} %all-to-all-done.1, s32[1024]{0:T(1024)S(1)} %bitcast.54), kind=kCustom, calls=%fused_computation.1 | custom fusion | bytes 16785408 | tf_op jit(solution)/shard_map/gather | solution.py:41
  732.8 5.7 fusion
  738.5 2.1 copy.30
  (33 shorter events, 0.6 us)
Async XLA Ops:
  0.6 24.4 %copy-start = (bf16[128,4096]{1,0:T(8,128)(2,1)S(1)}, bf16[128,4096]{1,0:T(8,128)(2,1)}, u32[]{:S(2)}) copy-start(bf16[128,4096]{1,0:T(8,128)(2,1)} %param.8) | copy-start | bytes 3145732
  17.5 33.5 %all-to-all-start.2 = ((bf16[16,1,72]{2,1,0:T(2,128)(2,1)}), bf16[16,1,72]{2,1,0:T(2,128)(2,1)S(1)}, u32[]{:S(2)}, u32[]{:S(2)}) async-start(bf16[16,1,72]{2,1,0:T(2,128)(2,1)} %all_to_all.20), calls=%async_computation.2 | async-start | bytes 16384 | tf_op jit(solution)/shard_map/all_to_all | solution.py:26
  51.1 7.4 %copy-start.2 = (bf16[128,4096]{1,0:T(8,128)(2,1)S(1)}, bf16[128,4096]{1,0:T(8,128)(2,1)}, u32[]{:S(2)}) copy-start(bf16[128,4096]{1,0:T(8,128)(2,1)} %param.11) | copy-start | bytes 3145732
  51.1 218.6 %all-to-all-start = ((bf16[16,72,4096]{2,1,0:T(8,128)(2,1)}), bf16[16,72,4096]{2,1,0:T(8,128)(2,1)}, u32[]{:S(2)}, u32[]{:S(2)}) async-start(bf16[16,72,4096]{2,1,0:T(8,128)(2,1)} %bitcast.56), calls=%async_computation | async-start | bytes 18874368 | tf_op jit(solution)/shard_map/all_to_all | solution.py:25
  269.7 8.2 %copy-start.4 = (f32[1,768]{1,0:T(1,128)S(1)}, f32[1,768]{1,0:T(1,128)}, u32[]{:S(2)}) copy-start(f32[1,768]{1,0:T(1,128)} %param.15) | copy-start | bytes 9220
  269.7 215.5 %all-to-all-start.3 = ((bf16[16,72,4096]{2,1,0:T(8,128)(2,1)}), bf16[16,72,4096]{2,1,0:T(8,128)(2,1)}, u32[]{:S(2)}, u32[]{:S(2)}) async-start(bf16[16,72,4096]{2,1,0:T(8,128)(2,1)} %bitcast.55), calls=%async_computation.3 | async-start | bytes 18874368 | tf_op jit(solution)/shard_map/all_to_all | solution.py:46
  277.9 26.2 %slice-start = ((s8[6291456]{0:T(1024)(128)(4,1)}), s8[4194304]{0:T(1024)(128)(4,1)S(1)}, s32[]{:S(2)}) async-start(s8[6291456]{0:T(1024)(128)(4,1)} %bitcast.64), calls=%async_computation.4 | async-start | bytes 8388608
  290.0 14.1 %slice-start.1 = ((s8[6291456]{0:T(1024)(128)(4,1)}), s8[2097152]{0:T(1024)(128)(4,1)S(1)}, s32[]{:S(2)}) async-start(s8[6291456]{0:T(1024)(128)(4,1)} %bitcast.64), calls=%async_computation.5 | async-start | bytes 4194304
  302.2 1.9 copy-start.5
  485.2 8.6 %copy-start.3 = (bf16[128,8]{0,1:T(8,128)(2,1)S(1)}, bf16[128,8]{0,1:T(8,128)(2,1)}, u32[]{:S(2)}) copy-start(bf16[128,8]{0,1:T(8,128)(2,1)} %param.10) | copy-start | bytes 6148
  485.2 213.3 %all-to-all-start.1 = ((bf16[16,72,4096]{2,1,0:T(8,128)(2,1)}), bf16[16,72,4096]{2,1,0:T(8,128)(2,1)}, u32[]{:S(2)}, u32[]{:S(2)}) async-start(bf16[16,72,4096]{2,1,0:T(8,128)(2,1)} %bitcast.57), calls=%async_computation.1 | async-start | bytes 18874368 | tf_op jit(solution)/shard_map/all_to_all | solution.py:34
  698.4 42.2 %copy-start.1 = (bf16[128,4096]{1,0:T(8,128)(2,1)S(1)}, bf16[128,4096]{1,0:T(8,128)(2,1)}, u32[]{:S(2)}) copy-start(bf16[128,4096]{1,0:T(8,128)(2,1)} %param.8) | copy-start | bytes 3145732
where the time goes:
time: 746 us; the launch traced here: 741 us
  waiting for transfers between devices  545 us (73%)
  local copies, waits for them, and re-layouts  101 us (14%)
  matrix products  52 us (7%)
  starting transfers between devices  31.6 us (4%)
    all_to_all x1, waiting for transfers between devices, shards(): lax.all_to_all(expert_out.reshape(owners, capacity, model_width), 'exp',...  189 us
    all_to_all x1, waiting for transfers between devices, shards(): lax.all_to_all(token_send, 'exp', split_axis=0, concat_axis=0, tiled=True)  185 us
    all_to_all x1, waiting for transfers between devices, shards(): lax.all_to_all(grad_send, 'exp', split_axis=0, concat_axis=0, tiled=True)  171 us
    unnamed x22, local copies, waits for them, and re-layouts  47.9 us
    gather x1, local copies, waits for them, and re-layouts, shards(): returned[flat_ids, slot_index].reshape(tok_rows, per_token, model_width)  34.4 us
  transfers between devices with their start and end apart: 4, of which 3 were waited for; matrix products, arithmetic and copies ran while one was open for 13% of the time, Pallas kernels for 0%

commit v1 on v0

--- a/solution.py
+++ b/solution.py
@@ -1,10 +1,520 @@
+import functools
+import math
+
 import jax
 import jax.numpy as jnp
 from jax import lax
+from jax.experimental import pallas as pl
+from jax.experimental.pallas import tpu as pltpu
 from jax.sharding import PartitionSpec as P
 
-
-def shards(tokens, expert_ids, route_weights, cotangent, w_gate, w_up, w_down, ia3_scale):
+PIECES = (2, 1)
+SHARES = (3, 3, 2)
+SLOTS = 3
+LANES = 128
+EARLY = 2
+F32 = jnp.float32
+BF16 = jnp.bfloat16
+VMEM_LIMIT = 60 * 1024 * 1024
+
+
+def ring_order(members):
+    return list(range(0, members, 2)) + list(reversed(range(1, members, 2)))
+
+
+def ring_perm(members, step):
+    order = ring_order(members)
+    perm = []
+    for parity in range(2):
+        for place, member in enumerate(order):
+            target = order[(place + step) % members]
+            perm.append((2 * member + parity, 2 * target + parity))
+    return perm
+
+
+def bounds_of(width, shares):
+    edges = [0]
+    for share in shares:
+        edges.append(edges[-1] + width * share // sum(shares))
+    return list(zip(edges[:-1], edges[1:]))
+
+
+def whole(shape):
+    return pl.BlockSpec(shape, lambda *_: (0,) * len(shape))
+
+
+def params():
+    return pltpu.CompilerParams(vmem_limit_bytes=VMEM_LIMIT)
+
+
+def cost(flops, *arrays):
+    moved = sum(math.prod(a.shape) * a.dtype.itemsize for a in arrays)
+    return pl.CostEstimate(flops=flops, transcendentals=0, bytes_accessed=moved)
+
+
+def cut_columns(core, w_gate, w_up, low, high):
+    depth, units = w_gate.shape
+    per_half, tiles = units // 2 // LANES, (high - low) // LANES
+    step = math.gcd(depth, 1024)
+
+    def body(core_ref, *refs):
+        out_ref = refs[-1]
+        for n, ref in enumerate(refs[:-1]):
+            out_ref[:, n * LANES : (n + 1) * LANES] = ref[...]
+
+    specs = [
+        pl.BlockSpec((step, LANES), lambda i, core_ref, n=n: (i, core_ref[0] * per_half + low // LANES + n))
+        for n in range(tiles)
+    ]
+    out = jax.ShapeDtypeStruct((depth, 2 * (high - low)), w_gate.dtype)
+    return pl.pallas_call(
+        body,
+        out_shape=out,
+        grid_spec=pltpu.PrefetchScalarGridSpec(
+            num_scalar_prefetch=1,
+            grid=(depth // step,),
+            in_specs=specs + specs,
+            out_specs=pl.BlockSpec((step, 2 * (high - low)), lambda i, core_ref: (i, 0)),
+        ),
+        cost_estimate=cost(0, out, out),
+        name="cut_columns",
+    )(core, *[w_gate] * tiles, *[w_up] * tiles)
+
+
+def cut_rows(core, w_down, bounds):
+    half, width = w_down.shape[0] // 2, w_down.shape[1]
+    step = half // 3 if half % 48 == 0 else half
+
+    def body(core_ref, in_ref, *out_refs):
+        for (low, high), out_ref in zip(bounds, out_refs):
+            out_ref[...] = in_ref[:, low:high]
+
+    outs = [jax.ShapeDtypeStruct((half, high - low), w_down.dtype) for low, high in bounds]
+    return pl.pallas_call(
+        body,
+        out_shape=outs,
+        grid_spec=pltpu.PrefetchScalarGridSpec(
+            num_scalar_prefetch=1,
+            grid=(half // step,),
+            in_specs=[pl.BlockSpec((step, width), lambda i, core_ref: (core_ref[0] * (half // step) + i, 0))],
+            out_specs=[pl.BlockSpec((step, high - low), lambda i, core_ref: (i, 0)) for low, high in bounds],
+        ),
+        cost_estimate=cost(0, *outs, *outs),
+        name="cut_rows",
+    )(core, w_down)
+
+
+def contract(blocks, groups, transposed, extras, outs, finish):
+    starts = [0]
+    for block in blocks:
+        starts.append(starts[-1] + block.shape[0])
+    rows, width = starts[-1], blocks[0].shape[1]
+    step = math.gcd(512, width)
+    arrays, copies_of, sizes = [], [], []
+    for parts in groups:
+        size = 0
+        for segments, take, place in parts:
+            at = 0
+            for array, length in segments:
+                if not any(array is other for other in arrays):
+                    arrays.append(array)
+                index = next(i for i, other in enumerate(arrays) if other is array)
+                assert length % step == 0
+                copies_of.append((len(sizes), index, at // step, length // step, take, place))
+                at += length
+            size = max(size, place + take.stop - take.start)
+        sizes.append(size)
+    steps = width // step
+    count, parts_count = len(blocks), len(copies_of)
+    slots = min(SLOTS, steps)
+
+    def body(*refs):
+        block_refs, refs = refs[:count], refs[count:]
+        array_refs, refs = refs[: len(arrays)], refs[len(arrays) :]
+        extra_refs, refs = refs[: len(extras)], refs[len(extras) :]
+        out_refs, refs = refs[: len(outs)], refs[len(outs) :]
+        held, sems, weight_sems, refs = refs[0], refs[1], refs[2], refs[3:]
+        weight_refs, totals = refs[: len(sizes)], refs[len(sizes) :]
+        k = pl.program_id(0)
+
+        def block_copies(at, slot):
+            columns = pl.ds(pl.multiple_of(at * step, step), step)
+            return [
+                pltpu.make_async_copy(
+                    ref.at[:, columns],
+                    held.at[slot, pl.ds(starts[i], blocks[i].shape[0]), :],
+                    sems.at[slot, i],
+                )
+                for i, ref in enumerate(block_refs)
+            ]
+
+        def weight_copy(part, at, slot):
+            j, index, first, _, take, place = copies_of[part]
+            along = pl.ds(pl.multiple_of((at - first) * step, step), step)
+            across = pl.ds(take.start, take.stop - take.start)
+            there = pl.ds(place, take.stop - take.start)
+            if transposed:
+                source, target = array_refs[index].at[across, along], weight_refs[j].at[slot, there, :]
+            else:
+                source, target = array_refs[index].at[along, across], weight_refs[j].at[slot, :, there]
+            return pltpu.make_async_copy(source, target, weight_sems.at[slot, part])
+
+        def each(at, slot, do):
+            for copy in block_copies(at, slot):
+                do(copy)
+            for part, (_, _, first, length, _, _) in enumerate(copies_of):
+                if length == steps:
+                    do(weight_copy(part, at, slot))
+                else:
+
+                    @pl.when((at >= first) & (at < first + length))
+                    def _():
+                        do(weight_copy(part, at, slot))
+
+        slot = lax.rem(k, slots)
+
+        @pl.when(k == 0)
+        def _():
+            for early in range(slots - 1):
+                each(early, early, lambda copy: copy.start())
+
+        @pl.when(k + slots - 1 < steps)
+        def _():
+            each(k + slots - 1, lax.rem(k + slots - 1, slots), lambda copy: copy.start())
+
+        each(k, slot, lambda copy: copy.wait())
+        dims = (((1,), (1 if transposed else 0,)), ((), ()))
+
+        def product(j):
+            return lax.dot_general(held[slot], weight_refs[j][slot], dims, preferred_element_type=F32)
+
+        @pl.when(k == 0)
+        def _():
+            for j, total in enumerate(totals):
+                total[...] = product(j)
+
+        @pl.when(k > 0)
+        def _():
+            for j, total in enumerate(totals):
+                total[...] += product(j)
+
+        @pl.when(k == steps - 1)
+        def _():
+            finish(totals, extra_refs, out_refs)
+
+    specs = [pl.BlockSpec(memory_space=pl.ANY)] * (count + len(arrays))
+    specs += [pl.BlockSpec(a.shape, lambda k: (0, 0), pipeline_mode=pl.Buffered(1)) for a in extras]
+    dtype = blocks[0].dtype
+    return pl.pallas_call(
+        body,
+        out_shape=outs,
+        grid=(steps,),
+        in_specs=specs,
+        out_specs=[whole(out.shape) for out in outs],
+        scratch_shapes=[
+            pltpu.VMEM((slots, rows, step), dtype),
+            pltpu.SemaphoreType.DMA((slots, count)),
+            pltpu.SemaphoreType.DMA((slots, parts_count)),
+            *[pltpu.VMEM((slots, size, step) if transposed else (slots, step, size), dtype) for size in sizes],
+            *[pltpu.VMEM((rows, size), F32) for size in sizes],
+        ],
+        compiler_params=params(),
+        cost_estimate=cost(2 * rows * sum(sizes) * width, *outs),
+    )(*blocks, *arrays, *extras)
+
+
+def silu(v):
+    return v / (1.0 + jnp.exp(-v))
+
+
+def finish_own(totals, extra_refs, out_refs):
+    act = silu(totals[0][...]) * totals[1][...]
+    out_refs[0][...] = (extra_refs[0][...] * act).astype(BF16)
+
+
+def finish_pair(totals, extra_refs, out_refs):
+    total = totals[0]
+    size = total.shape[1] // 4
+    for side in range(2):
+        gate, up = total[:, 2 * side * size : (2 * side + 1) * size], total[:, (2 * side + 1) * size : (2 * side + 2) * size]
+        columns = slice(side * size, (side + 1) * size)
+        out_refs[0][:, columns] = (extra_refs[0][:, columns] * (silu(gate) * up)).astype(BF16)
+
+
+def finish_grad(span, totals, extra_refs, out_refs):
+    weight, scale, hiddens = extra_refs[0], extra_refs[1], extra_refs[2:]
+    first = 0
+    for hidden in hiddens:
+        columns = slice(first, first + hidden.shape[1])
+        term = weight[...] * hidden[span, :].astype(F32) * totals[0][:, columns]
+        out_refs[0][:, columns] = jnp.sum(term, axis=0, keepdims=True) / scale[:, columns]
+        first += hidden.shape[1]
+
+
+def both_out(owns, pairs, takes, w_down, mine, other, weights, low, split):
+    rows = sum(own.shape[0] for own in owns)
+    units = w_down.shape[0]
+    width = mine.shape[1]
+    step = math.gcd(math.gcd(low, width), 512)
+
+    def body(*refs):
+        own_refs, refs = refs[: len(owns)], refs[len(owns) :]
+        pair_refs, refs = refs[: len(pairs)], refs[len(pairs) :]
+        w_ref, mine_ref, other_ref, weight_own, weight_pair, out_ref, near_ref, far_ref, hidden = refs
+
+        @pl.when(pl.program_id(0) == 0)
+        def _():
+            done = 0
+            for ref in own_refs:
+                hidden[0, done : done + ref.shape[0], :] = ref[...]
+                done += ref.shape[0]
+            done = 0
+            for ref in pair_refs:
+                hidden[1, :, done : done + ref.shape[1]] = ref[...]
+                done += ref.shape[1]
+
+        w = jnp.concatenate([ref[take, :] for take in takes for ref in (mine_ref, other_ref)], axis=0)
+        total = weight_own[...] * jnp.dot(hidden[0], w_ref[...], preferred_element_type=F32)
+        total += weight_pair[...] * jnp.dot(hidden[1], w, preferred_element_type=F32)
+        total = total.astype(BF16)
+        out_ref[...] = total
+        near_ref[...] = total[-2 * split : -split]
+        far_ref[...] = total[-split:]
+
+    def columns(height, first=0):
+        return pl.BlockSpec((height, step), lambda j: (0, first // step + j))
+
+    def fixed(a):
+        return pl.BlockSpec(a.shape, lambda j: (0, 0), pipeline_mode=pl.Buffered(1))
+
+    outs = [jax.ShapeDtypeStruct((height, width), BF16) for height in (rows, split, split)]
+    return pl.pallas_call(
+        body,
+        out_shape=outs,
+        grid=(width // step,),
+        in_specs=[fixed(a) for a in (*owns, *pairs)]
+        + [columns(units, low), columns(mine.shape[0]), columns(mine.shape[0])]
+        + [fixed(a) for a in weights],
+        out_specs=[columns(rows), columns(split), columns(split)],
+        scratch_shapes=[pltpu.VMEM((2, rows, units), BF16)],
+        compiler_params=params(),
+        cost_estimate=cost(4 * rows * units * width, *outs),
+    )(*owns, *pairs, w_down, mine, other, *weights)
+
+
+def hop_sum(total, step, rows, ahead, behind):
+    width = total.shape[1]
+    split = ahead.shape[0]
+
+    def body(toward_ref, back_ref, ahead_ref, behind_ref, out_toward, out_back):
+        if split == rows:
+            out_toward[...] = (toward_ref[...].astype(F32) + ahead_ref[...].astype(F32)).astype(BF16)
+            out_back[...] = (back_ref[...].astype(F32) + behind_ref[...].astype(F32)).astype(BF16)
+        else:
+            out_toward[:split, :] = toward_ref[:split, :]
+            out_toward[split:, :] = (toward_ref[split:, :].astype(F32) + ahead_ref[...].astype(F32)).astype(BF16)
+            out_back[:split, :] = (back_ref[:split, :].astype(F32) + behind_ref[...].astype(F32)).astype(BF16)
+            out_back[split:, :] = back_ref[split:, :]
+
+    out = jax.ShapeDtypeStruct((rows, width), BF16)
+    return pl.pallas_call(
+        body,
+        out_shape=[out, out],
+        grid=(1,),
+        in_specs=[
+            pl.BlockSpec((rows, width), lambda i: (2 * step, 0)),
+            pl.BlockSpec((rows, width), lambda i: (2 * step - 1, 0)),
+            whole(ahead.shape),
+            whole(behind.shape),
+        ],
+        out_specs=[whole(out.shape)] * 2,
+        compiler_params=params(),
+        cost_estimate=cost(0, out, out, out, out),
+    )(total, total, ahead, behind)
+
+
+def last_sum(chunks, rows, bounds):
+    flat = [a for chunk in chunks for a in chunk]
+
+    def body(*refs):
+        out_ref = refs[-1]
+        for n, (low, high) in enumerate(bounds):
+            own, ahead, behind = refs[3 * n : 3 * n + 3]
+            total = own[...].astype(F32) + ahead[...].astype(F32) + behind[...].astype(F32)
+            out_ref[:, low:high] = total.astype(BF16)
+
+    out = jax.ShapeDtypeStruct((rows, bounds[-1][1]), BF16)
+    return pl.pallas_call(
+        body,
+        out_shape=out,
+        grid=(1,),
+        in_specs=[pl.BlockSpec((rows, a.shape[1]), lambda i: (0, 0)) for a in flat],
+        out_specs=whole(out.shape),
+        compiler_params=params(),
+        cost_estimate=cost(0, out, out, out, out),
+    )(*flat)
+
+
+def gathered(tokens, expert_ids, route_weights, cotangent, w_gate, w_up, w_down, ia3_scale):
+    owners = lax.axis_size("exp")
+    members = owners // 2
+    rows, width = tokens.shape
+    units = w_gate.shape[2]
+    half_units = units // 2
+    me = lax.axis_index("exp")
+    rep = lax.axis_index("rep")
+    w_gate, w_up, w_down = w_gate[0], w_up[0], w_down[0]
+    forward, backward = ring_perm(members, 1), ring_perm(members, -1)
+    pair = [(i, i ^ 1) for i in range(owners)]
+    cores = [(0, 1), (1, 0)]
+    full = members // 2 - 1
+    split = rows // 2
+
+    def go(value, perm):
+        return lax.ppermute(value, "exp", perm)
+
+    def swap(value):
+        return lax.ppermute(value, "rep", cores)
+
+    def gather(block):
+        halves = (block[:split], block[split:])
+        ahead, behind = list(halves), list(halves)
+        blocks = [block]
+        for _ in range(1, full + 1):
+            ahead = [go(ahead[h], forward) for h in range(2)]
+            behind = [go(behind[h], backward) for h in range(2)]
+            blocks += ahead + behind
+        blocks.append(go(ahead[0], forward))
+        blocks.append(go(behind[1], backward))
+        return blocks
+
+    pieces = bounds_of(half_units, PIECES)
+    first = rep * half_units
+    core = jnp.full((1,), rep, jnp.int32)
+    projections = []
+    for low, high in pieces:
+        cut = cut_columns(core, w_gate, w_up, low, high)
+        mine = go(cut, pair)
+        projections.append((mine, swap(mine)))
+    bounds = bounds_of(width, SHARES)
+    cuts = cut_rows(core, w_down, bounds)
+    downs = []
+    for cut in cuts:
+        mine = go(cut, pair)
+        downs.append((mine, swap(mine)))
+
+    named = expert_ids[:, :, None] == jnp.arange(owners, dtype=jnp.int32)
+    table = jnp.sum(jnp.where(named, route_weights[:, :, None], 0).astype(F32), axis=1)
+    table = table.astype(BF16).T
+    member = me // 2
+    tables = table[None]
+    for bit in range(members.bit_length() - 1):
+        perm = [(i, i ^ (2 << bit)) for i in range(owners)]
+        other = go(tables, perm)
+        low = (member >> bit) % 2 == 0
+        tables = jnp.where(low, jnp.concatenate([tables, other]), jnp.concatenate([other, tables]))
+    order = ring_order(members)
+    places = jnp.array([order.index(m) for m in range(members)], jnp.int32)
+    offsets = [0]
+    for step in range(1, full + 1):
+        offsets += [-step, step]
+    offsets.append(members // 2)
+    place = places[member]
+    sources = jnp.array(order, jnp.int32)[(place + jnp.array(offsets, jnp.int32)) % members]
+    picked = jnp.take(tables, sources, axis=0).astype(F32)
+    pick = jnp.arange(owners, dtype=jnp.int32)[None, :, None]
+    weight_own = jnp.sum(jnp.where(pick == me, picked, 0), axis=1).reshape(-1, 1)
+    weight_pair = jnp.sum(jnp.where(pick == (me ^ 1), picked, 0), axis=1).reshape(-1, 1)
+
+    pair_scale = go(ia3_scale, pair)
+    scales = []
+    for low, high in pieces:
+        both = [
+            lax.dynamic_slice(pair_scale, (0, at + low), (1, high - low))
+            for at in (first, half_units - first)
+        ]
+        scales.append(jnp.concatenate(both, axis=1))
+    scale_pair = jnp.concatenate(scales, axis=1)
+
+    token_blocks = gather(tokens)
+    cotangent_blocks = gather(cotangent)
+    early = 1 + 4 * EARLY
+    count = rows * (1 + 2 * EARLY)
+    total_rows = rows * members
+    spans = (slice(0, count), slice(count, total_rows))
+    everything = slice(0, units)
+
+    def shape(height, size, dtype=F32):
+        return jax.ShapeDtypeStruct((height, size), dtype)
+
+    owns = []
+    for n, group in enumerate((token_blocks[:early], token_blocks[early:])):
+        height = spans[n].stop - spans[n].start
+        (hidden,) = contract(
+            group,
+            [[([(w, width)], everything, 0)] for w in (w_gate, w_up)],
+            False, [ia3_scale], [shape(height, units, BF16)], finish_own,
+        )
+        owns.append(hidden)
+
+    pairs = []
+    for piece, (low, high) in enumerate(pieces):
+        size = 2 * (high - low)
+        (hidden,) = contract(
+            token_blocks,
+            [[([(w, width)], slice(0, size), side * size) for side, w in enumerate(projections[piece])]],
+            False, [scales[piece]], [shape(total_rows, size, BF16)], finish_pair,
+        )
+        pairs.append(hidden)
+    takes = [slice(low, high) for low, high in pieces]
+
+    mixed = []
+    for chunk, (low, high) in enumerate(bounds):
+        total, behind, ahead = both_out(
+            owns, pairs, takes, w_down, *downs[chunk], (weight_own, weight_pair), low, split
+        )
+        ahead = go(ahead, forward)
+        behind = go(behind, backward)
+        for step in range(full, 0, -1):
+            toward, back = hop_sum(total, step, rows, ahead, behind)
+            ahead = go(toward, forward)
+            behind = go(back, backward)
+        mixed.append((total, ahead, behind))
+    mixed = last_sum(mixed, rows, bounds)
+
+    grad_own, grad_pair = 0.0, 0.0
+    for n, group in enumerate((cotangent_blocks[:early], cotangent_blocks[early:])):
+        (grad,) = contract(
+            group, [[([(w_down, width)], everything, 0)]], True,
+            [weight_own[spans[n]], ia3_scale, owns[n]], [shape(1, units)],
+            functools.partial(finish_grad, slice(None)),
+        )
+        grad_own += grad
+        parts, place = [], 0
+        for low, high in pieces:
+            for side in range(2):
+                segments = [(down[side], down[side].shape[1]) for down in downs]
+                parts.append((segments, slice(low, high), place))
+                place += high - low
+        (grad,) = contract(
+            group, [parts], True, [weight_pair[spans[n]], scale_pair, *pairs], [shape(1, units)],
+            functools.partial(finish_grad, spans[n]),
+        )
+        grad_pair += grad
+    sides, at = ([], []), 0
+    for low, high in pieces:
+        for side in range(2):
+            sides[side].append(grad_pair[:, at : at + high - low])
+            at += high - low
+    mine, other = (jnp.concatenate(side, axis=1) for side in sides)
+    halves = [jnp.concatenate(both, axis=1) for both in ((mine, other), (other, mine))]
+    grad_pair = jnp.where(rep == 0, *halves)
+    total = grad_own + go(grad_pair, pair)
+    total = total + swap(total)
+    return mixed, total
+
+
+def exchanged(tokens, expert_ids, route_weights, cotangent, w_gate, w_up, w_down, ia3_scale):
     owners = lax.axis_size("exp")
     tok_rows, model_width = tokens.shape
     per_token = expert_ids.shape[1]
@@ -56,6 +566,16 @@
     return (mixed, summed[None, :])
 
 
+def dense(owners, per_token):
+    return owners in (16,) and 2 * per_token >= owners
+
+
+def shards(*arrays):
+    if not dense(lax.axis_size("exp"), arrays[1].shape[1]):
+        return exchanged(*arrays)
+    return gathered(*arrays)
+
+
 def solution(mesh):
     in_specs = (
         P(("rep", "exp"), None),

time: 746 us -> 429 us (0.58)
  waiting for transfers between devices: 545 us -> 181 us
  Pallas kernels: 0 us -> 154 us
  local copies, waits for them, and re-layouts: 101 us -> 16 us
  matrix products: 52 us -> 0 us
  starting transfers between devices: 31.6 us -> 69.2 us
    all_to_all x4 -> x0, waiting for transfers between devices: 545 us -> none  [the longest x1 189 us: shards(): lax.all_to_all(expert_out.reshape(owners, capacity, model_width), 'exp',...]
    ppermute x0 -> x68, waiting for transfers between devices: none -> 181 us  [the longest x62 181 us: go(): return lax.ppermute(value, 'exp', perm)]
    pallas_call x0 -> x24, Pallas kernels: none -> 154 us  [the longest x8 91.3 us: contract(): pl.pallas_call(body, out_shape=outs, grid=(steps,), in_specs=specs, out_s...]
    ppermute x0 -> x68, starting transfers between devices: none -> 69.2 us  [the longest x62 68.5 us: go(): return lax.ppermute(value, 'exp', perm)]
    dot_general x5 -> x0, matrix products: 52 us -> none  [the longest x1 12.5 us: shards(): lax.dot_general(grad_recv.reshape(-1, model_width), w_down[0], (((1,), (1...]
    gather x3 -> x2, local copies, waits for them, and re-layouts: 49.8 us -> 1.2 us  [the longest x1 0.64 us: gathered(): jnp.array(order, jnp.int32)]
    unnamed x22 -> x120, local copies, waits for them, and re-layouts: 47.9 us -> 11.2 us
    all_to_all x4 -> x0, starting transfers between devices: 31.6 us -> none  [the longest x1 8.57 us: shards(): lax.all_to_all(expert_out.reshape(owners, capacity, model_width), 'exp',...]
  transfers between devices with their start and end apart: 4 -> 68, of which waited for: 3 -> 19; matrix products, arithmetic and copies ran while one was open for 13% -> 3% of each run, Pallas kernels for 0% -> 34%
where the time goes in v1:
time: 429 us; the launch traced here: 426 us
  waiting for transfers between devices  181 us (42%)
  Pallas kernels  154 us (36%)
  starting transfers between devices  69.2 us (16%)
  local copies, waits for them, and re-layouts  16 us (4%)
    ppermute x62, waiting for transfers between devices, go(): return lax.ppermute(value, 'exp', perm)  181 us
    pallas_call x8, Pallas kernels, contract(): pl.pallas_call(body, out_shape=outs, grid=(steps,), in_specs=specs, out_s...  91.3 us
    ppermute x62, starting transfers between devices, go(): return lax.ppermute(value, 'exp', perm)  68.5 us
    pallas_call x3, Pallas kernels, both_out(): pl.pallas_call(body, out_shape=outs, grid=(width // step,), in_specs=[fix...  26.8 us
    pallas_call x9, Pallas kernels, hop_sum(): pl.pallas_call(body, out_shape=[out, out], grid=(1,), in_specs=[pl.BlockS...  19.8 us
    unnamed x120, local copies, waits for them, and re-layouts  11.2 us
    pallas_call x2, Pallas kernels, cut_columns(): pl.pallas_call(body, out_shape=out, grid_spec=pltpu.PrefetchScalarGridSpe...  8.96 us
  transfers between devices with their start and end apart: 68, of which 19 were waited for; matrix products, arithmetic and copies ran while one was open for 3% of the time, Pallas kernels for 34%

profile of v1, /device:TPU:12, one launch (start us, length us, event | category | flops | bytes accessed | tf_op | source)
XLA Modules:
  0.0 425.5 jit_solution(1680278066124637334)
XLA Ops:
  0.7 5.1 %cut_columns.2 = bf16[4096,512]{1,0:T(8,128)(2,1)} custom-call(s32[1]{0:T(128)} %bitcast.2.core_ref, bf16[4096,768]{1,0:T(8,128)(2,1)} %bitcast.48, bf16[4096,768]{1,0:T(8,128)(2,1)} %bitcast.49, bf16[4096,768]{1,0:T(8,128)(2,1)} %bitcast.53, bf16[4096,768]{1,0:T(8,128)(2,1)} %bitcast.54), custom_call_target="tpu_custom_call" | custom-call | bytes 8388608 | tf_op jit(solution)/shard_map/cut_columns/pallas_call | solution.py:70
  7.8 3.1 collective-permute-done.21
  14.2 3.9 cut_columns.3
  19.6 79.9 %collective-permute-done.16 = f32[1,768]{1,0:T(1,128)S(1)} collective-permute-done((f32[1,768]{1,0:T(1,128)S(1)}, f32[1,768]{1,0:T(1,128)S(1)}, u32[]{:S(2)}, u32[]{:S(2)}) %collective-permute-start.16) | collective-permute-done | bytes 3104 | tf_op jit(solution)/shard_map/ppermute | solution.py:374
  99.5 2.6 collective-permute-start.23
  108.5 10.4 %collective-permute-done.2.refs_3_ = bf16[64,4096]{1,0:T(8,128)(2,1)S(1)} collective-permute-done((bf16[64,4096]{1,0:T(8,128)(2,1)S(1)}, bf16[64,4096]{1,0:T(8,128)(2,1)S(1)}, u32[]{:S(2)}, u32[]{:S(2)}) %collective-permute-start.2) | collective-permute-done | bytes 524320 | tf_op jit(solution)/shard_map/ppermute | solution.py:374
  120.7 9.6 %collective-permute-done.3.refs_4_ = bf16[64,4096]{1,0:T(8,128)(2,1)} collective-permute-done((bf16[64,4096]{1,0:T(8,128)(2,1)S(1)}, bf16[64,4096]{1,0:T(8,128)(2,1)}, u32[]{:S(2)}, u32[]{:S(2)}) %collective-permute-start.3) | collective-permute-done | bytes 524320 | tf_op jit(solution)/shard_map/ppermute | solution.py:374
  131.7 4.4 %cut_rows.1 = (bf16[384,1536]{1,0:T(8,128)(2,1)}, bf16[384,1536]{1,0:T(8,128)(2,1)}, bf16[384,1024]{1,0:T(8,128)(2,1)}) custom-call(s32[1]{0:T(128)} %bitcast.2.core_ref, bf16[768,4096]{1,0:T(8,128)(2,1)} %bitcast.42), custom_call_target="tpu_custom_call" | custom-call | bytes 6291456 | tf_op jit(solution)/shard_map/cut_rows/pallas_call | solution.py:93
  136.8 8.4 %collective-permute-done.53.refs_2_ = bf16[64,4096]{1,0:T(8,128)(2,1)} collective-permute-done((bf16[64,4096]{1,0:T(8,128)(2,1)S(1)}, bf16[64,4096]{1,0:T(8,128)(2,1)}, u32[]{:S(2)}, u32[]{:S(2)}) %collective-permute-start.53) | collective-permute-done | bytes 524320 | tf_op jit(solution)/shard_map/ppermute | solution.py:374
  147.2 6.0 %collective-permute-done.4.refs_5_ = bf16[64,4096]{1,0:T(8,128)(2,1)} collective-permute-done((bf16[64,4096]{1,0:T(8,128)(2,1)S(1)}, bf16[64,4096]{1,0:T(8,128)(2,1)}, u32[]{:S(2)}, u32[]{:S(2)}) %collective-permute-start.4) | collective-permute-done | bytes 524320 | tf_op jit(solution)/shard_map/ppermute | solution.py:374
  154.9 7.5 %collective-permute-done.5.refs_6_ = bf16[64,4096]{1,0:T(8,128)(2,1)} collective-permute-done((bf16[64,4096]{1,0:T(8,128)(2,1)}, bf16[64,4096]{1,0:T(8,128)(2,1)}, u32[]{:S(2)}, u32[]{:S(2)}) %collective-permute-start.5) | collective-permute-done | bytes 524320 | tf_op jit(solution)/shard_map/ppermute | solution.py:374
  162.4 2.7 collective-permute-start.7
  168.2 4.6 %collective-permute-done.7.refs_8_ = bf16[64,4096]{1,0:T(8,128)(2,1)} collective-permute-done((bf16[64,4096]{1,0:T(8,128)(2,1)}, bf16[64,4096]{1,0:T(8,128)(2,1)}, u32[]{:S(2)}, u32[]{:S(2)}) %collective-permute-start.7) | collective-permute-done | bytes 524320 | tf_op jit(solution)/shard_map/ppermute | solution.py:374
  172.8 2.5 collective-permute-start.10
  175.4 3.6 collective-permute-done.8.refs_0_.refs_9_
  188.9 7.3 %collective-permute-done.11.refs_3_.refs_12_ = bf16[64,4096]{1,0:T(8,128)(2,1)} collective-permute-done((bf16[64,4096]{1,0:T(8,128)(2,1)}, bf16[64,4096]{1,0:T(8,128)(2,1)}, u32[]{:S(2)}, u32[]{:S(2)}) %collective-permute-start.11) | collective-permute-done | bytes 524320 | tf_op jit(solution)/shard_map/ppermute | solution.py:374
  198.7 14.6 %shard_map.122.refs_0_.refs_12_ = bf16[640,768]{1,0:T(8,128)(2,1)} custom-call(bf16[128,4096]{1,0:T(8,128)(2,1)} %refs_0_.7, bf16[64,4096]{1,0:T(8,128)(2,1)} %copy-done.45, bf16[64,4096]{1,0:T(8,128)(2,1)} %collective-permute-done.1.refs_2_, bf16[64,4096]{1,0:T(8,128)(2,1)} %copy-done.46, bf16[64,4096]{1,0:T(8,128)(2,1)} %collective-permute-done.3.refs_4_, ...), custom_call_target="tpu_custom_call" | custom-call | flops 8053063680 | bytes 983040 | tf_op jit(solution)/shard_map/pallas_call | solution.py:208
  218.0 10.5 %shard_map.123.refs_1_.refs_9_ = bf16[384,768]{1,0:T(8,128)(2,1)} custom-call(bf16[64,4096]{1,0:T(8,128)(2,1)} %collective-permute-done.8.refs_0_.refs_9_, bf16[64,4096]{1,0:T(8,128)(2,1)} %collective-permute-done.9.refs_1_.refs_10_, bf16[64,4096]{1,0:T(8,128)(2,1)} %collective-permute-done.10.refs_2_.refs_11_, ...), custom_call_target="tpu_custom_call" | custom-call | flops 4831838208 | bytes 589824 | tf_op jit(solution)/shard_map/pallas_call | solution.py:208
  228.7 10.9 %shard_map.125.refs_3_.refs_18_.refs_15_ = bf16[1024,256]{1,0:T(8,128)(2,1)} custom-call(bf16[128,4096]{1,0:T(8,128)(2,1)} %refs_0_.7, bf16[64,4096]{1,0:T(8,128)(2,1)} %copy-done.45, bf16[64,4096]{1,0:T(8,128)(2,1)} %collective-permute-done.1.refs_2_, bf16[64,4096]{1,0:T(8,128)(2,1)} %copy-done.46, bf16[64,4096]{1,0:T(8,128)(2,1)} %collective-permute-done.3.refs_4_, ...), custom_call_target="tpu_custom_call" | custom-call | flops 4294967296 | bytes 524288 | tf_op jit(solution)/shard_map/pallas_call | solution.py:208
  242.2 15.8 %shard_map.124.refs_2_.refs_17_.refs_14_ = bf16[1024,512]{1,0:T(8,128)(2,1)} custom-call(bf16[128,4096]{1,0:T(8,128)(2,1)} %refs_0_.7, bf16[64,4096]{1,0:T(8,128)(2,1)} %copy-done.45, bf16[64,4096]{1,0:T(8,128)(2,1)} %collective-permute-done.1.refs_2_, bf16[64,4096]{1,0:T(8,128)(2,1)} %copy-done.46, bf16[64,4096]{1,0:T(8,128)(2,1)} %collective-permute-done.3.refs_4_, ...), custom_call_target="tpu_custom_call" | custom-call | flops 8589934592 | bytes 1048576 | tf_op jit(solution)/shard_map/pallas_call | solution.py:208
  260.4 9.5 %shard_map.126 = (bf16[1024,1536]{1,0:T(8,128)(2,1)}, bf16[64,1536]{1,0:T(8,128)(2,1)}, bf16[64,1536]{1,0:T(8,128)(2,1)}) custom-call(bf16[640,768]{1,0:T(8,128)(2,1)} %shard_map.122.refs_0_.refs_12_, bf16[384,768]{1,0:T(8,128)(2,1)} %shard_map.123.refs_1_.refs_9_, bf16[1024,512]{1,0:T(8,128)(2,1)} %shard_map.124.refs_2_.refs_17_.refs_14_, ...), custom_call_target="tpu_custom_call" | custom-call | flops 4831838208 | bytes 3538944 | tf_op jit(solution)/shard_map/pallas_call | solution.py:291
  271.8 7.7 %shard_map.134 = (bf16[1024,1024]{1,0:T(8,128)(2,1)}, bf16[64,1024]{1,0:T(8,128)(2,1)}, bf16[64,1024]{1,0:T(8,128)(2,1)}) custom-call(bf16[640,768]{1,0:T(8,128)(2,1)} %shard_map.122.refs_0_.refs_12_, bf16[384,768]{1,0:T(8,128)(2,1)} %shard_map.123.refs_1_.refs_9_, bf16[1024,512]{1,0:T(8,128)(2,1)} %shard_map.124.refs_2_.refs_17_.refs_14_, ...), custom_call_target="tpu_custom_call" | custom-call | flops 3221225472 | bytes 2359296 | tf_op jit(solution)/shard_map/pallas_call | solution.py:291
  279.9 4.5 %collective-permute-done.60.refs_0_ = bf16[64,4096]{1,0:T(8,128)(2,1)S(1)} collective-permute-done((bf16[64,4096]{1,0:T(8,128)(2,1)}, bf16[64,4096]{1,0:T(8,128)(2,1)S(1)}, u32[]{:S(2)}, u32[]{:S(2)}) %collective-permute-start.60) | collective-permute-done | bytes 524320 | tf_op jit(solution)/shard_map/ppermute | solution.py:374
  285.8 10.5 %shard_map.139 = f32[1,768]{1,0:T(1,128)} custom-call(bf16[128,4096]{1,0:T(8,128)(2,1)} %refs_0_.9, bf16[64,4096]{1,0:T(8,128)(2,1)} %copy-done.43, bf16[64,4096]{1,0:T(8,128)(2,1)} %collective-permute-done.53.refs_2_, bf16[64,4096]{1,0:T(8,128)(2,1)} %collective-permute-done.54.refs_3_, bf16[64,4096]{1,0:T(8,128)(2,1)} %collective-permute-done.55.refs_4_, ...), custom_call_target="tpu_custom_call" | custom-call | flops 4026531840 | bytes 3072 | tf_op jit(solution)/shard_map/pallas_call | solution.py:208
  301.1 9.6 %shard_map.130 = (bf16[1024,1536]{1,0:T(8,128)(2,1)}, bf16[64,1536]{1,0:T(8,128)(2,1)}, bf16[64,1536]{1,0:T(8,128)(2,1)}) custom-call(bf16[640,768]{1,0:T(8,128)(2,1)} %shard_map.122.refs_0_.refs_12_, bf16[384,768]{1,0:T(8,128)(2,1)} %shard_map.123.refs_1_.refs_9_, bf16[1024,512]{1,0:T(8,128)(2,1)} %shard_map.124.refs_2_.refs_17_.refs_14_, ...), custom_call_target="tpu_custom_call" | custom-call | flops 4831838208 | bytes 3538944 | tf_op jit(solution)/shard_map/pallas_call | solution.py:291
  312.7 11.4 %collective-permute-done.25.behind_ref = bf16[64,1536]{1,0:T(8,128)(2,1)S(1)} collective-permute-done((bf16[64,1536]{1,0:T(8,128)(2,1)S(1)}, bf16[64,1536]{1,0:T(8,128)(2,1)S(1)}, u32[]{:S(2)}, u32[]{:S(2)}) %collective-permute-start.25) | collective-permute-done | bytes 196640 | tf_op jit(solution)/shard_map/ppermute | solution.py:374
  324.7 11.2 %shard_map.141 = f32[1,768]{1,0:T(1,128)} custom-call(bf16[128,4096]{1,0:T(8,128)(2,1)} %refs_0_.9, bf16[64,4096]{1,0:T(8,128)(2,1)} %copy-done.43, bf16[64,4096]{1,0:T(8,128)(2,1)} %collective-permute-done.53.refs_2_, bf16[64,4096]{1,0:T(8,128)(2,1)} %collective-permute-done.54.refs_3_, bf16[64,4096]{1,0:T(8,128)(2,1)} %collective-permute-done.55.refs_4_, ...), custom_call_target="tpu_custom_call" | custom-call | flops 4026531840 | bytes 3072 | tf_op jit(solution)/shard_map/pallas_call | solution.py:208
  342.4 9.1 %shard_map.142 = f32[1,768]{1,0:T(1,128)} custom-call(bf16[64,4096]{1,0:T(8,128)(2,1)} %copy-done.3, bf16[64,4096]{1,0:T(8,128)(2,1)} %copy-done.5, bf16[64,4096]{1,0:T(8,128)(2,1)} %copy-done.6, bf16[64,4096]{1,0:T(8,128)(2,1)} %copy-done.4, bf16[64,4096]{1,0:T(8,128)(2,1)} %copy-done.7, bf16[64,4096]{1,0:T(8,128)(2,1)} %copy-done.8, ...), custom_call_target="tpu_custom_call" | custom-call | flops 2415919104 | bytes 3072 | tf_op jit(solution)/shard_map/pallas_call | solution.py:208
  369.0 3.9 collective-permute-done.37.behind_ref
  380.0 8.5 %shard_map.140 = f32[1,768]{1,0:T(1,128)} custom-call(bf16[64,4096]{1,0:T(8,128)(2,1)} %copy-done.3, bf16[64,4096]{1,0:T(8,128)(2,1)} %copy-done.5, bf16[64,4096]{1,0:T(8,128)(2,1)} %copy-done.6, bf16[64,4096]{1,0:T(8,128)(2,1)} %copy-done.4, bf16[64,4096]{1,0:T(8,128)(2,1)} %copy-done.7, bf16[64,4096]{1,0:T(8,128)(2,1)} %copy-done.8, ...), custom_call_target="tpu_custom_call" | custom-call | flops 2415919104 | bytes 3072 | tf_op jit(solution)/shard_map/pallas_call | solution.py:208
  404.4 16.1 %collective-permute-done.51.refs_8_ = bf16[128,1024]{1,0:T(8,128)(2,1)S(1)} collective-permute-done((bf16[128,1024]{1,0:T(8,128)(2,1)S(1)}, bf16[128,1024]{1,0:T(8,128)(2,1)S(1)}, u32[]{:S(2)}, u32[]{:S(2)}) %collective-permute-start.51) | collective-permute-done | bytes 262176 | tf_op jit(solution)/shard_map/ppermute | solution.py:374
  422.3 3.2 shard_map.138
  (278 shorter events, 105.6 us)
Async XLA Ops:
  5.7 102.2 %collective-permute-start.14 = (bf16[4096,512]{1,0:T(8,128)(2,1)}, bf16[4096,512]{1,0:T(8,128)(2,1)}, u32[]{:S(2)}, u32[]{:S(2)}) collective-permute-start(bf16[4096,512]{1,0:T(8,128)(2,1)} %cut_columns.2), channel_id=1, source_target_pairs={{0,1},{1,0},{2,3},{3,2},{4,5},{5,4},{6,7},{7,6},{8,9},{9,8},{10,11... | collective-permute-start | bytes 12582920 | tf_op jit(solution)/shard_map/ppermute | solution.py:374
  11.5 94.4 %collective-permute-start = (bf16[64,4096]{1,0:T(8,128)(2,1)S(1)}, bf16[64,4096]{1,0:T(8,128)(2,1)S(1)}, u32[]{:S(2)}, u32[]{:S(2)}) collective-permute-start(bf16[64,4096]{1,0:T(8,128)(2,1)S(1)} %get-tuple-element.67), channel_id=1, source_target_pairs={{0,4},{4,8},{8,12},{12,14},{14,10},{10,6},{6,2},{2,0},{1,5},{5,9},... | collective-permute-start | bytes 1572872 | tf_op jit(solution)/shard_map/ppermute | solution.py:374
  13.1 94.5 %collective-permute-start.1 = (bf16[64,4096]{1,0:T(8,128)(2,1)S(1)}, bf16[64,4096]{1,0:T(8,128)(2,1)}, u32[]{:S(2)}, u32[]{:S(2)}) collective-permute-start(bf16[64,4096]{1,0:T(8,128)(2,1)S(1)} %get-tuple-element.66), channel_id=1, source_target_pairs={{0,4},{4,8},{8,12},{12,14},{14,10},{10,6},{6,2},{2,0},{1,5},{5,9},... | collective-permute-start | bytes 1572872 | tf_op jit(solution)/shard_map/ppermute | solution.py:374
  13.6 85.9 %collective-permute-start.16 = (f32[1,768]{1,0:T(1,128)S(1)}, f32[1,768]{1,0:T(1,128)S(1)}, u32[]{:S(2)}, u32[]{:S(2)}) collective-permute-start(f32[1,768]{1,0:T(1,128)S(1)} %copy-done.38), channel_id=1, source_target_pairs={{0,1},{1,0},{2,3},{3,2},{4,5},{5,4},{6,7},{7,6},{8,9},{9,8},{10,11... | collective-permute-start | bytes 9224 | tf_op jit(solution)/shard_map/ppermute | solution.py:374
  18.1 148.5 %collective-permute-start.17 = (bf16[4096,256]{1,0:T(8,128)(2,1)}, bf16[4096,256]{1,0:T(8,128)(2,1)}, u32[]{:S(2)}, u32[]{:S(2)}) collective-permute-start(bf16[4096,256]{1,0:T(8,128)(2,1)} %cut_columns.3), channel_id=1, source_target_pairs={{0,1},{1,0},{2,3},{3,2},{4,5},{5,4},{6,7},{7,6},{8,9},{9,8},{10,11... | collective-permute-start | bytes 6291464 | tf_op jit(solution)/shard_map/ppermute | solution.py:374
  105.9 24.4 %collective-permute-start.3 = (bf16[64,4096]{1,0:T(8,128)(2,1)S(1)}, bf16[64,4096]{1,0:T(8,128)(2,1)}, u32[]{:S(2)}, u32[]{:S(2)}) collective-permute-start(bf16[64,4096]{1,0:T(8,128)(2,1)S(1)} %get-tuple-element.66), channel_id=1, source_target_pairs={{0,2},{4,0},{8,4},{12,8},{14,12},{10,14},{6,10},{2,6},{1,3},{5,1},... | collective-permute-start | bytes 1572872 | tf_op jit(solution)/shard_map/ppermute | solution.py:374
  107.6 23.1 %collective-permute-start.52 = (bf16[64,4096]{1,0:T(8,128)(2,1)}, bf16[64,4096]{1,0:T(8,128)(2,1)S(1)}, u32[]{:S(2)}, u32[]{:S(2)}) collective-permute-start(bf16[64,4096]{1,0:T(8,128)(2,1)} %get-tuple-element.65), channel_id=1, source_target_pairs={{0,4},{4,8},{8,12},{12,14},{14,10},{10,6},{6,2},{2,0},{1,5},{5,9},... | collective-permute-start | bytes 1572872 | tf_op jit(solution)/shard_map/ppermute | solution.py:374
  107.9 133.8 %collective-permute-start.15 = (bf16[4096,512]{1,0:T(8,128)(2,1)}, bf16[4096,512]{1,0:T(8,128)(2,1)}, u32[]{:S(2)}, u32[]{:S(2)}) collective-permute-start(bf16[4096,512]{1,0:T(8,128)(2,1)} %collective-permute-done.14.refs_15_), channel_id=1, source_target_pairs={{0,16},{16,0},{1,17},{17,1},{2,18},{18,2},{3,19},{19,3},{4,20},{20... | collective-permute-start | bytes 12582920 | tf_op jit(solution)/shard_map/ppermute | solution.py:377
  118.9 27.7 %collective-permute-start.54 = (bf16[64,4096]{1,0:T(8,128)(2,1)}, bf16[64,4096]{1,0:T(8,128)(2,1)}, u32[]{:S(2)}, u32[]{:S(2)}) collective-permute-start(bf16[64,4096]{1,0:T(8,128)(2,1)} %get-tuple-element.65), channel_id=1, source_target_pairs={{0,2},{4,0},{8,4},{12,8},{14,12},{10,14},{6,10},{2,6},{1,3},{5,1},... | collective-permute-start | bytes 1572872 | tf_op jit(solution)/shard_map/ppermute | solution.py:374
  130.7 22.4 %collective-permute-start.4 = (bf16[64,4096]{1,0:T(8,128)(2,1)S(1)}, bf16[64,4096]{1,0:T(8,128)(2,1)}, u32[]{:S(2)}, u32[]{:S(2)}) collective-permute-start(bf16[64,4096]{1,0:T(8,128)(2,1)S(1)} %collective-permute-done.refs_1_), channel_id=1, source_target_pairs={{0,4},{4,8},{8,12},{12,14},{14,10},{10,6},{6,2},{2,0},{1,5},{5,9},... | collective-permute-start | bytes 1572872 | tf_op jit(solution)/shard_map/ppermute | solution.py:374
  145.2 27.7 %collective-permute-start.19 = (bf16[384,1536]{1,0:T(8,128)(2,1)}, bf16[384,1536]{1,0:T(8,128)(2,1)S(1)}, u32[]{:S(2)}, u32[]{:S(2)}) collective-permute-start(bf16[384,1536]{1,0:T(8,128)(2,1)} %get-tuple-element.32), channel_id=1, source_target_pairs={{0,1},{1,0},{2,3},{3,2},{4,5},{5,4},{6,7},{7,6},{8,9},{9,8},{10,11... | collective-permute-start | bytes 3538952 | tf_op jit(solution)/shard_map/ppermute | solution.py:374
  166.5 62.1 %collective-permute-start.18 = (bf16[4096,256]{1,0:T(8,128)(2,1)}, bf16[4096,256]{1,0:T(8,128)(2,1)}, u32[]{:S(2)}, u32[]{:S(2)}) collective-permute-start(bf16[4096,256]{1,0:T(8,128)(2,1)} %collective-permute-done.17.refs_15_), channel_id=1, source_target_pairs={{0,16},{16,0},{1,17},{17,1},{2,18},{18,2},{3,19},{19,3},{4,20},{20... | collective-permute-start | bytes 6291464 | tf_op jit(solution)/shard_map/ppermute | solution.py:377
  186.8 54.9 %collective-permute-start.32 = (bf16[384,1536]{1,0:T(8,128)(2,1)}, bf16[384,1536]{1,0:T(8,128)(2,1)}, u32[]{:S(2)}, u32[]{:S(2)}) collective-permute-start(bf16[384,1536]{1,0:T(8,128)(2,1)} %get-tuple-element.42), channel_id=1, source_target_pairs={{0,1},{1,0},{2,3},{3,2},{4,5},{5,4},{6,7},{7,6},{8,9},{9,8},{10,11... | collective-permute-start | bytes 3538952 | tf_op jit(solution)/shard_map/ppermute | solution.py:374
  188.3 25.0 %collective-permute-start.12 = (bf16[64,4096]{1,0:T(8,128)(2,1)}, bf16[64,4096]{1,0:T(8,128)(2,1)S(1)}, u32[]{:S(2)}, u32[]{:S(2)}) collective-permute-start(bf16[64,4096]{1,0:T(8,128)(2,1)} %collective-permute-done.8.refs_0_.refs_9_), channel_id=1, source_target_pairs={{0,4},{4,8},{8,12},{12,14},{14,10},{10,6},{6,2},{2,0},{1,5},{5,9},... | collective-permute-start | bytes 1572872 | tf_op jit(solution)/shard_map/ppermute | solution.py:374
  213.4 26.2 %collective-permute-start.55 = (bf16[64,4096]{1,0:T(8,128)(2,1)S(1)}, bf16[64,4096]{1,0:T(8,128)(2,1)}, u32[]{:S(2)}, u32[]{:S(2)}) collective-permute-start(bf16[64,4096]{1,0:T(8,128)(2,1)S(1)} %get-tuple-element.64), channel_id=1, source_target_pairs={{0,2},{4,0},{8,4},{12,8},{14,12},{10,14},{6,10},{2,6},{1,3},{5,1},... | collective-permute-start | bytes 1572872 | tf_op jit(solution)/shard_map/ppermute | solution.py:374
  216.5 23.2 %collective-permute-start.42 = (bf16[384,1024]{1,0:T(8,128)(2,1)S(1)}, bf16[384,1024]{1,0:T(8,128)(2,1)S(1)}, u32[]{:S(2)}, u32[]{:S(2)}) collective-permute-start(bf16[384,1024]{1,0:T(8,128)(2,1)S(1)} %copy-done.42), channel_id=1, source_target_pairs={{0,1},{1,0},{2,3},{3,2},{4,5},{5,4},{6,7},{7,6},{8,9},{9,8},{10,11... | collective-permute-start | bytes 2359304 | tf_op jit(solution)/shard_map/ppermute | solution.py:374
  228.6 31.6 %collective-permute-start.20 = (bf16[384,1536]{1,0:T(8,128)(2,1)S(1)}, bf16[384,1536]{1,0:T(8,128)(2,1)}, u32[]{:S(2)}, u32[]{:S(2)}) collective-permute-start(bf16[384,1536]{1,0:T(8,128)(2,1)S(1)} %collective-permute-done.19.refs_5_.refs_9_.refs_6_), channel_id=1, source_target_pairs={{0,16},{16,0},{1,17},{17,1},{2,18},{18,2},{3,19},{19,3},{4,20},{20... | collective-permute-start | bytes 3538952 | tf_op jit(solution)/shard_map/ppermute | solution.py:377
  241.7 28.3 %collective-permute-start.43 = (bf16[384,1024]{1,0:T(8,128)(2,1)S(1)}, bf16[384,1024]{1,0:T(8,128)(2,1)S(1)}, u32[]{:S(2)}, u32[]{:S(2)}) collective-permute-start(bf16[384,1024]{1,0:T(8,128)(2,1)S(1)} %collective-permute-done.42.refs_5_.refs_11_.refs_8_), channel_id=1, source_target_pairs={{0,16},{16,0},{1,17},{17,1},{2,18},{18,2},{3,19},{19,3},{4,20},{20... | collective-permute-start | bytes 2359304 | tf_op jit(solution)/shard_map/ppermute | solution.py:377
  241.7 55.3 %collective-permute-start.33 = (bf16[384,1536]{1,0:T(8,128)(2,1)}, bf16[384,1536]{1,0:T(8,128)(2,1)}, u32[]{:S(2)}, u32[]{:S(2)}) collective-permute-start(bf16[384,1536]{1,0:T(8,128)(2,1)} %collective-permute-done.32.refs_5_.refs_10_.refs_7_), channel_id=1, source_target_pairs={{0,16},{16,0},{1,17},{17,1},{2,18},{18,2},{3,19},{19,3},{4,20},{20... | collective-permute-start | bytes 3538952 | tf_op jit(solution)/shard_map/ppermute | solution.py:377
  258.1 21.4 %collective-permute-start.57 = (bf16[64,4096]{1,0:T(8,128)(2,1)}, bf16[64,4096]{1,0:T(8,128)(2,1)}, u32[]{:S(2)}, u32[]{:S(2)}) collective-permute-start(bf16[64,4096]{1,0:T(8,128)(2,1)} %collective-permute-done.53.refs_2_), channel_id=1, source_target_pairs={{0,4},{4,8},{8,12},{12,14},{14,10},{10,6},{6,2},{2,0},{1,5},{5,9},... | collective-permute-start | bytes 1572872 | tf_op jit(solution)/shard_map/ppermute | solution.py:374
  260.2 24.2 %collective-permute-start.60 = (bf16[64,4096]{1,0:T(8,128)(2,1)}, bf16[64,4096]{1,0:T(8,128)(2,1)S(1)}, u32[]{:S(2)}, u32[]{:S(2)}) collective-permute-start(bf16[64,4096]{1,0:T(8,128)(2,1)} %collective-permute-done.56.refs_5_), channel_id=1, source_target_pairs={{0,4},{4,8},{8,12},{12,14},{14,10},{10,6},{6,2},{2,0},{1,5},{5,9},... | collective-permute-start | bytes 1572872 | tf_op jit(solution)/shard_map/ppermute | solution.py:374
  270.0 26.3 %collective-permute-start.63 = (bf16[64,4096]{1,0:T(8,128)(2,1)}, bf16[64,4096]{1,0:T(8,128)(2,1)S(1)}, u32[]{:S(2)}, u32[]{:S(2)}) collective-permute-start(bf16[64,4096]{1,0:T(8,128)(2,1)} %copy-done.48), channel_id=1, source_target_pairs={{0,2},{4,0},{8,4},{12,8},{14,12},{10,14},{6,10},{2,6},{1,3},{5,1},... | collective-permute-start | bytes 1572872 | tf_op jit(solution)/shard_map/ppermute | solution.py:374
  296.3 41.7 %collective-permute-start.61 = (bf16[64,4096]{1,0:T(8,128)(2,1)}, bf16[64,4096]{1,0:T(8,128)(2,1)S(1)}, u32[]{:S(2)}, u32[]{:S(2)}) collective-permute-start(bf16[64,4096]{1,0:T(8,128)(2,1)} %collective-permute-done.57.refs_6_), channel_id=1, source_target_pairs={{0,4},{4,8},{8,12},{12,14},{14,10},{10,6},{6,2},{2,0},{1,5},{5,9},... | collective-permute-start | bytes 1572872 | tf_op jit(solution)/shard_map/ppermute | solution.py:374
  297.0 41.6 %collective-permute-start.62 = (bf16[64,4096]{1,0:T(8,128)(2,1)}, bf16[64,4096]{1,0:T(8,128)(2,1)S(1)}, u32[]{:S(2)}, u32[]{:S(2)}) collective-permute-start(bf16[64,4096]{1,0:T(8,128)(2,1)} %collective-permute-done.58.refs_7_), channel_id=1, source_target_pairs={{0,2},{4,0},{8,4},{12,8},{14,12},{10,14},{6,10},{2,6},{1,3},{5,1},... | collective-permute-start | bytes 1572872 | tf_op jit(solution)/shard_map/ppermute | solution.py:374
  298.4 41.7 %collective-permute-start.64 = (bf16[64,4096]{1,0:T(8,128)(2,1)S(1)}, bf16[64,4096]{1,0:T(8,128)(2,1)S(1)}, u32[]{:S(2)}, u32[]{:S(2)}) collective-permute-start(bf16[64,4096]{1,0:T(8,128)(2,1)S(1)} %collective-permute-done.60.refs_0_), channel_id=1, source_target_pairs={{0,4},{4,8},{8,12},{12,14},{14,10},{10,6},{6,2},{2,0},{1,5},{5,9},... | collective-permute-start | bytes 1572872 | tf_op jit(solution)/shard_map/ppermute | solution.py:374
  299.1 42.5 %collective-permute-start.65 = (bf16[64,4096]{1,0:T(8,128)(2,1)S(1)}, bf16[64,4096]{1,0:T(8,128)(2,1)S(1)}, u32[]{:S(2)}, u32[]{:S(2)}) collective-permute-start(bf16[64,4096]{1,0:T(8,128)(2,1)S(1)} %collective-permute-done.63.refs_3_), channel_id=1, source_target_pairs={{0,2},{4,0},{8,4},{12,8},{14,12},{10,14},{6,10},{2,6},{1,3},{5,1},... | collective-permute-start | bytes 1572872 | tf_op jit(solution)/shard_map/ppermute | solution.py:374
  300.5 23.7 %collective-permute-start.25 = (bf16[64,1536]{1,0:T(8,128)(2,1)S(1)}, bf16[64,1536]{1,0:T(8,128)(2,1)S(1)}, u32[]{:S(2)}, u32[]{:S(2)}) collective-permute-start(bf16[64,1536]{1,0:T(8,128)(2,1)S(1)} %copy-done.52), channel_id=1, source_target_pairs={{0,2},{4,0},{8,4},{12,8},{14,12},{10,14},{6,10},{2,6},{1,3},{5,1},... | collective-permute-start | bytes 589832 | tf_op jit(solution)/shard_map/ppermute | solution.py:374
  324.1 33.0 %collective-permute-start.46 = (bf16[128,1024]{1,0:T(8,128)(2,1)}, bf16[128,1024]{1,0:T(8,128)(2,1)S(1)}, u32[]{:S(2)}, u32[]{:S(2)}) collective-permute-start(bf16[128,1024]{1,0:T(8,128)(2,1)} %get-tuple-element.56), channel_id=1, source_target_pairs={{0,4},{4,8},{8,12},{12,14},{14,10},{10,6},{6,2},{2,0},{1,5},{5,9},... | collective-permute-start | bytes 786440 | tf_op jit(solution)/shard_map/ppermute | solution.py:374
  364.5 26.2 %collective-permute-start.66 = (f32[1,768]{1,0:T(1,128)S(1)}, f32[1,768]{1,0:T(1,128)S(1)}, u32[]{:S(2)}, u32[]{:S(2)}) collective-permute-start(f32[1,768]{1,0:T(1,128)S(1)} %broadcast_select_fusion.1), channel_id=1, source_target_pairs={{0,1},{1,0},{2,3},{3,2},{4,5},{5,4},{6,7},{7,6},{8,9},{9,8},{10,11... | collective-permute-start | bytes 9224 | tf_op jit(solution)/shard_map/ppermute | solution.py:374
  368.5 22.7 %collective-permute-start.28 = (bf16[128,1536]{1,0:T(8,128)(2,1)}, bf16[128,1536]{1,0:T(8,128)(2,1)S(1)}, u32[]{:S(2)}, u32[]{:S(2)}) collective-permute-start(bf16[128,1536]{1,0:T(8,128)(2,1)} %get-tuple-element.38), channel_id=1, source_target_pairs={{0,4},{4,8},{8,12},{12,14},{14,10},{10,6},{6,2},{2,0},{1,5},{5,9},... | collective-permute-start | bytes 1179656 | tf_op jit(solution)/shard_map/ppermute | solution.py:374
  395.1 25.3 %collective-permute-start.30 = (bf16[128,1536]{1,0:T(8,128)(2,1)}, bf16[128,1536]{1,0:T(8,128)(2,1)S(1)}, u32[]{:S(2)}, u32[]{:S(2)}) collective-permute-start(bf16[128,1536]{1,0:T(8,128)(2,1)} %get-tuple-element.40), channel_id=1, source_target_pairs={{0,4},{4,8},{8,12},{12,14},{14,10},{10,6},{6,2},{2,0},{1,5},{5,9},... | collective-permute-start | bytes 1179656 | tf_op jit(solution)/shard_map/ppermute | solution.py:374
  395.6 24.9 %collective-permute-start.31 = (bf16[128,1536]{1,0:T(8,128)(2,1)}, bf16[128,1536]{1,0:T(8,128)(2,1)S(1)}, u32[]{:S(2)}, u32[]{:S(2)}) collective-permute-start(bf16[128,1536]{1,0:T(8,128)(2,1)} %get-tuple-element.41), channel_id=1, source_target_pairs={{0,2},{4,0},{8,4},{12,8},{14,12},{10,14},{6,10},{2,6},{1,3},{5,1},... | collective-permute-start | bytes 1179656 | tf_op jit(solution)/shard_map/ppermute | solution.py:374
  (91 other events, 1347.5 us)

commit v2 on v1

--- a/solution.py
+++ b/solution.py
@@ -8,14 +8,17 @@
 from jax.experimental.pallas import tpu as pltpu
 from jax.sharding import PartitionSpec as P
 
+TILES = (1, 1, 1)
 PIECES = (2, 1)
 SHARES = (3, 3, 2)
 SLOTS = 3
 LANES = 128
 EARLY = 2
+EARLY_BACK = 1
 F32 = jnp.float32
 BF16 = jnp.bfloat16
 VMEM_LIMIT = 60 * 1024 * 1024
+SMALL_LIMIT = 8 * 1024 * 1024
 
 
 def ring_order(members):
@@ -77,6 +80,7 @@
             out_specs=pl.BlockSpec((step, 2 * (high - low)), lambda i, core_ref: (i, 0)),
         ),
         cost_estimate=cost(0, out, out),
+        compiler_params=params(),
         name="cut_columns",
     )(core, *[w_gate] * tiles, *[w_up] * tiles)
 
@@ -100,6 +104,7 @@
             out_specs=[pl.BlockSpec((step, high - low), lambda i, core_ref: (i, 0)) for low, high in bounds],
         ),
         cost_estimate=cost(0, *outs, *outs),
+        compiler_params=params(),
         name="cut_rows",
     )(core, w_down)
 
@@ -202,7 +207,7 @@
         def _():
             finish(totals, extra_refs, out_refs)
 
-    specs = [pl.BlockSpec(memory_space=pl.ANY)] * (count + len(arrays))
+    specs = [pl.BlockSpec(memory_space=pltpu.HBM)] * (count + len(arrays))
     specs += [pl.BlockSpec(a.shape, lambda k: (0, 0), pipeline_mode=pl.Buffered(1)) for a in extras]
     dtype = blocks[0].dtype
     return pl.pallas_call(
@@ -253,6 +258,7 @@
 
 def both_out(owns, pairs, takes, w_down, mine, other, weights, low, split):
     rows = sum(own.shape[0] for own in owns)
+    heights = [2 * split] * (rows // split // 2 - 1) + [split, split]
     units = w_down.shape[0]
     width = mine.shape[1]
     step = math.gcd(math.gcd(low, width), 512)
@@ -260,7 +266,7 @@
     def body(*refs):
         own_refs, refs = refs[: len(owns)], refs[len(owns) :]
         pair_refs, refs = refs[: len(pairs)], refs[len(pairs) :]
-        w_ref, mine_ref, other_ref, weight_own, weight_pair, out_ref, near_ref, far_ref, hidden = refs
+        w_ref, mine_ref, other_ref, weight_own, weight_pair, *out_refs, hidden = refs
 
         @pl.when(pl.program_id(0) == 0)
         def _():
@@ -277,9 +283,10 @@
         total = weight_own[...] * jnp.dot(hidden[0], w_ref[...], preferred_element_type=F32)
         total += weight_pair[...] * jnp.dot(hidden[1], w, preferred_element_type=F32)
         total = total.astype(BF16)
-        out_ref[...] = total
-        near_ref[...] = total[-2 * split : -split]
-        far_ref[...] = total[-split:]
+        done = 0
+        for out_ref in out_refs:
+            out_ref[...] = total[done : done + out_ref.shape[0]]
+            done += out_ref.shape[0]
 
     def columns(height, first=0):
         return pl.BlockSpec((height, step), lambda j: (0, first // step + j))
@@ -287,7 +294,7 @@
     def fixed(a):
         return pl.BlockSpec(a.shape, lambda j: (0, 0), pipeline_mode=pl.Buffered(1))
 
-    outs = [jax.ShapeDtypeStruct((height, width), BF16) for height in (rows, split, split)]
+    outs = [jax.ShapeDtypeStruct((height, width), BF16) for height in heights]
     return pl.pallas_call(
         body,
         out_shape=outs,
@@ -295,62 +302,82 @@
         in_specs=[fixed(a) for a in (*owns, *pairs)]
         + [columns(units, low), columns(mine.shape[0]), columns(mine.shape[0])]
         + [fixed(a) for a in weights],
-        out_specs=[columns(rows), columns(split), columns(split)],
+        out_specs=[columns(height) for height in heights],
         scratch_shapes=[pltpu.VMEM((2, rows, units), BF16)],
         compiler_params=params(),
         cost_estimate=cost(4 * rows * units * width, *outs),
     )(*owns, *pairs, w_down, mine, other, *weights)
 
 
-def hop_sum(total, step, rows, ahead, behind):
-    width = total.shape[1]
+def hop_sum(near, far, ahead, behind):
+    rows, width = near.shape
     split = ahead.shape[0]
 
-    def body(toward_ref, back_ref, ahead_ref, behind_ref, out_toward, out_back):
-        if split == rows:
-            out_toward[...] = (toward_ref[...].astype(F32) + ahead_ref[...].astype(F32)).astype(BF16)
-            out_back[...] = (back_ref[...].astype(F32) + behind_ref[...].astype(F32)).astype(BF16)
-        else:
-            out_toward[:split, :] = toward_ref[:split, :]
-            out_toward[split:, :] = (toward_ref[split:, :].astype(F32) + ahead_ref[...].astype(F32)).astype(BF16)
-            out_back[:split, :] = (back_ref[:split, :].astype(F32) + behind_ref[...].astype(F32)).astype(BF16)
-            out_back[split:, :] = back_ref[split:, :]
+    def body(near_ref, far_ref, ahead_ref, behind_ref, out_toward, out_back, toward, back, fore, aft, sems):
+        sources = (near_ref, far_ref, ahead_ref, behind_ref)
+        copies = [
+            pltpu.make_async_copy(source, target, sems.at[i])
+            for i, (source, target) in enumerate(zip(sources, (toward, back, fore, aft)))
+        ]
+        for copy in copies:
+            copy.start()
+        for copy in copies:
+            copy.wait()
+        low, high = (slice(None), slice(None)) if split == rows else (slice(0, split), slice(split, rows))
+        if split != rows:
+            out_toward[low, :] = toward[low, :]
+            out_back[high, :] = back[high, :]
+        out_toward[high, :] = (toward[high, :].astype(F32) + fore[...].astype(F32)).astype(BF16)
+        out_back[low, :] = (back[low, :].astype(F32) + aft[...].astype(F32)).astype(BF16)
 
     out = jax.ShapeDtypeStruct((rows, width), BF16)
     return pl.pallas_call(
         body,
         out_shape=[out, out],
         grid=(1,),
-        in_specs=[
-            pl.BlockSpec((rows, width), lambda i: (2 * step, 0)),
-            pl.BlockSpec((rows, width), lambda i: (2 * step - 1, 0)),
-            whole(ahead.shape),
-            whole(behind.shape),
+        in_specs=[pl.BlockSpec(memory_space=pltpu.HBM)] * 4,
+        out_specs=[whole(out.shape)] * 2,
+        scratch_shapes=[
+            pltpu.VMEM(out.shape, BF16),
+            pltpu.VMEM(out.shape, BF16),
+            pltpu.VMEM(ahead.shape, BF16),
+            pltpu.VMEM(behind.shape, BF16),
+            pltpu.SemaphoreType.DMA((4,)),
         ],
-        out_specs=[whole(out.shape)] * 2,
-        compiler_params=params(),
+        compiler_params=pltpu.CompilerParams(vmem_limit_bytes=SMALL_LIMIT),
         cost_estimate=cost(0, out, out, out, out),
-    )(total, total, ahead, behind)
+    )(near, far, ahead, behind)
 
 
 def last_sum(chunks, rows, bounds):
     flat = [a for chunk in chunks for a in chunk]
 
     def body(*refs):
-        out_ref = refs[-1]
+        out_ref, held, sems = refs[len(flat) :]
+        copies = []
         for n, (low, high) in enumerate(bounds):
-            own, ahead, behind = refs[3 * n : 3 * n + 3]
-            total = own[...].astype(F32) + ahead[...].astype(F32) + behind[...].astype(F32)
-            out_ref[:, low:high] = total.astype(BF16)
+            for i, ref in enumerate(refs[3 * n : 3 * n + 3]):
+                source = ref.at[pl.ds(0, rows), :]
+                copies.append(pltpu.make_async_copy(source, held.at[i, :, pl.ds(low, high - low)], sems.at[n, i]))
+        for copy in copies:
+            copy.start()
+        for copy in copies:
+            copy.wait()
+        total = held[0].astype(F32) + held[1].astype(F32) + held[2].astype(F32)
+        out_ref[...] = total.astype(BF16)
 
     out = jax.ShapeDtypeStruct((rows, bounds[-1][1]), BF16)
     return pl.pallas_call(
         body,
         out_shape=out,
         grid=(1,),
-        in_specs=[pl.BlockSpec((rows, a.shape[1]), lambda i: (0, 0)) for a in flat],
+        in_specs=[pl.BlockSpec(memory_space=pltpu.HBM)] * len(flat),
         out_specs=whole(out.shape),
-        compiler_params=params(),
+        scratch_shapes=[
+            pltpu.VMEM((3, *out.shape), BF16),
+            pltpu.SemaphoreType.DMA((len(bounds), 3)),
+        ],
+        compiler_params=pltpu.CompilerParams(vmem_limit_bytes=SMALL_LIMIT),
         cost_estimate=cost(0, out, out, out, out),
     )(*flat)
 
@@ -392,10 +419,10 @@
     first = rep * half_units
     core = jnp.full((1,), rep, jnp.int32)
     projections = []
-    for low, high in pieces:
+    for low, high in bounds_of(half_units, TILES):
         cut = cut_columns(core, w_gate, w_up, low, high)
         mine = go(cut, pair)
-        projections.append((mine, swap(mine)))
+        projections.append((low, high, mine, swap(mine)))
     bounds = bounds_of(width, SHARES)
     cuts = cut_rows(core, w_down, bounds)
     downs = []
@@ -459,48 +486,61 @@
 
     pairs = []
     for piece, (low, high) in enumerate(pieces):
-        size = 2 * (high - low)
+        size = high - low
+        parts = []
+        for start, stop, *arrays in projections:
+            if low <= start < high:
+                for side, array in enumerate(arrays):
+                    for half in range(2):
+                        take = slice(half * (stop - start), (half + 1) * (stop - start))
+                        parts.append(([(array, width)], take, (2 * side + half) * size + start - low))
         (hidden,) = contract(
-            token_blocks,
-            [[([(w, width)], slice(0, size), side * size) for side, w in enumerate(projections[piece])]],
-            False, [scales[piece]], [shape(total_rows, size, BF16)], finish_pair,
+            token_blocks, [parts], False, [scales[piece]], [shape(total_rows, 2 * size, BF16)],
+            finish_pair,
         )
         pairs.append(hidden)
     takes = [slice(low, high) for low, high in pieces]
 
     mixed = []
     for chunk, (low, high) in enumerate(bounds):
-        total, behind, ahead = both_out(
+        *blocks, behind, ahead = both_out(
             owns, pairs, takes, w_down, *downs[chunk], (weight_own, weight_pair), low, split
         )
         ahead = go(ahead, forward)
         behind = go(behind, backward)
         for step in range(full, 0, -1):
-            toward, back = hop_sum(total, step, rows, ahead, behind)
+            toward, back = hop_sum(blocks[2 * step], blocks[2 * step - 1], ahead, behind)
             ahead = go(toward, forward)
             behind = go(back, backward)
-        mixed.append((total, ahead, behind))
+        mixed.append((blocks[0], ahead, behind))
     mixed = last_sum(mixed, rows, bounds)
 
-    grad_own, grad_pair = 0.0, 0.0
-    for n, group in enumerate((cotangent_blocks[:early], cotangent_blocks[early:])):
+    grad_own = 0.0
+    early_back = 1 + 4 * EARLY_BACK
+    middle = rows * (1 + 2 * EARLY_BACK)
+    for n, (group, span) in enumerate(
+        (
+            (cotangent_blocks[:early_back], slice(0, middle)),
+            (cotangent_blocks[early_back:], slice(middle, total_rows)),
+        )
+    ):
+        hidden_rows = owns[0] if n == 0 else jnp.concatenate([owns[0][middle:], owns[1]])
         (grad,) = contract(
             group, [[([(w_down, width)], everything, 0)]], True,
-            [weight_own[spans[n]], ia3_scale, owns[n]], [shape(1, units)],
-            functools.partial(finish_grad, slice(None)),
+            [weight_own[span], ia3_scale, hidden_rows], [shape(1, units)],
+            functools.partial(finish_grad, slice(0, span.stop - span.start)),
         )
         grad_own += grad
-        parts, place = [], 0
-        for low, high in pieces:
-            for side in range(2):
-                segments = [(down[side], down[side].shape[1]) for down in downs]
-                parts.append((segments, slice(low, high), place))
-                place += high - low
-        (grad,) = contract(
-            group, [parts], True, [weight_pair[spans[n]], scale_pair, *pairs], [shape(1, units)],
-            functools.partial(finish_grad, spans[n]),
-        )
-        grad_pair += grad
+    parts, place = [], 0
+    for low, high in pieces:
+        for side in range(2):
+            segments = [(down[side], down[side].shape[1]) for down in downs]
+            parts.append((segments, slice(low, high), place))
+            place += high - low
+    (grad_pair,) = contract(
+        cotangent_blocks, [parts], True, [weight_pair, scale_pair, *pairs], [shape(1, units)],
+        functools.partial(finish_grad, slice(None)),
+    )
     sides, at = ([], []), 0
     for low, high in pieces:
         for side in range(2):

time: 429 us -> 419 us (0.977)
  Pallas kernels: 154 us -> 138 us
  waiting for transfers between devices: 181 us -> 191 us
  local copies, waits for them, and re-layouts: 16 us -> 10.3 us
    pallas_call x9, Pallas kernels: 19.8 us -> 9.06 us  [hop_sum(): pl.pallas_call(body, out_shape=[out, out], grid=(1,), in_specs=[pl.BlockS...]
    ppermute x62 -> x63, waiting for transfers between devices: 181 us -> 191 us  [go(): return lax.ppermute(value, 'exp', perm)]
    unnamed x120 -> x88, local copies, waits for them, and re-layouts: 11.2 us -> 2.74 us
    pallas_call x8 -> x7, Pallas kernels: 91.3 us -> 84.6 us  [contract(): pl.pallas_call(body, out_shape=outs, grid=(steps,), in_specs=specs, out_s...]
    pallas_call x2 -> x3, Pallas kernels: 8.96 us -> 11.9 us  [cut_columns(): pl.pallas_call(body, out_shape=out, grid_spec=pltpu.PrefetchScalarGridSpe...]
    ppermute x62 -> x63, starting transfers between devices: 68.5 us -> 67.8 us  [go(): return lax.ppermute(value, 'exp', perm)]
  transfers between devices with their start and end apart: 68 -> 70, of which waited for: 19 -> 19; matrix products, arithmetic and copies ran while one was open for 3% -> 3% of each run, Pallas kernels for 34% -> 33%
where the time goes in v2:
time: 419 us; the launch traced here: 415 us
  waiting for transfers between devices  191 us (46%)
  Pallas kernels  138 us (33%)
  starting transfers between devices  68.4 us (16%)
  local copies, waits for them, and re-layouts  10.3 us (2%)
  other arithmetic  5.56 us (1%)
    ppermute x63, waiting for transfers between devices, go(): return lax.ppermute(value, 'exp', perm)  191 us
    pallas_call x7, Pallas kernels, contract(): pl.pallas_call(body, out_shape=outs, grid=(steps,), in_specs=specs, out_s...  84.6 us
    ppermute x63, starting transfers between devices, go(): return lax.ppermute(value, 'exp', perm)  67.8 us
    pallas_call x3, Pallas kernels, both_out(): pl.pallas_call(body, out_shape=outs, grid=(width // step,), in_specs=[fix...  26.2 us
    pallas_call x3, Pallas kernels, cut_columns(): pl.pallas_call(body, out_shape=out, grid_spec=pltpu.PrefetchScalarGridSpe...  11.9 us
    pallas_call x9, Pallas kernels, hop_sum(): pl.pallas_call(body, out_shape=[out, out], grid=(1,), in_specs=[pl.BlockS...  9.06 us
  transfers between devices with their start and end apart: 70, of which 19 were waited for; matrix products, arithmetic and copies ran while one was open for 3% of the time, Pallas kernels for 33%

profile of v2, /device:TPU:12, one launch (start us, length us, event | category | flops | bytes accessed | tf_op | source)
XLA Modules:
  0.0 414.6 jit_solution(15345119841773050531)
XLA Ops:
  2.0 3.1 collective-permute-done.23
  12.0 2.7 collective-permute-start.25
  15.7 18.7 %collective-permute-done.25 = bf16[4,16,128]{2,1,0:T(8,128)(2,1)S(1)} collective-permute-done((bf16[4,16,128]{2,1,0:T(8,128)(2,1)S(1)}, bf16[4,16,128]{2,1,0:T(8,128)(2,1)S(1)}, u32[]{:S(2)}, u32[]{:S(2)}) %collective-permute-start.25) | collective-permute-done | bytes 16416 | tf_op jit(solution)/shard_map/ppermute | solution.py:401
  34.5 2.1 collective-permute-start.56
  36.5 4.4 %cut_rows.1 = (bf16[384,1536]{1,0:T(8,128)(2,1)}, bf16[384,1536]{1,0:T(8,128)(2,1)}, bf16[384,1024]{1,0:T(8,128)(2,1)}) custom-call(s32[1]{0:T(128)} %bitcast.2.core_ref, bf16[768,4096]{1,0:T(8,128)(2,1)} %bitcast.38), custom_call_target="tpu_custom_call" | custom-call | bytes 6291456 | tf_op jit(solution)/shard_map/cut_rows/pallas_call | solution.py:97
  42.5 3.9 cut_columns.3
  46.4 4.1 cut_columns.4
  52.6 3.1 collective-permute-done.55.refs_2_
  57.7 3.9 cut_columns.5
  61.6 3.4 collective-permute-done.57.refs_4_
  70.8 8.2 %collective-permute-done.5.refs_6_ = bf16[64,4096]{1,0:T(8,128)(2,1)} collective-permute-done((bf16[64,4096]{1,0:T(8,128)(2,1)}, bf16[64,4096]{1,0:T(8,128)(2,1)}, u32[]{:S(2)}, u32[]{:S(2)}) %collective-permute-start.5) | collective-permute-done | bytes 524320 | tf_op jit(solution)/shard_map/ppermute | solution.py:401
  81.6 7.2 %collective-permute-done.7.refs_8_ = bf16[64,4096]{1,0:T(8,128)(2,1)S(1)} collective-permute-done((bf16[64,4096]{1,0:T(8,128)(2,1)}, bf16[64,4096]{1,0:T(8,128)(2,1)S(1)}, u32[]{:S(2)}, u32[]{:S(2)}) %collective-permute-start.7) | collective-permute-done | bytes 524320 | tf_op jit(solution)/shard_map/ppermute | solution.py:401
  94.1 12.6 %collective-permute-done.14.refs_15_ = bf16[4096,256]{1,0:T(8,128)(2,1)} collective-permute-done((bf16[4096,256]{1,0:T(8,128)(2,1)S(1)}, bf16[4096,256]{1,0:T(8,128)(2,1)}, u32[]{:S(2)}, u32[]{:S(2)}) %collective-permute-start.14) | collective-permute-done | bytes 2097184 | tf_op jit(solution)/shard_map/ppermute | solution.py:401
  106.7 44.9 %collective-permute-done.16.refs_17_ = bf16[4096,256]{1,0:T(8,128)(2,1)} collective-permute-done((bf16[4096,256]{1,0:T(8,128)(2,1)}, bf16[4096,256]{1,0:T(8,128)(2,1)}, u32[]{:S(2)}, u32[]{:S(2)}) %collective-permute-start.16) | collective-permute-done | bytes 2097184 | tf_op jit(solution)/shard_map/ppermute | solution.py:401
  153.3 2.0 collective-permute-start.11
  155.5 35.4 %collective-permute-done.19.refs_15_ = bf16[4096,256]{1,0:T(8,128)(2,1)} collective-permute-done((bf16[4096,256]{1,0:T(8,128)(2,1)}, bf16[4096,256]{1,0:T(8,128)(2,1)}, u32[]{:S(2)}, u32[]{:S(2)}) %collective-permute-start.19) | collective-permute-done | bytes 2097184 | tf_op jit(solution)/shard_map/ppermute | solution.py:401
  198.6 14.6 %shard_map.122.refs_0_.refs_8_ = bf16[640,768]{1,0:T(8,128)(2,1)} custom-call(bf16[128,4096]{1,0:T(8,128)(2,1)} %refs_0_.7, bf16[64,4096]{1,0:T(8,128)(2,1)} %collective-permute-done.refs_1_, bf16[64,4096]{1,0:T(8,128)(2,1)} %copy-done.33, bf16[64,4096]{1,0:T(8,128)(2,1)} %copy-done.32, bf16[64,4096]{1,0:T(8,128)(2,1)} %collective-permute-done.3.refs_4_, ...), custom_call_target="tpu_custom_call" | custom-call | flops 8053063680 | bytes 983040 | tf_op jit(solution)/shard_map/pallas_call | solution.py:213
  213.9 10.5 %shard_map.123.refs_1_ = bf16[384,768]{1,0:T(8,128)(2,1)} custom-call(bf16[64,4096]{1,0:T(8,128)(2,1)} %copy-done.35, bf16[64,4096]{1,0:T(8,128)(2,1)} %collective-permute-done.9.refs_1_.refs_10_, bf16[64,4096]{1,0:T(8,128)(2,1)} %collective-permute-done.10.refs_2_.refs_11_, bf16[64,4096]{1,0:T(8,128)(2,1)} %copy-done.36, ...), custom_call_target="tpu_custom_call" | custom-call | flops 4831838208 | bytes 589824 | tf_op jit(solution)/shard_map/pallas_call | solution.py:213
  226.7 15.4 %shard_map.124.refs_2_.refs_23_ = bf16[1024,512]{1,0:T(8,128)(2,1)} custom-call(bf16[128,4096]{1,0:T(8,128)(2,1)} %refs_0_.7, bf16[64,4096]{1,0:T(8,128)(2,1)} %collective-permute-done.refs_1_, bf16[64,4096]{1,0:T(8,128)(2,1)} %copy-done.33, bf16[64,4096]{1,0:T(8,128)(2,1)} %copy-done.32, bf16[64,4096]{1,0:T(8,128)(2,1)} %collective-permute-done.3.refs_4_, ...), custom_call_target="tpu_custom_call" | custom-call | flops 8589934592 | bytes 1048576 | tf_op jit(solution)/shard_map/pallas_call | solution.py:213
  242.2 7.5 %collective-permute-done.34.refs_5_.refs_16_ = bf16[384,1536]{1,0:T(8,128)(2,1)} collective-permute-done((bf16[384,1536]{1,0:T(8,128)(2,1)S(1)}, bf16[384,1536]{1,0:T(8,128)(2,1)}, u32[]{:S(2)}, u32[]{:S(2)}) %collective-permute-start.34) | collective-permute-done | bytes 1179680 | tf_op jit(solution)/shard_map/ppermute | solution.py:401
  250.1 10.3 %shard_map.125.refs_3_.refs_24_ = bf16[1024,256]{1,0:T(8,128)(2,1)} custom-call(bf16[128,4096]{1,0:T(8,128)(2,1)} %refs_0_.7, bf16[64,4096]{1,0:T(8,128)(2,1)} %collective-permute-done.refs_1_, bf16[64,4096]{1,0:T(8,128)(2,1)} %copy-done.33, bf16[64,4096]{1,0:T(8,128)(2,1)} %copy-done.32, bf16[64,4096]{1,0:T(8,128)(2,1)} %collective-permute-done.3.refs_4_, ...), custom_call_target="tpu_custom_call" | custom-call | flops 4294967296 | bytes 524288 | tf_op jit(solution)/shard_map/pallas_call | solution.py:213
  262.9 9.3 %shard_map.126 = (bf16[128,1536]{1,0:T(8,128)(2,1)}, bf16[128,1536]{1,0:T(8,128)(2,1)}, bf16[128,1536]{1,0:T(8,128)(2,1)}, bf16[128,1536]{1,0:T(8,128)(2,1)}, bf...) custom-call(bf16[640,768]{1,0:T(8,128)(2,1)} %shard_map.122.refs_0_., ...), custom_call_target="tpu_custom_call" | custom-call | flops 4831838208 | bytes 3145728 | tf_op jit(solution)/shard_map/pallas_call | solution.py:298
  274.0 7.5 %shard_map.134 = (bf16[128,1024]{1,0:T(8,128)(2,1)}, bf16[128,1024]{1,0:T(8,128)(2,1)}, bf16[128,1024]{1,0:T(8,128)(2,1)}, bf16[128,1024]{1,0:T(8,128)(2,1)}, bf...) custom-call(bf16[640,768]{1,0:T(8,128)(2,1)} %shard_map.122.refs_0_., ...), custom_call_target="tpu_custom_call" | custom-call | flops 3221225472 | bytes 2097152 | tf_op jit(solution)/shard_map/pallas_call | solution.py:298
  283.0 3.9 collective-permute-done.62.refs_4_.refs_9_
  288.3 8.7 %shard_map.139 = f32[1,768]{1,0:T(1,128)} custom-call(bf16[128,4096]{1,0:T(8,128)(2,1)} %refs_0_.9, bf16[64,4096]{1,0:T(8,128)(2,1)} %collective-permute-done.54.refs_1_, bf16[64,4096]{1,0:T(8,128)(2,1)} %collective-permute-done.55.refs_2_, bf16[64,4096]{1,0:T(8,128)(2,1)} %collective-permute-done.56.refs_3_, bf16[64,4096]{1,0:T(8,128)(2,1)} %copy-done.27, ...), custom_call_target="tpu_custom_call" | custom-call | flops 2415919104 | bytes 3072 | tf_op jit(solution)/shard_map/pallas_call | solution.py:213
  302.8 9.4 %shard_map.130 = (bf16[128,1536]{1,0:T(8,128)(2,1)}, bf16[128,1536]{1,0:T(8,128)(2,1)}, bf16[128,1536]{1,0:T(8,128)(2,1)}, bf16[128,1536]{1,0:T(8,128)(2,1)}, bf...) custom-call(bf16[640,768]{1,0:T(8,128)(2,1)} %shard_map.122.refs_0_., ...), custom_call_target="tpu_custom_call" | custom-call | flops 4831838208 | bytes 3145728 | tf_op jit(solution)/shard_map/pallas_call | solution.py:298
  312.7 12.3 %collective-permute-done.27.behind_ref = bf16[64,1536]{1,0:T(8,128)(2,1)S(1)} collective-permute-done((bf16[64,1536]{1,0:T(8,128)(2,1)S(1)}, bf16[64,1536]{1,0:T(8,128)(2,1)S(1)}, u32[]{:S(2)}, u32[]{:S(2)}) %collective-permute-start.27) | collective-permute-done | bytes 196640 | tf_op jit(solution)/shard_map/ppermute | solution.py:401
  331.5 14.2 %shard_map.141 = f32[1,768]{1,0:T(1,128)} custom-call(bf16[128,4096]{1,0:T(8,128)(2,1)} %refs_0_.9, bf16[64,4096]{1,0:T(8,128)(2,1)} %collective-permute-done.54.refs_1_, bf16[64,4096]{1,0:T(8,128)(2,1)} %collective-permute-done.55.refs_2_, bf16[64,4096]{1,0:T(8,128)(2,1)} %collective-permute-done.56.refs_3_, bf16[64,4096]{1,0:T(8,128)(2,1)} %copy-done.27, ...), custom_call_target="tpu_custom_call" | custom-call | flops 6442450944 | bytes 3072 | tf_op jit(solution)/shard_map/pallas_call | solution.py:213
  354.2 3.5 collective-permute-done.29.behind_ref
  361.5 4.7 %collective-permute-done.39.behind_ref = bf16[128,1536]{1,0:T(8,128)(2,1)S(1)} collective-permute-done((bf16[128,1536]{1,0:T(8,128)(2,1)S(1)}, bf16[128,1536]{1,0:T(8,128)(2,1)S(1)}, u32[]{:S(2)}, u32[]{:S(2)}) %collective-permute-start.39) | collective-permute-done | bytes 393248 | tf_op jit(solution)/shard_map/ppermute | solution.py:401
  373.5 10.8 %shard_map.140 = f32[1,768]{1,0:T(1,128)} custom-call(bf16[64,4096]{1,0:T(8,128)(2,1)} %collective-permute-done.58.refs_0_.refs_5_, bf16[64,4096]{1,0:T(8,128)(2,1)} %collective-permute-done.59.refs_1_.refs_6_, bf16[64,4096]{1,0:T(8,128)(2,1)} %collective-permute-done.60.refs_2_.refs_7_, bf16[64,4096]{1,0:T(8,128)(2,1)} %collective-permute-done.61.refs_3_.refs_8_, ...), custom_call_target="tpu_custom_call" | custom-call | flops 4026531840 | bytes 3072 | tf_op jit(solution)/shard_map/pallas_call | solution.py:213
  394.2 18.5 %collective-permute-done.53.refs_8_ = bf16[128,1024]{1,0:T(8,128)(2,1)S(1)} collective-permute-done((bf16[128,1024]{1,0:T(8,128)(2,1)S(1)}, bf16[128,1024]{1,0:T(8,128)(2,1)S(1)}, u32[]{:S(2)}, u32[]{:S(2)}) %collective-permute-start.53) | collective-permute-done | bytes 262176 | tf_op jit(solution)/shard_map/ppermute | solution.py:401
  (251 shorter events, 92.4 us)
Async XLA Ops:
  6.9 27.6 %collective-permute-start = (bf16[64,4096]{1,0:T(8,128)(2,1)S(1)}, bf16[64,4096]{1,0:T(8,128)(2,1)}, u32[]{:S(2)}, u32[]{:S(2)}) collective-permute-start(bf16[64,4096]{1,0:T(8,128)(2,1)S(1)} %get-tuple-element.103), channel_id=1, source_target_pairs={{0,4},{4,8},{8,12},{12,14},{14,10},{10,6},{6,2},{2,0},{1,5},{5,9},... | collective-permute-start | bytes 1572872 | tf_op jit(solution)/shard_map/ppermute | solution.py:401
  8.5 32.4 %collective-permute-start.2 = (bf16[64,4096]{1,0:T(8,128)(2,1)S(1)}, bf16[64,4096]{1,0:T(8,128)(2,1)S(1)}, u32[]{:S(2)}, u32[]{:S(2)}) collective-permute-start(bf16[64,4096]{1,0:T(8,128)(2,1)S(1)} %get-tuple-element.103), channel_id=1, source_target_pairs={{0,2},{4,0},{8,4},{12,8},{14,12},{10,14},{6,10},{2,6},{1,3},{5,1},... | collective-permute-start | bytes 1572872 | tf_op jit(solution)/shard_map/ppermute | solution.py:401
  9.7 24.8 %collective-permute-start.1 = (bf16[64,4096]{1,0:T(8,128)(2,1)S(1)}, bf16[64,4096]{1,0:T(8,128)(2,1)S(1)}, u32[]{:S(2)}, u32[]{:S(2)}) collective-permute-start(bf16[64,4096]{1,0:T(8,128)(2,1)S(1)} %get-tuple-element.102), channel_id=1, source_target_pairs={{0,4},{4,8},{8,12},{12,14},{14,10},{10,6},{6,2},{2,0},{1,5},{5,9},... | collective-permute-start | bytes 1572872 | tf_op jit(solution)/shard_map/ppermute | solution.py:401
  15.7 34.8 %collective-permute-start.3 = (bf16[64,4096]{1,0:T(8,128)(2,1)S(1)}, bf16[64,4096]{1,0:T(8,128)(2,1)}, u32[]{:S(2)}, u32[]{:S(2)}) collective-permute-start(bf16[64,4096]{1,0:T(8,128)(2,1)S(1)} %get-tuple-element.102), channel_id=1, source_target_pairs={{0,2},{4,0},{8,4},{12,8},{14,12},{10,14},{6,10},{2,6},{1,3},{5,1},... | collective-permute-start | bytes 1572872 | tf_op jit(solution)/shard_map/ppermute | solution.py:401
  40.9 26.2 %collective-permute-start.44 = (bf16[384,1024]{1,0:T(8,128)(2,1)}, bf16[384,1024]{1,0:T(8,128)(2,1)S(1)}, u32[]{:S(2)}, u32[]{:S(2)}) collective-permute-start(bf16[384,1024]{1,0:T(8,128)(2,1)} %get-tuple-element.82), channel_id=1, source_target_pairs={{0,1},{1,0},{2,3},{3,2},{4,5},{5,4},{6,7},{7,6},{8,9},{9,8},{10,11... | collective-permute-start | bytes 2359304 | tf_op jit(solution)/shard_map/ppermute | solution.py:401
  50.5 56.2 %collective-permute-start.14 = (bf16[4096,256]{1,0:T(8,128)(2,1)S(1)}, bf16[4096,256]{1,0:T(8,128)(2,1)}, u32[]{:S(2)}, u32[]{:S(2)}) collective-permute-start(bf16[4096,256]{1,0:T(8,128)(2,1)S(1)} %copy-done.24), channel_id=1, source_target_pairs={{0,1},{1,0},{2,3},{3,2},{4,5},{5,4},{6,7},{7,6},{8,9},{9,8},{10,11... | collective-permute-start | bytes 6291464 | tf_op jit(solution)/shard_map/ppermute | solution.py:401
  51.3 100.3 %collective-permute-start.16 = (bf16[4096,256]{1,0:T(8,128)(2,1)}, bf16[4096,256]{1,0:T(8,128)(2,1)}, u32[]{:S(2)}, u32[]{:S(2)}) collective-permute-start(bf16[4096,256]{1,0:T(8,128)(2,1)} %cut_columns.4), channel_id=1, source_target_pairs={{0,1},{1,0},{2,3},{3,2},{4,5},{5,4},{6,7},{7,6},{8,9},{9,8},{10,11... | collective-permute-start | bytes 6291464 | tf_op jit(solution)/shard_map/ppermute | solution.py:401
  65.1 125.9 %collective-permute-start.19 = (bf16[4096,256]{1,0:T(8,128)(2,1)}, bf16[4096,256]{1,0:T(8,128)(2,1)}, u32[]{:S(2)}, u32[]{:S(2)}) collective-permute-start(bf16[4096,256]{1,0:T(8,128)(2,1)} %cut_columns.5), channel_id=1, source_target_pairs={{0,1},{1,0},{2,3},{3,2},{4,5},{5,4},{6,7},{7,6},{8,9},{9,8},{10,11... | collective-permute-start | bytes 6291464 | tf_op jit(solution)/shard_map/ppermute | solution.py:401
  88.7 64.6 %collective-permute-start.9 = (bf16[64,4096]{1,0:T(8,128)(2,1)}, bf16[64,4096]{1,0:T(8,128)(2,1)}, u32[]{:S(2)}, u32[]{:S(2)}) collective-permute-start(bf16[64,4096]{1,0:T(8,128)(2,1)} %collective-permute-done.5.refs_6_), channel_id=1, source_target_pairs={{0,4},{4,8},{8,12},{12,14},{14,10},{10,6},{6,2},{2,0},{1,5},{5,9},... | collective-permute-start | bytes 1572872 | tf_op jit(solution)/shard_map/ppermute | solution.py:401
  92.5 62.8 %collective-permute-start.10 = (bf16[64,4096]{1,0:T(8,128)(2,1)}, bf16[64,4096]{1,0:T(8,128)(2,1)}, u32[]{:S(2)}, u32[]{:S(2)}) collective-permute-start(bf16[64,4096]{1,0:T(8,128)(2,1)} %collective-permute-done.6.refs_7_), channel_id=1, source_target_pairs={{0,2},{4,0},{8,4},{12,8},{14,12},{10,14},{6,10},{2,6},{1,3},{5,1},... | collective-permute-start | bytes 1572872 | tf_op jit(solution)/shard_map/ppermute | solution.py:401
  106.7 118.4 %collective-permute-start.15 = (bf16[4096,256]{1,0:T(8,128)(2,1)}, bf16[4096,256]{1,0:T(8,128)(2,1)}, u32[]{:S(2)}, u32[]{:S(2)}) collective-permute-start(bf16[4096,256]{1,0:T(8,128)(2,1)} %collective-permute-done.14.refs_15_), channel_id=1, source_target_pairs={{0,16},{16,0},{1,17},{17,1},{2,18},{18,2},{3,19},{19,3},{4,20},{20... | collective-permute-start | bytes 6291464 | tf_op jit(solution)/shard_map/ppermute | solution.py:404
  151.6 75.1 %collective-permute-start.17 = (bf16[4096,256]{1,0:T(8,128)(2,1)}, bf16[4096,256]{1,0:T(8,128)(2,1)}, u32[]{:S(2)}, u32[]{:S(2)}) collective-permute-start(bf16[4096,256]{1,0:T(8,128)(2,1)} %collective-permute-done.16.refs_17_), channel_id=1, source_target_pairs={{0,16},{16,0},{1,17},{17,1},{2,18},{18,2},{3,19},{19,3},{4,20},{20... | collective-permute-start | bytes 6291464 | tf_op jit(solution)/shard_map/ppermute | solution.py:404
  153.3 41.5 %collective-permute-start.11 = (bf16[64,4096]{1,0:T(8,128)(2,1)}, bf16[64,4096]{1,0:T(8,128)(2,1)S(1)}, u32[]{:S(2)}, u32[]{:S(2)}) collective-permute-start(bf16[64,4096]{1,0:T(8,128)(2,1)} %copy-done.34), channel_id=1, source_target_pairs={{0,2},{4,0},{8,4},{12,8},{14,12},{10,14},{6,10},{2,6},{1,3},{5,1},... | collective-permute-start | bytes 1572872 | tf_op jit(solution)/shard_map/ppermute | solution.py:401
  155.3 41.8 %collective-permute-start.12 = (bf16[64,4096]{1,0:T(8,128)(2,1)}, bf16[64,4096]{1,0:T(8,128)(2,1)}, u32[]{:S(2)}, u32[]{:S(2)}) collective-permute-start(bf16[64,4096]{1,0:T(8,128)(2,1)} %copy-done.35), channel_id=1, source_target_pairs={{0,4},{4,8},{8,12},{12,14},{14,10},{10,6},{6,2},{2,0},{1,5},{5,9},... | collective-permute-start | bytes 1572872 | tf_op jit(solution)/shard_map/ppermute | solution.py:401
  190.9 58.7 %collective-permute-start.20 = (bf16[4096,256]{1,0:T(8,128)(2,1)}, bf16[4096,256]{1,0:T(8,128)(2,1)}, u32[]{:S(2)}, u32[]{:S(2)}) collective-permute-start(bf16[4096,256]{1,0:T(8,128)(2,1)} %collective-permute-done.19.refs_15_), channel_id=1, source_target_pairs={{0,16},{16,0},{1,17},{17,1},{2,18},{18,2},{3,19},{19,3},{4,20},{20... | collective-permute-start | bytes 6291464 | tf_op jit(solution)/shard_map/ppermute | solution.py:404
  195.6 29.1 %collective-permute-start.21 = (bf16[384,1536]{1,0:T(8,128)(2,1)}, bf16[384,1536]{1,0:T(8,128)(2,1)S(1)}, u32[]{:S(2)}, u32[]{:S(2)}) collective-permute-start(bf16[384,1536]{1,0:T(8,128)(2,1)} %get-tuple-element.50), channel_id=1, source_target_pairs={{0,1},{1,0},{2,3},{3,2},{4,5},{5,4},{6,7},{7,6},{8,9},{9,8},{10,11... | collective-permute-start | bytes 3538952 | tf_op jit(solution)/shard_map/ppermute | solution.py:401
  213.3 36.4 %collective-permute-start.34 = (bf16[384,1536]{1,0:T(8,128)(2,1)S(1)}, bf16[384,1536]{1,0:T(8,128)(2,1)}, u32[]{:S(2)}, u32[]{:S(2)}) collective-permute-start(bf16[384,1536]{1,0:T(8,128)(2,1)S(1)} %copy-done.30), channel_id=1, source_target_pairs={{0,1},{1,0},{2,3},{3,2},{4,5},{5,4},{6,7},{7,6},{8,9},{9,8},{10,11... | collective-permute-start | bytes 3538952 | tf_op jit(solution)/shard_map/ppermute | solution.py:401
  224.7 35.8 %collective-permute-start.58 = (bf16[64,4096]{1,0:T(8,128)(2,1)}, bf16[64,4096]{1,0:T(8,128)(2,1)}, u32[]{:S(2)}, u32[]{:S(2)}) collective-permute-start(bf16[64,4096]{1,0:T(8,128)(2,1)} %collective-permute-done.54.refs_1_), channel_id=1, source_target_pairs={{0,4},{4,8},{8,12},{12,14},{14,10},{10,6},{6,2},{2,0},{1,5},{5,9},... | collective-permute-start | bytes 1572872 | tf_op jit(solution)/shard_map/ppermute | solution.py:401
  225.1 35.8 %collective-permute-start.61 = (bf16[64,4096]{1,0:T(8,128)(2,1)S(1)}, bf16[64,4096]{1,0:T(8,128)(2,1)}, u32[]{:S(2)}, u32[]{:S(2)}) collective-permute-start(bf16[64,4096]{1,0:T(8,128)(2,1)S(1)} %collective-permute-done.57.refs_4_), channel_id=1, source_target_pairs={{0,2},{4,0},{8,4},{12,8},{14,12},{10,14},{6,10},{2,6},{1,3},{5,1},... | collective-permute-start | bytes 1572872 | tf_op jit(solution)/shard_map/ppermute | solution.py:401
  226.7 35.8 %collective-permute-start.22 = (bf16[384,1536]{1,0:T(8,128)(2,1)S(1)}, bf16[384,1536]{1,0:T(8,128)(2,1)}, u32[]{:S(2)}, u32[]{:S(2)}) collective-permute-start(bf16[384,1536]{1,0:T(8,128)(2,1)S(1)} %collective-permute-done.21.refs_5_.refs_15_), channel_id=1, source_target_pairs={{0,16},{16,0},{1,17},{17,1},{2,18},{18,2},{3,19},{19,3},{4,20},{20... | collective-permute-start | bytes 3538952 | tf_op jit(solution)/shard_map/ppermute | solution.py:404
  249.6 48.1 %collective-permute-start.35 = (bf16[384,1536]{1,0:T(8,128)(2,1)}, bf16[384,1536]{1,0:T(8,128)(2,1)}, u32[]{:S(2)}, u32[]{:S(2)}) collective-permute-start(bf16[384,1536]{1,0:T(8,128)(2,1)} %collective-permute-done.34.refs_5_.refs_16_), channel_id=1, source_target_pairs={{0,16},{16,0},{1,17},{17,1},{2,18},{18,2},{3,19},{19,3},{4,20},{20... | collective-permute-start | bytes 3538952 | tf_op jit(solution)/shard_map/ppermute | solution.py:404
  262.6 24.3 %collective-permute-start.62 = (bf16[64,4096]{1,0:T(8,128)(2,1)}, bf16[64,4096]{1,0:T(8,128)(2,1)}, u32[]{:S(2)}, u32[]{:S(2)}) collective-permute-start(bf16[64,4096]{1,0:T(8,128)(2,1)} %collective-permute-done.58.refs_0_.refs_5_), channel_id=1, source_target_pairs={{0,4},{4,8},{8,12},{12,14},{14,10},{10,6},{6,2},{2,0},{1,5},{5,9},... | collective-permute-start | bytes 1572872 | tf_op jit(solution)/shard_map/ppermute | solution.py:401
  272.3 24.8 %collective-permute-start.65 = (bf16[64,4096]{1,0:T(8,128)(2,1)}, bf16[64,4096]{1,0:T(8,128)(2,1)}, u32[]{:S(2)}, u32[]{:S(2)}) collective-permute-start(bf16[64,4096]{1,0:T(8,128)(2,1)} %collective-permute-done.61.refs_3_.refs_8_), channel_id=1, source_target_pairs={{0,2},{4,0},{8,4},{12,8},{14,12},{10,14},{6,10},{2,6},{1,3},{5,1},... | collective-permute-start | bytes 1572872 | tf_op jit(solution)/shard_map/ppermute | solution.py:401
  297.1 30.0 %collective-permute-start.63 = (bf16[64,4096]{1,0:T(8,128)(2,1)}, bf16[64,4096]{1,0:T(8,128)(2,1)}, u32[]{:S(2)}, u32[]{:S(2)}) collective-permute-start(bf16[64,4096]{1,0:T(8,128)(2,1)} %collective-permute-done.59.refs_1_.refs_6_), channel_id=1, source_target_pairs={{0,4},{4,8},{8,12},{12,14},{14,10},{10,6},{6,2},{2,0},{1,5},{5,9},... | collective-permute-start | bytes 1572872 | tf_op jit(solution)/shard_map/ppermute | solution.py:401
  297.7 31.0 %collective-permute-start.64 = (bf16[64,4096]{1,0:T(8,128)(2,1)}, bf16[64,4096]{1,0:T(8,128)(2,1)}, u32[]{:S(2)}, u32[]{:S(2)}) collective-permute-start(bf16[64,4096]{1,0:T(8,128)(2,1)} %collective-permute-done.60.refs_2_.refs_7_), channel_id=1, source_target_pairs={{0,2},{4,0},{8,4},{12,8},{14,12},{10,14},{6,10},{2,6},{1,3},{5,1},... | collective-permute-start | bytes 1572872 | tf_op jit(solution)/shard_map/ppermute | solution.py:401
  299.2 30.0 %collective-permute-start.66 = (bf16[64,4096]{1,0:T(8,128)(2,1)}, bf16[64,4096]{1,0:T(8,128)(2,1)}, u32[]{:S(2)}, u32[]{:S(2)}) collective-permute-start(bf16[64,4096]{1,0:T(8,128)(2,1)} %collective-permute-done.62.refs_4_.refs_9_), channel_id=1, source_target_pairs={{0,4},{4,8},{8,12},{12,14},{14,10},{10,6},{6,2},{2,0},{1,5},{5,9},... | collective-permute-start | bytes 1572872 | tf_op jit(solution)/shard_map/ppermute | solution.py:401
  299.8 31.0 %collective-permute-start.67 = (bf16[64,4096]{1,0:T(8,128)(2,1)}, bf16[64,4096]{1,0:T(8,128)(2,1)}, u32[]{:S(2)}, u32[]{:S(2)}) collective-permute-start(bf16[64,4096]{1,0:T(8,128)(2,1)} %collective-permute-done.65.refs_7_.refs_12_), channel_id=1, source_target_pairs={{0,2},{4,0},{8,4},{12,8},{14,12},{10,14},{6,10},{2,6},{1,3},{5,1},... | collective-permute-start | bytes 1572872 | tf_op jit(solution)/shard_map/ppermute | solution.py:401
  357.8 26.8 %collective-permute-start.68 = (f32[1,768]{1,0:T(1,128)S(1)}, f32[1,768]{1,0:T(1,128)S(1)}, u32[]{:S(2)}, u32[]{:S(2)}) collective-permute-start(f32[1,768]{1,0:T(1,128)S(1)} %broadcast_select_fusion.1), channel_id=1, source_target_pairs={{0,1},{1,0},{2,3},{3,2},{4,5},{5,4},{6,7},{7,6},{8,9},{9,8},{10,11... | collective-permute-start | bytes 9224 | tf_op jit(solution)/shard_map/ppermute | solution.py:401
  360.9 24.8 %collective-permute-start.30 = (bf16[128,1536]{1,0:T(8,128)(2,1)}, bf16[128,1536]{1,0:T(8,128)(2,1)S(1)}, u32[]{:S(2)}, u32[]{:S(2)}) collective-permute-start(bf16[128,1536]{1,0:T(8,128)(2,1)} %get-tuple-element.62), channel_id=1, source_target_pairs={{0,4},{4,8},{8,12},{12,14},{14,10},{10,6},{6,2},{2,0},{1,5},{5,9},... | collective-permute-start | bytes 1179656 | tf_op jit(solution)/shard_map/ppermute | solution.py:401
  386.8 25.9 %collective-permute-start.32 = (bf16[128,1536]{1,0:T(8,128)(2,1)S(1)}, bf16[128,1536]{1,0:T(8,128)(2,1)S(1)}, u32[]{:S(2)}, u32[]{:S(2)}) collective-permute-start(bf16[128,1536]{1,0:T(8,128)(2,1)S(1)} %get-tuple-element.64), channel_id=1, source_target_pairs={{0,4},{4,8},{8,12},{12,14},{14,10},{10,6},{6,2},{2,0},{1,5},{5,9},... | collective-permute-start | bytes 1179656 | tf_op jit(solution)/shard_map/ppermute | solution.py:401
  387.4 25.3 %collective-permute-start.33 = (bf16[128,1536]{1,0:T(8,128)(2,1)S(1)}, bf16[128,1536]{1,0:T(8,128)(2,1)S(1)}, u32[]{:S(2)}, u32[]{:S(2)}) collective-permute-start(bf16[128,1536]{1,0:T(8,128)(2,1)S(1)} %get-tuple-element.65), channel_id=1, source_target_pairs={{0,2},{4,0},{8,4},{12,8},{14,12},{10,14},{6,10},{2,6},{1,3},{5,1},... | collective-permute-start | bytes 1179656 | tf_op jit(solution)/shard_map/ppermute | solution.py:401
  389.9 22.8 %collective-permute-start.42 = (bf16[128,1536]{1,0:T(8,128)(2,1)S(1)}, bf16[128,1536]{1,0:T(8,128)(2,1)S(1)}, u32[]{:S(2)}, u32[]{:S(2)}) collective-permute-start(bf16[128,1536]{1,0:T(8,128)(2,1)S(1)} %get-tuple-element.80), channel_id=1, source_target_pairs={{0,4},{4,8},{8,12},{12,14},{14,10},{10,6},{6,2},{2,0},{1,5},{5,9},... | collective-permute-start | bytes 1179656 | tf_op jit(solution)/shard_map/ppermute | solution.py:401
  (80 other events, 1552.6 us)

commit v3 on v2

--- a/solution.py
+++ b/solution.py
@@ -57,32 +57,47 @@
 
 def cut_columns(core, w_gate, w_up, low, high):
     depth, units = w_gate.shape
-    per_half, tiles = units // 2 // LANES, (high - low) // LANES
+    half, size = units // 2, high - low
     step = math.gcd(depth, 1024)
-
-    def body(core_ref, *refs):
-        out_ref = refs[-1]
-        for n, ref in enumerate(refs[:-1]):
-            out_ref[:, n * LANES : (n + 1) * LANES] = ref[...]
-
-    specs = [
-        pl.BlockSpec((step, LANES), lambda i, core_ref, n=n: (i, core_ref[0] * per_half + low // LANES + n))
-        for n in range(tiles)
-    ]
-    out = jax.ShapeDtypeStruct((depth, 2 * (high - low)), w_gate.dtype)
+    steps = depth // step
+
+    def body(core_ref, gate_ref, up_ref, out_ref, held, sems, out_sems):
+        first = pl.multiple_of(core_ref[0] * half + low, LANES)
+        ins, outs = [], []
+        for i in range(steps):
+            span = pl.ds(i * step, step)
+            for n, ref in enumerate((gate_ref, up_ref)):
+                source = ref.at[span, pl.ds(first, size)]
+                ins.append(pltpu.make_async_copy(source, held.at[span, pl.ds(n * size, size)], sems.at[i, n]))
+            outs.append(pltpu.make_async_copy(held.at[span, :], out_ref.at[span, :], out_sems.at[i]))
+        for copy in ins:
+            copy.start()
+        for i in range(steps):
+            ins[2 * i].wait()
+            ins[2 * i + 1].wait()
+            outs[i].start()
+        for copy in outs:
+            copy.wait()
+
+    out = jax.ShapeDtypeStruct((depth, 2 * size), w_gate.dtype)
     return pl.pallas_call(
         body,
         out_shape=out,
         grid_spec=pltpu.PrefetchScalarGridSpec(
             num_scalar_prefetch=1,
-            grid=(depth // step,),
-            in_specs=specs + specs,
-            out_specs=pl.BlockSpec((step, 2 * (high - low)), lambda i, core_ref: (i, 0)),
+            grid=(1,),
+            in_specs=[pl.BlockSpec(memory_space=pltpu.HBM)] * 2,
+            out_specs=pl.BlockSpec(memory_space=pltpu.HBM),
+            scratch_shapes=[
+                pltpu.VMEM(out.shape, out.dtype),
+                pltpu.SemaphoreType.DMA((steps, 2)),
+                pltpu.SemaphoreType.DMA((steps,)),
+            ],
         ),
+        compiler_params=params(),
         cost_estimate=cost(0, out, out),
-        compiler_params=params(),
         name="cut_columns",
-    )(core, *[w_gate] * tiles, *[w_up] * tiles)
+    )(core, w_gate, w_up)
 
 
 def cut_rows(core, w_down, bounds):
@@ -114,7 +129,8 @@
     for block in blocks:
         starts.append(starts[-1] + block.shape[0])
     rows, width = starts[-1], blocks[0].shape[1]
-    step = math.gcd(512, width)
+    lengths = [length for parts in groups for segments, _, _ in parts for _, length in segments]
+    step = math.gcd(1024, width, *lengths)
     arrays, copies_of, sizes = [], [], []
     for parts in groups:
         size = 0

time: 419 us -> 417 us (level)
  Pallas kernels: 138 us -> 131 us
  waiting for transfers between devices: 191 us -> 196 us
    ppermute x63, waiting for transfers between devices: 191 us -> 196 us  [go(): return lax.ppermute(value, 'exp', perm)]
    pallas_call x3, Pallas kernels: 11.9 us -> 7.66 us  [cut_columns(): pl.pallas_call(body, out_shape=out, grid_spec=pltpu.PrefetchScalarGridSpe...]
  transfers between devices with their start and end apart: 70 -> 70, of which waited for: 19 -> 20; matrix products, arithmetic and copies ran while one was open for 3% -> 3% of each run, Pallas kernels for 33% -> 31%
where the time goes in v3:
time: 417 us; the launch traced here: 413 us
  waiting for transfers between devices  196 us (47%)
  Pallas kernels  131 us (31%)
  starting transfers between devices  68.6 us (16%)
  local copies, waits for them, and re-layouts  10.3 us (2%)
  other arithmetic  5.56 us (1%)
    ppermute x63, waiting for transfers between devices, go(): return lax.ppermute(value, 'exp', perm)  196 us
    pallas_call x7, Pallas kernels, contract(): pl.pallas_call(body, out_shape=outs, grid=(steps,), in_specs=specs, out_s...  81.9 us
    ppermute x63, starting transfers between devices, go(): return lax.ppermute(value, 'exp', perm)  68 us
    pallas_call x3, Pallas kernels, both_out(): pl.pallas_call(body, out_shape=outs, grid=(width // step,), in_specs=[fix...  26.2 us
    pallas_call x9, Pallas kernels, hop_sum(): pl.pallas_call(body, out_shape=[out, out], grid=(1,), in_specs=[pl.BlockS...  9.06 us
  transfers between devices with their start and end apart: 70, of which 20 were waited for; matrix products, arithmetic and copies ran while one was open for 3% of the time, Pallas kernels for 31%

profile of v3, /device:TPU:12, one launch (start us, length us, event | category | flops | bytes accessed | tf_op | source)
XLA Modules:
  0.0 412.6 jit_solution(6391851973341804833)
XLA Ops:
  2.0 3.1 collective-permute-done.23
  12.0 2.7 collective-permute-start.25
  15.7 18.7 %collective-permute-done.25 = bf16[4,16,128]{2,1,0:T(8,128)(2,1)S(1)} collective-permute-done((bf16[4,16,128]{2,1,0:T(8,128)(2,1)S(1)}, bf16[4,16,128]{2,1,0:T(8,128)(2,1)S(1)}, u32[]{:S(2)}, u32[]{:S(2)}) %collective-permute-start.25) | collective-permute-done | bytes 16416 | tf_op jit(solution)/shard_map/ppermute | solution.py:417
  34.5 2.1 collective-permute-start.56
  36.5 4.4 %cut_rows.1 = (bf16[384,1536]{1,0:T(8,128)(2,1)}, bf16[384,1536]{1,0:T(8,128)(2,1)}, bf16[384,1024]{1,0:T(8,128)(2,1)}) custom-call(s32[1]{0:T(128)} %bitcast.2.core_ref, bf16[768,4096]{1,0:T(8,128)(2,1)} %bitcast.38), custom_call_target="tpu_custom_call" | custom-call | bytes 6291456 | tf_op jit(solution)/shard_map/cut_rows/pallas_call | solution.py:112
  42.5 2.5 cut_columns.3
  45.0 2.7 cut_columns.4
  51.0 4.6 %collective-permute-done.55.refs_2_ = bf16[64,4096]{1,0:T(8,128)(2,1)} collective-permute-done((bf16[64,4096]{1,0:T(8,128)(2,1)}, bf16[64,4096]{1,0:T(8,128)(2,1)}, u32[]{:S(2)}, u32[]{:S(2)}) %collective-permute-start.55) | collective-permute-done | bytes 524320 | tf_op jit(solution)/shard_map/ppermute | solution.py:417
  57.7 2.5 cut_columns.5
  60.2 4.9 %collective-permute-done.57.refs_4_ = bf16[64,4096]{1,0:T(8,128)(2,1)S(1)} collective-permute-done((bf16[64,4096]{1,0:T(8,128)(2,1)}, bf16[64,4096]{1,0:T(8,128)(2,1)S(1)}, u32[]{:S(2)}, u32[]{:S(2)}) %collective-permute-start.57) | collective-permute-done | bytes 524320 | tf_op jit(solution)/shard_map/ppermute | solution.py:417
  70.8 8.2 %collective-permute-done.5.refs_6_ = bf16[64,4096]{1,0:T(8,128)(2,1)} collective-permute-done((bf16[64,4096]{1,0:T(8,128)(2,1)}, bf16[64,4096]{1,0:T(8,128)(2,1)}, u32[]{:S(2)}, u32[]{:S(2)}) %collective-permute-start.5) | collective-permute-done | bytes 524320 | tf_op jit(solution)/shard_map/ppermute | solution.py:417
  81.6 7.2 %collective-permute-done.7.refs_8_ = bf16[64,4096]{1,0:T(8,128)(2,1)S(1)} collective-permute-done((bf16[64,4096]{1,0:T(8,128)(2,1)}, bf16[64,4096]{1,0:T(8,128)(2,1)S(1)}, u32[]{:S(2)}, u32[]{:S(2)}) %collective-permute-start.7) | collective-permute-done | bytes 524320 | tf_op jit(solution)/shard_map/ppermute | solution.py:417
  94.1 12.6 %collective-permute-done.14.refs_15_ = bf16[4096,256]{1,0:T(8,128)(2,1)} collective-permute-done((bf16[4096,256]{1,0:T(8,128)(2,1)S(1)}, bf16[4096,256]{1,0:T(8,128)(2,1)}, u32[]{:S(2)}, u32[]{:S(2)}) %collective-permute-start.14) | collective-permute-done | bytes 2097184 | tf_op jit(solution)/shard_map/ppermute | solution.py:417
  106.7 44.9 %collective-permute-done.16.refs_17_ = bf16[4096,256]{1,0:T(8,128)(2,1)} collective-permute-done((bf16[4096,256]{1,0:T(8,128)(2,1)}, bf16[4096,256]{1,0:T(8,128)(2,1)}, u32[]{:S(2)}, u32[]{:S(2)}) %collective-permute-start.16) | collective-permute-done | bytes 2097184 | tf_op jit(solution)/shard_map/ppermute | solution.py:417
  153.3 2.0 collective-permute-start.11
  155.5 35.4 %collective-permute-done.19.refs_15_ = bf16[4096,256]{1,0:T(8,128)(2,1)} collective-permute-done((bf16[4096,256]{1,0:T(8,128)(2,1)}, bf16[4096,256]{1,0:T(8,128)(2,1)}, u32[]{:S(2)}, u32[]{:S(2)}) %collective-permute-start.19) | collective-permute-done | bytes 2097184 | tf_op jit(solution)/shard_map/ppermute | solution.py:417
  198.6 14.5 %shard_map.122.refs_0_.refs_8_ = bf16[640,768]{1,0:T(8,128)(2,1)} custom-call(bf16[128,4096]{1,0:T(8,128)(2,1)} %refs_0_.7, bf16[64,4096]{1,0:T(8,128)(2,1)} %collective-permute-done.refs_1_, bf16[64,4096]{1,0:T(8,128)(2,1)} %copy-done.33, bf16[64,4096]{1,0:T(8,128)(2,1)} %copy-done.32, bf16[64,4096]{1,0:T(8,128)(2,1)} %collective-permute-done.3.refs_4_, ...), custom_call_target="tpu_custom_call" | custom-call | flops 8053063680 | bytes 983040 | tf_op jit(solution)/shard_map/pallas_call | solution.py:229
  213.7 10.3 %shard_map.123.refs_1_ = bf16[384,768]{1,0:T(8,128)(2,1)} custom-call(bf16[64,4096]{1,0:T(8,128)(2,1)} %copy-done.35, bf16[64,4096]{1,0:T(8,128)(2,1)} %collective-permute-done.9.refs_1_.refs_10_, bf16[64,4096]{1,0:T(8,128)(2,1)} %collective-permute-done.10.refs_2_.refs_11_, bf16[64,4096]{1,0:T(8,128)(2,1)} %copy-done.36, ...), custom_call_target="tpu_custom_call" | custom-call | flops 4831838208 | bytes 589824 | tf_op jit(solution)/shard_map/pallas_call | solution.py:229
  226.7 14.9 %shard_map.124.refs_2_.refs_23_ = bf16[1024,512]{1,0:T(8,128)(2,1)} custom-call(bf16[128,4096]{1,0:T(8,128)(2,1)} %refs_0_.7, bf16[64,4096]{1,0:T(8,128)(2,1)} %collective-permute-done.refs_1_, bf16[64,4096]{1,0:T(8,128)(2,1)} %copy-done.33, bf16[64,4096]{1,0:T(8,128)(2,1)} %copy-done.32, bf16[64,4096]{1,0:T(8,128)(2,1)} %collective-permute-done.3.refs_4_, ...), custom_call_target="tpu_custom_call" | custom-call | flops 8589934592 | bytes 1048576 | tf_op jit(solution)/shard_map/pallas_call | solution.py:229
  241.6 8.0 %collective-permute-done.34.refs_5_.refs_16_ = bf16[384,1536]{1,0:T(8,128)(2,1)} collective-permute-done((bf16[384,1536]{1,0:T(8,128)(2,1)S(1)}, bf16[384,1536]{1,0:T(8,128)(2,1)}, u32[]{:S(2)}, u32[]{:S(2)}) %collective-permute-start.34) | collective-permute-done | bytes 1179680 | tf_op jit(solution)/shard_map/ppermute | solution.py:417
  250.1 9.8 %shard_map.125.refs_3_.refs_24_ = bf16[1024,256]{1,0:T(8,128)(2,1)} custom-call(bf16[128,4096]{1,0:T(8,128)(2,1)} %refs_0_.7, bf16[64,4096]{1,0:T(8,128)(2,1)} %collective-permute-done.refs_1_, bf16[64,4096]{1,0:T(8,128)(2,1)} %copy-done.33, bf16[64,4096]{1,0:T(8,128)(2,1)} %copy-done.32, bf16[64,4096]{1,0:T(8,128)(2,1)} %collective-permute-done.3.refs_4_, ...), custom_call_target="tpu_custom_call" | custom-call | flops 4294967296 | bytes 524288 | tf_op jit(solution)/shard_map/pallas_call | solution.py:229
  262.4 9.3 %shard_map.126 = (bf16[128,1536]{1,0:T(8,128)(2,1)}, bf16[128,1536]{1,0:T(8,128)(2,1)}, bf16[128,1536]{1,0:T(8,128)(2,1)}, bf16[128,1536]{1,0:T(8,128)(2,1)}, bf...) custom-call(bf16[640,768]{1,0:T(8,128)(2,1)} %shard_map.122.refs_0_., ...), custom_call_target="tpu_custom_call" | custom-call | flops 4831838208 | bytes 3145728 | tf_op jit(solution)/shard_map/pallas_call | solution.py:314
  273.5 7.5 %shard_map.134 = (bf16[128,1024]{1,0:T(8,128)(2,1)}, bf16[128,1024]{1,0:T(8,128)(2,1)}, bf16[128,1024]{1,0:T(8,128)(2,1)}, bf16[128,1024]{1,0:T(8,128)(2,1)}, bf...) custom-call(bf16[640,768]{1,0:T(8,128)(2,1)} %shard_map.122.refs_0_., ...), custom_call_target="tpu_custom_call" | custom-call | flops 3221225472 | bytes 2097152 | tf_op jit(solution)/shard_map/pallas_call | solution.py:314
  282.5 3.9 collective-permute-done.62.refs_4_.refs_9_
  287.8 7.8 %shard_map.139 = f32[1,768]{1,0:T(1,128)} custom-call(bf16[128,4096]{1,0:T(8,128)(2,1)} %refs_0_.9, bf16[64,4096]{1,0:T(8,128)(2,1)} %collective-permute-done.54.refs_1_, bf16[64,4096]{1,0:T(8,128)(2,1)} %collective-permute-done.55.refs_2_, bf16[64,4096]{1,0:T(8,128)(2,1)} %collective-permute-done.56.refs_3_, bf16[64,4096]{1,0:T(8,128)(2,1)} %copy-done.27, ...), custom_call_target="tpu_custom_call" | custom-call | flops 2415919104 | bytes 3072 | tf_op jit(solution)/shard_map/pallas_call | solution.py:229
  301.6 9.4 %shard_map.130 = (bf16[128,1536]{1,0:T(8,128)(2,1)}, bf16[128,1536]{1,0:T(8,128)(2,1)}, bf16[128,1536]{1,0:T(8,128)(2,1)}, bf16[128,1536]{1,0:T(8,128)(2,1)}, bf...) custom-call(bf16[640,768]{1,0:T(8,128)(2,1)} %shard_map.122.refs_0_., ...), custom_call_target="tpu_custom_call" | custom-call | flops 4831838208 | bytes 3145728 | tf_op jit(solution)/shard_map/pallas_call | solution.py:314
  311.5 12.0 %collective-permute-done.27.behind_ref = bf16[64,1536]{1,0:T(8,128)(2,1)S(1)} collective-permute-done((bf16[64,1536]{1,0:T(8,128)(2,1)S(1)}, bf16[64,1536]{1,0:T(8,128)(2,1)S(1)}, u32[]{:S(2)}, u32[]{:S(2)}) %collective-permute-start.27) | collective-permute-done | bytes 196640 | tf_op jit(solution)/shard_map/ppermute | solution.py:417
  329.8 14.2 %shard_map.141 = f32[1,768]{1,0:T(1,128)} custom-call(bf16[128,4096]{1,0:T(8,128)(2,1)} %refs_0_.9, bf16[64,4096]{1,0:T(8,128)(2,1)} %collective-permute-done.54.refs_1_, bf16[64,4096]{1,0:T(8,128)(2,1)} %collective-permute-done.55.refs_2_, bf16[64,4096]{1,0:T(8,128)(2,1)} %collective-permute-done.56.refs_3_, bf16[64,4096]{1,0:T(8,128)(2,1)} %copy-done.27, ...), custom_call_target="tpu_custom_call" | custom-call | flops 6442450944 | bytes 3072 | tf_op jit(solution)/shard_map/pallas_call | solution.py:229
  352.6 3.5 collective-permute-done.29.behind_ref
  359.8 4.7 %collective-permute-done.39.behind_ref = bf16[128,1536]{1,0:T(8,128)(2,1)S(1)} collective-permute-done((bf16[128,1536]{1,0:T(8,128)(2,1)S(1)}, bf16[128,1536]{1,0:T(8,128)(2,1)S(1)}, u32[]{:S(2)}, u32[]{:S(2)}) %collective-permute-start.39) | collective-permute-done | bytes 393248 | tf_op jit(solution)/shard_map/ppermute | solution.py:417
  371.8 10.4 %shard_map.140 = f32[1,768]{1,0:T(1,128)} custom-call(bf16[64,4096]{1,0:T(8,128)(2,1)} %collective-permute-done.58.refs_0_.refs_5_, bf16[64,4096]{1,0:T(8,128)(2,1)} %collective-permute-done.59.refs_1_.refs_6_, bf16[64,4096]{1,0:T(8,128)(2,1)} %collective-permute-done.60.refs_2_.refs_7_, bf16[64,4096]{1,0:T(8,128)(2,1)} %collective-permute-done.61.refs_3_.refs_8_, ...), custom_call_target="tpu_custom_call" | custom-call | flops 4026531840 | bytes 3072 | tf_op jit(solution)/shard_map/pallas_call | solution.py:229
  392.2 18.4 %collective-permute-done.53.refs_8_ = bf16[128,1024]{1,0:T(8,128)(2,1)S(1)} collective-permute-done((bf16[128,1024]{1,0:T(8,128)(2,1)S(1)}, bf16[128,1024]{1,0:T(8,128)(2,1)S(1)}, u32[]{:S(2)}, u32[]{:S(2)}) %collective-permute-start.53) | collective-permute-done | bytes 262176 | tf_op jit(solution)/shard_map/ppermute | solution.py:417
  (251 shorter events, 94.0 us)
Async XLA Ops:
  6.9 27.6 %collective-permute-start = (bf16[64,4096]{1,0:T(8,128)(2,1)S(1)}, bf16[64,4096]{1,0:T(8,128)(2,1)}, u32[]{:S(2)}, u32[]{:S(2)}) collective-permute-start(bf16[64,4096]{1,0:T(8,128)(2,1)S(1)} %get-tuple-element.103), channel_id=1, source_target_pairs={{0,4},{4,8},{8,12},{12,14},{14,10},{10,6},{6,2},{2,0},{1,5},{5,9},... | collective-permute-start | bytes 1572872 | tf_op jit(solution)/shard_map/ppermute | solution.py:417
  8.5 32.4 %collective-permute-start.2 = (bf16[64,4096]{1,0:T(8,128)(2,1)S(1)}, bf16[64,4096]{1,0:T(8,128)(2,1)S(1)}, u32[]{:S(2)}, u32[]{:S(2)}) collective-permute-start(bf16[64,4096]{1,0:T(8,128)(2,1)S(1)} %get-tuple-element.103), channel_id=1, source_target_pairs={{0,2},{4,0},{8,4},{12,8},{14,12},{10,14},{6,10},{2,6},{1,3},{5,1},... | collective-permute-start | bytes 1572872 | tf_op jit(solution)/shard_map/ppermute | solution.py:417
  9.7 24.8 %collective-permute-start.1 = (bf16[64,4096]{1,0:T(8,128)(2,1)S(1)}, bf16[64,4096]{1,0:T(8,128)(2,1)S(1)}, u32[]{:S(2)}, u32[]{:S(2)}) collective-permute-start(bf16[64,4096]{1,0:T(8,128)(2,1)S(1)} %get-tuple-element.102), channel_id=1, source_target_pairs={{0,4},{4,8},{8,12},{12,14},{14,10},{10,6},{6,2},{2,0},{1,5},{5,9},... | collective-permute-start | bytes 1572872 | tf_op jit(solution)/shard_map/ppermute | solution.py:417
  15.7 32.0 %collective-permute-start.3 = (bf16[64,4096]{1,0:T(8,128)(2,1)S(1)}, bf16[64,4096]{1,0:T(8,128)(2,1)}, u32[]{:S(2)}, u32[]{:S(2)}) collective-permute-start(bf16[64,4096]{1,0:T(8,128)(2,1)S(1)} %get-tuple-element.102), channel_id=1, source_target_pairs={{0,2},{4,0},{8,4},{12,8},{14,12},{10,14},{6,10},{2,6},{1,3},{5,1},... | collective-permute-start | bytes 1572872 | tf_op jit(solution)/shard_map/ppermute | solution.py:417
  40.9 26.2 %collective-permute-start.44 = (bf16[384,1024]{1,0:T(8,128)(2,1)}, bf16[384,1024]{1,0:T(8,128)(2,1)S(1)}, u32[]{:S(2)}, u32[]{:S(2)}) collective-permute-start(bf16[384,1024]{1,0:T(8,128)(2,1)} %get-tuple-element.82), channel_id=1, source_target_pairs={{0,1},{1,0},{2,3},{3,2},{4,5},{5,4},{6,7},{7,6},{8,9},{9,8},{10,11... | collective-permute-start | bytes 2359304 | tf_op jit(solution)/shard_map/ppermute | solution.py:417
  47.7 58.9 %collective-permute-start.14 = (bf16[4096,256]{1,0:T(8,128)(2,1)S(1)}, bf16[4096,256]{1,0:T(8,128)(2,1)}, u32[]{:S(2)}, u32[]{:S(2)}) collective-permute-start(bf16[4096,256]{1,0:T(8,128)(2,1)S(1)} %copy-done.24), channel_id=1, source_target_pairs={{0,1},{1,0},{2,3},{3,2},{4,5},{5,4},{6,7},{7,6},{8,9},{9,8},{10,11... | collective-permute-start | bytes 6291464 | tf_op jit(solution)/shard_map/ppermute | solution.py:417
  49.5 102.1 %collective-permute-start.16 = (bf16[4096,256]{1,0:T(8,128)(2,1)}, bf16[4096,256]{1,0:T(8,128)(2,1)}, u32[]{:S(2)}, u32[]{:S(2)}) collective-permute-start(bf16[4096,256]{1,0:T(8,128)(2,1)} %cut_columns.4), channel_id=1, source_target_pairs={{0,1},{1,0},{2,3},{3,2},{4,5},{5,4},{6,7},{7,6},{8,9},{9,8},{10,11... | collective-permute-start | bytes 6291464 | tf_op jit(solution)/shard_map/ppermute | solution.py:417
  65.1 125.9 %collective-permute-start.19 = (bf16[4096,256]{1,0:T(8,128)(2,1)}, bf16[4096,256]{1,0:T(8,128)(2,1)}, u32[]{:S(2)}, u32[]{:S(2)}) collective-permute-start(bf16[4096,256]{1,0:T(8,128)(2,1)} %cut_columns.5), channel_id=1, source_target_pairs={{0,1},{1,0},{2,3},{3,2},{4,5},{5,4},{6,7},{7,6},{8,9},{9,8},{10,11... | collective-permute-start | bytes 6291464 | tf_op jit(solution)/shard_map/ppermute | solution.py:417
  88.7 64.6 %collective-permute-start.9 = (bf16[64,4096]{1,0:T(8,128)(2,1)}, bf16[64,4096]{1,0:T(8,128)(2,1)}, u32[]{:S(2)}, u32[]{:S(2)}) collective-permute-start(bf16[64,4096]{1,0:T(8,128)(2,1)} %collective-permute-done.5.refs_6_), channel_id=1, source_target_pairs={{0,4},{4,8},{8,12},{12,14},{14,10},{10,6},{6,2},{2,0},{1,5},{5,9},... | collective-permute-start | bytes 1572872 | tf_op jit(solution)/shard_map/ppermute | solution.py:417
  92.5 62.8 %collective-permute-start.10 = (bf16[64,4096]{1,0:T(8,128)(2,1)}, bf16[64,4096]{1,0:T(8,128)(2,1)}, u32[]{:S(2)}, u32[]{:S(2)}) collective-permute-start(bf16[64,4096]{1,0:T(8,128)(2,1)} %collective-permute-done.6.refs_7_), channel_id=1, source_target_pairs={{0,2},{4,0},{8,4},{12,8},{14,12},{10,14},{6,10},{2,6},{1,3},{5,1},... | collective-permute-start | bytes 1572872 | tf_op jit(solution)/shard_map/ppermute | solution.py:417
  106.7 118.4 %collective-permute-start.15 = (bf16[4096,256]{1,0:T(8,128)(2,1)}, bf16[4096,256]{1,0:T(8,128)(2,1)}, u32[]{:S(2)}, u32[]{:S(2)}) collective-permute-start(bf16[4096,256]{1,0:T(8,128)(2,1)} %collective-permute-done.14.refs_15_), channel_id=1, source_target_pairs={{0,16},{16,0},{1,17},{17,1},{2,18},{18,2},{3,19},{19,3},{4,20},{20... | collective-permute-start | bytes 6291464 | tf_op jit(solution)/shard_map/ppermute | solution.py:420
  151.6 75.1 %collective-permute-start.17 = (bf16[4096,256]{1,0:T(8,128)(2,1)}, bf16[4096,256]{1,0:T(8,128)(2,1)}, u32[]{:S(2)}, u32[]{:S(2)}) collective-permute-start(bf16[4096,256]{1,0:T(8,128)(2,1)} %collective-permute-done.16.refs_17_), channel_id=1, source_target_pairs={{0,16},{16,0},{1,17},{17,1},{2,18},{18,2},{3,19},{19,3},{4,20},{20... | collective-permute-start | bytes 6291464 | tf_op jit(solution)/shard_map/ppermute | solution.py:420
  153.3 41.5 %collective-permute-start.11 = (bf16[64,4096]{1,0:T(8,128)(2,1)}, bf16[64,4096]{1,0:T(8,128)(2,1)S(1)}, u32[]{:S(2)}, u32[]{:S(2)}) collective-permute-start(bf16[64,4096]{1,0:T(8,128)(2,1)} %copy-done.34), channel_id=1, source_target_pairs={{0,2},{4,0},{8,4},{12,8},{14,12},{10,14},{6,10},{2,6},{1,3},{5,1},... | collective-permute-start | bytes 1572872 | tf_op jit(solution)/shard_map/ppermute | solution.py:417
  155.3 41.8 %collective-permute-start.12 = (bf16[64,4096]{1,0:T(8,128)(2,1)}, bf16[64,4096]{1,0:T(8,128)(2,1)}, u32[]{:S(2)}, u32[]{:S(2)}) collective-permute-start(bf16[64,4096]{1,0:T(8,128)(2,1)} %copy-done.35), channel_id=1, source_target_pairs={{0,4},{4,8},{8,12},{12,14},{14,10},{10,6},{6,2},{2,0},{1,5},{5,9},... | collective-permute-start | bytes 1572872 | tf_op jit(solution)/shard_map/ppermute | solution.py:417
  190.9 58.7 %collective-permute-start.20 = (bf16[4096,256]{1,0:T(8,128)(2,1)}, bf16[4096,256]{1,0:T(8,128)(2,1)}, u32[]{:S(2)}, u32[]{:S(2)}) collective-permute-start(bf16[4096,256]{1,0:T(8,128)(2,1)} %collective-permute-done.19.refs_15_), channel_id=1, source_target_pairs={{0,16},{16,0},{1,17},{17,1},{2,18},{18,2},{3,19},{19,3},{4,20},{20... | collective-permute-start | bytes 6291464 | tf_op jit(solution)/shard_map/ppermute | solution.py:420
  195.6 29.1 %collective-permute-start.21 = (bf16[384,1536]{1,0:T(8,128)(2,1)}, bf16[384,1536]{1,0:T(8,128)(2,1)S(1)}, u32[]{:S(2)}, u32[]{:S(2)}) collective-permute-start(bf16[384,1536]{1,0:T(8,128)(2,1)} %get-tuple-element.50), channel_id=1, source_target_pairs={{0,1},{1,0},{2,3},{3,2},{4,5},{5,4},{6,7},{7,6},{8,9},{9,8},{10,11... | collective-permute-start | bytes 3538952 | tf_op jit(solution)/shard_map/ppermute | solution.py:417
  213.1 36.5 %collective-permute-start.34 = (bf16[384,1536]{1,0:T(8,128)(2,1)S(1)}, bf16[384,1536]{1,0:T(8,128)(2,1)}, u32[]{:S(2)}, u32[]{:S(2)}) collective-permute-start(bf16[384,1536]{1,0:T(8,128)(2,1)S(1)} %copy-done.30), channel_id=1, source_target_pairs={{0,1},{1,0},{2,3},{3,2},{4,5},{5,4},{6,7},{7,6},{8,9},{9,8},{10,11... | collective-permute-start | bytes 3538952 | tf_op jit(solution)/shard_map/ppermute | solution.py:417
  224.7 35.3 %collective-permute-start.58 = (bf16[64,4096]{1,0:T(8,128)(2,1)}, bf16[64,4096]{1,0:T(8,128)(2,1)}, u32[]{:S(2)}, u32[]{:S(2)}) collective-permute-start(bf16[64,4096]{1,0:T(8,128)(2,1)} %collective-permute-done.54.refs_1_), channel_id=1, source_target_pairs={{0,4},{4,8},{8,12},{12,14},{14,10},{10,6},{6,2},{2,0},{1,5},{5,9},... | collective-permute-start | bytes 1572872 | tf_op jit(solution)/shard_map/ppermute | solution.py:417
  225.1 35.3 %collective-permute-start.61 = (bf16[64,4096]{1,0:T(8,128)(2,1)S(1)}, bf16[64,4096]{1,0:T(8,128)(2,1)}, u32[]{:S(2)}, u32[]{:S(2)}) collective-permute-start(bf16[64,4096]{1,0:T(8,128)(2,1)S(1)} %collective-permute-done.57.refs_4_), channel_id=1, source_target_pairs={{0,2},{4,0},{8,4},{12,8},{14,12},{10,14},{6,10},{2,6},{1,3},{5,1},... | collective-permute-start | bytes 1572872 | tf_op jit(solution)/shard_map/ppermute | solution.py:417
  226.7 35.3 %collective-permute-start.22 = (bf16[384,1536]{1,0:T(8,128)(2,1)S(1)}, bf16[384,1536]{1,0:T(8,128)(2,1)}, u32[]{:S(2)}, u32[]{:S(2)}) collective-permute-start(bf16[384,1536]{1,0:T(8,128)(2,1)S(1)} %collective-permute-done.21.refs_5_.refs_15_), channel_id=1, source_target_pairs={{0,16},{16,0},{1,17},{17,1},{2,18},{18,2},{3,19},{19,3},{4,20},{20... | collective-permute-start | bytes 3538952 | tf_op jit(solution)/shard_map/ppermute | solution.py:420
  249.6 46.7 %collective-permute-start.35 = (bf16[384,1536]{1,0:T(8,128)(2,1)}, bf16[384,1536]{1,0:T(8,128)(2,1)}, u32[]{:S(2)}, u32[]{:S(2)}) collective-permute-start(bf16[384,1536]{1,0:T(8,128)(2,1)} %collective-permute-done.34.refs_5_.refs_16_), channel_id=1, source_target_pairs={{0,16},{16,0},{1,17},{17,1},{2,18},{18,2},{3,19},{19,3},{4,20},{20... | collective-permute-start | bytes 3538952 | tf_op jit(solution)/shard_map/ppermute | solution.py:420
  262.1 24.3 %collective-permute-start.62 = (bf16[64,4096]{1,0:T(8,128)(2,1)}, bf16[64,4096]{1,0:T(8,128)(2,1)}, u32[]{:S(2)}, u32[]{:S(2)}) collective-permute-start(bf16[64,4096]{1,0:T(8,128)(2,1)} %collective-permute-done.58.refs_0_.refs_5_), channel_id=1, source_target_pairs={{0,4},{4,8},{8,12},{12,14},{14,10},{10,6},{6,2},{2,0},{1,5},{5,9},... | collective-permute-start | bytes 1572872 | tf_op jit(solution)/shard_map/ppermute | solution.py:417
  271.8 23.9 %collective-permute-start.65 = (bf16[64,4096]{1,0:T(8,128)(2,1)}, bf16[64,4096]{1,0:T(8,128)(2,1)}, u32[]{:S(2)}, u32[]{:S(2)}) collective-permute-start(bf16[64,4096]{1,0:T(8,128)(2,1)} %collective-permute-done.61.refs_3_.refs_8_), channel_id=1, source_target_pairs={{0,2},{4,0},{8,4},{12,8},{14,12},{10,14},{6,10},{2,6},{1,3},{5,1},... | collective-permute-start | bytes 1572872 | tf_op jit(solution)/shard_map/ppermute | solution.py:417
  295.7 30.0 %collective-permute-start.63 = (bf16[64,4096]{1,0:T(8,128)(2,1)}, bf16[64,4096]{1,0:T(8,128)(2,1)}, u32[]{:S(2)}, u32[]{:S(2)}) collective-permute-start(bf16[64,4096]{1,0:T(8,128)(2,1)} %collective-permute-done.59.refs_1_.refs_6_), channel_id=1, source_target_pairs={{0,4},{4,8},{8,12},{12,14},{14,10},{10,6},{6,2},{2,0},{1,5},{5,9},... | collective-permute-start | bytes 1572872 | tf_op jit(solution)/shard_map/ppermute | solution.py:417
  296.3 31.1 %collective-permute-start.64 = (bf16[64,4096]{1,0:T(8,128)(2,1)}, bf16[64,4096]{1,0:T(8,128)(2,1)}, u32[]{:S(2)}, u32[]{:S(2)}) collective-permute-start(bf16[64,4096]{1,0:T(8,128)(2,1)} %collective-permute-done.60.refs_2_.refs_7_), channel_id=1, source_target_pairs={{0,2},{4,0},{8,4},{12,8},{14,12},{10,14},{6,10},{2,6},{1,3},{5,1},... | collective-permute-start | bytes 1572872 | tf_op jit(solution)/shard_map/ppermute | solution.py:417
  297.8 30.0 %collective-permute-start.66 = (bf16[64,4096]{1,0:T(8,128)(2,1)}, bf16[64,4096]{1,0:T(8,128)(2,1)}, u32[]{:S(2)}, u32[]{:S(2)}) collective-permute-start(bf16[64,4096]{1,0:T(8,128)(2,1)} %collective-permute-done.62.refs_4_.refs_9_), channel_id=1, source_target_pairs={{0,4},{4,8},{8,12},{12,14},{14,10},{10,6},{6,2},{2,0},{1,5},{5,9},... | collective-permute-start | bytes 1572872 | tf_op jit(solution)/shard_map/ppermute | solution.py:417
  298.3 31.1 %collective-permute-start.67 = (bf16[64,4096]{1,0:T(8,128)(2,1)}, bf16[64,4096]{1,0:T(8,128)(2,1)}, u32[]{:S(2)}, u32[]{:S(2)}) collective-permute-start(bf16[64,4096]{1,0:T(8,128)(2,1)} %collective-permute-done.65.refs_7_.refs_12_), channel_id=1, source_target_pairs={{0,2},{4,0},{8,4},{12,8},{14,12},{10,14},{6,10},{2,6},{1,3},{5,1},... | collective-permute-start | bytes 1572872 | tf_op jit(solution)/shard_map/ppermute | solution.py:417
  356.1 26.5 %collective-permute-start.68 = (f32[1,768]{1,0:T(1,128)S(1)}, f32[1,768]{1,0:T(1,128)S(1)}, u32[]{:S(2)}, u32[]{:S(2)}) collective-permute-start(f32[1,768]{1,0:T(1,128)S(1)} %broadcast_select_fusion.1), channel_id=1, source_target_pairs={{0,1},{1,0},{2,3},{3,2},{4,5},{5,4},{6,7},{7,6},{8,9},{9,8},{10,11... | collective-permute-start | bytes 9224 | tf_op jit(solution)/shard_map/ppermute | solution.py:417
  359.2 24.5 %collective-permute-start.30 = (bf16[128,1536]{1,0:T(8,128)(2,1)}, bf16[128,1536]{1,0:T(8,128)(2,1)S(1)}, u32[]{:S(2)}, u32[]{:S(2)}) collective-permute-start(bf16[128,1536]{1,0:T(8,128)(2,1)} %get-tuple-element.62), channel_id=1, source_target_pairs={{0,4},{4,8},{8,12},{12,14},{14,10},{10,6},{6,2},{2,0},{1,5},{5,9},... | collective-permute-start | bytes 1179656 | tf_op jit(solution)/shard_map/ppermute | solution.py:417
  384.8 25.9 %collective-permute-start.32 = (bf16[128,1536]{1,0:T(8,128)(2,1)S(1)}, bf16[128,1536]{1,0:T(8,128)(2,1)S(1)}, u32[]{:S(2)}, u32[]{:S(2)}) collective-permute-start(bf16[128,1536]{1,0:T(8,128)(2,1)S(1)} %get-tuple-element.64), channel_id=1, source_target_pairs={{0,4},{4,8},{8,12},{12,14},{14,10},{10,6},{6,2},{2,0},{1,5},{5,9},... | collective-permute-start | bytes 1179656 | tf_op jit(solution)/shard_map/ppermute | solution.py:417
  385.4 25.3 %collective-permute-start.33 = (bf16[128,1536]{1,0:T(8,128)(2,1)S(1)}, bf16[128,1536]{1,0:T(8,128)(2,1)S(1)}, u32[]{:S(2)}, u32[]{:S(2)}) collective-permute-start(bf16[128,1536]{1,0:T(8,128)(2,1)S(1)} %get-tuple-element.65), channel_id=1, source_target_pairs={{0,2},{4,0},{8,4},{12,8},{14,12},{10,14},{6,10},{2,6},{1,3},{5,1},... | collective-permute-start | bytes 1179656 | tf_op jit(solution)/shard_map/ppermute | solution.py:417
  387.8 22.8 %collective-permute-start.42 = (bf16[128,1536]{1,0:T(8,128)(2,1)S(1)}, bf16[128,1536]{1,0:T(8,128)(2,1)S(1)}, u32[]{:S(2)}, u32[]{:S(2)}) collective-permute-start(bf16[128,1536]{1,0:T(8,128)(2,1)S(1)} %get-tuple-element.80), channel_id=1, source_target_pairs={{0,4},{4,8},{8,12},{12,14},{14,10},{10,6},{6,2},{2,0},{1,5},{5,9},... | collective-permute-start | bytes 1179656 | tf_op jit(solution)/shard_map/ppermute | solution.py:417
  (80 other events, 1546.7 us)

commit v4 on v3

--- a/solution.py
+++ b/solution.py
@@ -14,7 +14,7 @@
 SLOTS = 3
 LANES = 128
 EARLY = 2
-EARLY_BACK = 1
+EARLY_BACK = 2
 F32 = jnp.float32
 BF16 = jnp.bfloat16
 VMEM_LIMIT = 60 * 1024 * 1024
@@ -102,11 +102,23 @@
 
 def cut_rows(core, w_down, bounds):
     half, width = w_down.shape[0] // 2, w_down.shape[1]
-    step = half // 3 if half % 48 == 0 else half
-
-    def body(core_ref, in_ref, *out_refs):
-        for (low, high), out_ref in zip(bounds, out_refs):
-            out_ref[...] = in_ref[:, low:high]
+    count = len(bounds)
+
+    def body(core_ref, in_ref, *refs):
+        out_refs, (held, sems, out_sems) = refs[:count], refs[count:]
+        rows = pl.ds(pl.multiple_of(core_ref[0] * half, half), half)
+        ins, outs = [], []
+        for n, (low, high) in enumerate(bounds):
+            span = pl.ds(low, high - low)
+            ins.append(pltpu.make_async_copy(in_ref.at[rows, span], held.at[:, span], sems.at[n]))
+            outs.append(pltpu.make_async_copy(held.at[:, span], out_refs[n], out_sems.at[n]))
+        for copy in ins:
+            copy.start()
+        for copy, out in zip(ins, outs):
+            copy.wait()
+            out.start()
+        for out in outs:
+            out.wait()
 
     outs = [jax.ShapeDtypeStruct((half, high - low), w_down.dtype) for low, high in bounds]
     return pl.pallas_call(
@@ -114,12 +126,17 @@
         out_shape=outs,
         grid_spec=pltpu.PrefetchScalarGridSpec(
             num_scalar_prefetch=1,
-            grid=(half // step,),
-            in_specs=[pl.BlockSpec((step, width), lambda i, core_ref: (core_ref[0] * (half // step) + i, 0))],
-            out_specs=[pl.BlockSpec((step, high - low), lambda i, core_ref: (i, 0)) for low, high in bounds],
+            grid=(1,),
+            in_specs=[pl.BlockSpec(memory_space=pltpu.HBM)],
+            out_specs=[pl.BlockSpec(memory_space=pltpu.HBM)] * count,
+            scratch_shapes=[
+                pltpu.VMEM((half, width), w_down.dtype),
+                pltpu.SemaphoreType.DMA((count,)),
+                pltpu.SemaphoreType.DMA((count,)),
+            ],
         ),
+        compiler_params=params(),
         cost_estimate=cost(0, *outs, *outs),
-        compiler_params=params(),
         name="cut_rows",
     )(core, w_down)
 

time: 417 us -> 425 us (1.019)
  waiting for transfers between devices: 196 us -> 214 us
  starting transfers between devices: 68.6 us -> 62.6 us
    ppermute x63, waiting for transfers between devices: 196 us -> 214 us  [go(): return lax.ppermute(value, 'exp', perm)]
    ppermute x63, starting transfers between devices: 68 us -> 62 us  [go(): return lax.ppermute(value, 'exp', perm)]
  transfers between devices with their start and end apart: 70 -> 70, of which waited for: 20 -> 22; matrix products, arithmetic and copies ran while one was open for 3% -> 3% of each run, Pallas kernels for 31% -> 30%
where the time goes in v4:
time: 425 us; the launch traced here: 422 us
  waiting for transfers between devices  214 us (50%)
  Pallas kernels  129 us (30%)
  starting transfers between devices  62.6 us (15%)
  local copies, waits for them, and re-layouts  10.1 us (2%)
  other arithmetic  4.53 us (1%)
    ppermute x63, waiting for transfers between devices, go(): return lax.ppermute(value, 'exp', perm)  214 us
    pallas_call x7, Pallas kernels, contract(): pl.pallas_call(body, out_shape=outs, grid=(steps,), in_specs=specs, out_s...  81.5 us
    ppermute x63, starting transfers between devices, go(): return lax.ppermute(value, 'exp', perm)  62 us
    pallas_call x3, Pallas kernels, both_out(): pl.pallas_call(body, out_shape=outs, grid=(width // step,), in_specs=[fix...  26.5 us
    pallas_call x9, Pallas kernels, hop_sum(): pl.pallas_call(body, out_shape=[out, out], grid=(1,), in_specs=[pl.BlockS...  9.06 us
  transfers between devices with their start and end apart: 70, of which 22 were waited for; matrix products, arithmetic and copies ran while one was open for 3% of the time, Pallas kernels for 30%

profile of v4, /device:TPU:12, one launch (start us, length us, event | category | flops | bytes accessed | tf_op | source)
XLA Modules:
  0.0 422.5 jit_solution(11039840092784339867)
XLA Ops:
  2.0 3.1 collective-permute-done.23
  18.2 14.7 %collective-permute-done.25 = bf16[4,16,128]{2,1,0:T(8,128)(2,1)S(1)} collective-permute-done((bf16[4,16,128]{2,1,0:T(8,128)(2,1)S(1)}, bf16[4,16,128]{2,1,0:T(8,128)(2,1)S(1)}, u32[]{:S(2)}, u32[]{:S(2)}) %collective-permute-start.25) | collective-permute-done | bytes 16416 | tf_op jit(solution)/shard_map/ppermute | solution.py:434
  33.3 3.0 cut_rows.1
  41.5 6.5 %collective-permute-done.54.refs_1_ = bf16[64,4096]{1,0:T(8,128)(2,1)} collective-permute-done((bf16[64,4096]{1,0:T(8,128)(2,1)}, bf16[64,4096]{1,0:T(8,128)(2,1)}, u32[]{:S(2)}, u32[]{:S(2)}) %collective-permute-start.54) | collective-permute-done | bytes 524320 | tf_op jit(solution)/shard_map/ppermute | solution.py:434
  48.4 2.5 cut_columns.3
  50.9 2.7 cut_columns.4
  53.7 5.4 %collective-permute-done.55.refs_2_ = bf16[64,4096]{1,0:T(8,128)(2,1)S(1)} collective-permute-done((bf16[64,4096]{1,0:T(8,128)(2,1)}, bf16[64,4096]{1,0:T(8,128)(2,1)S(1)}, u32[]{:S(2)}, u32[]{:S(2)}) %collective-permute-start.55) | collective-permute-done | bytes 524320 | tf_op jit(solution)/shard_map/ppermute | solution.py:434
  65.2 5.3 %collective-permute-done.4.refs_5_ = bf16[64,4096]{1,0:T(8,128)(2,1)} collective-permute-done((bf16[64,4096]{1,0:T(8,128)(2,1)}, bf16[64,4096]{1,0:T(8,128)(2,1)}, u32[]{:S(2)}, u32[]{:S(2)}) %collective-permute-start.4) | collective-permute-done | bytes 524320 | tf_op jit(solution)/shard_map/ppermute | solution.py:434
  71.2 2.5 cut_columns.5
  73.7 4.3 %collective-permute-done.5.refs_6_ = bf16[64,4096]{1,0:T(8,128)(2,1)} collective-permute-done((bf16[64,4096]{1,0:T(8,128)(2,1)}, bf16[64,4096]{1,0:T(8,128)(2,1)}, u32[]{:S(2)}, u32[]{:S(2)}) %collective-permute-start.5) | collective-permute-done | bytes 524320 | tf_op jit(solution)/shard_map/ppermute | solution.py:434
  80.6 3.2 collective-permute-done.7.refs_8_
  85.5 9.6 %collective-permute-done.58.refs_5_ = bf16[64,4096]{1,0:T(8,128)(2,1)} collective-permute-done((bf16[64,4096]{1,0:T(8,128)(2,1)}, bf16[64,4096]{1,0:T(8,128)(2,1)}, u32[]{:S(2)}, u32[]{:S(2)}) %collective-permute-start.58) | collective-permute-done | bytes 524320 | tf_op jit(solution)/shard_map/ppermute | solution.py:434
  95.7 10.7 %collective-permute-done.59.refs_6_ = bf16[64,4096]{1,0:T(8,128)(2,1)} collective-permute-done((bf16[64,4096]{1,0:T(8,128)(2,1)}, bf16[64,4096]{1,0:T(8,128)(2,1)}, u32[]{:S(2)}, u32[]{:S(2)}) %collective-permute-start.59) | collective-permute-done | bytes 524320 | tf_op jit(solution)/shard_map/ppermute | solution.py:434
  107.0 10.5 %collective-permute-done.8.refs_0_.refs_9_ = bf16[64,4096]{1,0:T(8,128)(2,1)S(1)} collective-permute-done((bf16[64,4096]{1,0:T(8,128)(2,1)}, bf16[64,4096]{1,0:T(8,128)(2,1)S(1)}, u32[]{:S(2)}, u32[]{:S(2)}) %collective-permute-start.8) | collective-permute-done | bytes 524320 | tf_op jit(solution)/shard_map/ppermute | solution.py:434
  118.1 5.8 %collective-permute-done.9.refs_1_.refs_10_ = bf16[64,4096]{1,0:T(8,128)(2,1)S(1)} collective-permute-done((bf16[64,4096]{1,0:T(8,128)(2,1)}, bf16[64,4096]{1,0:T(8,128)(2,1)S(1)}, u32[]{:S(2)}, u32[]{:S(2)}) %collective-permute-start.9) | collective-permute-done | bytes 524320 | tf_op jit(solution)/shard_map/ppermute | solution.py:434
  124.8 27.8 %collective-permute-done.16.refs_17_ = bf16[4096,256]{1,0:T(8,128)(2,1)} collective-permute-done((bf16[4096,256]{1,0:T(8,128)(2,1)}, bf16[4096,256]{1,0:T(8,128)(2,1)}, u32[]{:S(2)}, u32[]{:S(2)}) %collective-permute-start.16) | collective-permute-done | bytes 2097184 | tf_op jit(solution)/shard_map/ppermute | solution.py:434
  156.6 32.9 %collective-permute-done.19.refs_15_ = bf16[4096,256]{1,0:T(8,128)(2,1)} collective-permute-done((bf16[4096,256]{1,0:T(8,128)(2,1)}, bf16[4096,256]{1,0:T(8,128)(2,1)}, u32[]{:S(2)}, u32[]{:S(2)}) %collective-permute-start.19) | collective-permute-done | bytes 2097184 | tf_op jit(solution)/shard_map/ppermute | solution.py:434
  195.4 14.5 %shard_map.122.refs_0_.refs_12_ = bf16[640,768]{1,0:T(8,128)(2,1)} custom-call(bf16[128,4096]{1,0:T(8,128)(2,1)} %refs_0_.7, bf16[64,4096]{1,0:T(8,128)(2,1)} %collective-permute-done.refs_1_, bf16[64,4096]{1,0:T(8,128)(2,1)} %collective-permute-done.1.refs_2_, bf16[64,4096]{1,0:T(8,128)(2,1)} %copy-done.29, ...), custom_call_target="tpu_custom_call" | custom-call | flops 8053063680 | bytes 983040 | tf_op jit(solution)/shard_map/pallas_call | solution.py:246
  209.9 10.3 %shard_map.123.refs_1_.refs_9_ = bf16[384,768]{1,0:T(8,128)(2,1)} custom-call(bf16[64,4096]{1,0:T(8,128)(2,1)} %copy-done.31, bf16[64,4096]{1,0:T(8,128)(2,1)} %copy-done.32, bf16[64,4096]{1,0:T(8,128)(2,1)} %collective-permute-done.10.refs_2_.refs_11_, bf16[64,4096]{1,0:T(8,128)(2,1)} %collective-permute-done.11.refs_3_.refs_12_, ...), custom_call_target="tpu_custom_call" | custom-call | flops 4831838208 | bytes 589824 | tf_op jit(solution)/shard_map/pallas_call | solution.py:246
  222.9 24.5 %collective-permute-done.34.refs_5_.refs_16_ = bf16[384,1536]{1,0:T(8,128)(2,1)} collective-permute-done((bf16[384,1536]{1,0:T(8,128)(2,1)}, bf16[384,1536]{1,0:T(8,128)(2,1)}, u32[]{:S(2)}, u32[]{:S(2)}) %collective-permute-start.34) | collective-permute-done | bytes 1179680 | tf_op jit(solution)/shard_map/ppermute | solution.py:434
  247.9 14.9 %shard_map.124.refs_2_.refs_23_ = bf16[1024,512]{1,0:T(8,128)(2,1)} custom-call(bf16[128,4096]{1,0:T(8,128)(2,1)} %refs_0_.7, bf16[64,4096]{1,0:T(8,128)(2,1)} %collective-permute-done.refs_1_, bf16[64,4096]{1,0:T(8,128)(2,1)} %collective-permute-done.1.refs_2_, bf16[64,4096]{1,0:T(8,128)(2,1)} %copy-done.29, ...), custom_call_target="tpu_custom_call" | custom-call | flops 8589934592 | bytes 1048576 | tf_op jit(solution)/shard_map/pallas_call | solution.py:246
  263.2 9.8 %shard_map.125.refs_3_.refs_24_ = bf16[1024,256]{1,0:T(8,128)(2,1)} custom-call(bf16[128,4096]{1,0:T(8,128)(2,1)} %refs_0_.7, bf16[64,4096]{1,0:T(8,128)(2,1)} %collective-permute-done.refs_1_, bf16[64,4096]{1,0:T(8,128)(2,1)} %collective-permute-done.1.refs_2_, bf16[64,4096]{1,0:T(8,128)(2,1)} %copy-done.29, ...), custom_call_target="tpu_custom_call" | custom-call | flops 4294967296 | bytes 524288 | tf_op jit(solution)/shard_map/pallas_call | solution.py:246
  275.7 7.5 %shard_map.134 = (bf16[128,1024]{1,0:T(8,128)(2,1)}, bf16[128,1024]{1,0:T(8,128)(2,1)}, bf16[128,1024]{1,0:T(8,128)(2,1)}, bf16[128,1024]{1,0:T(8,128)(2,1)}, bf...) custom-call(bf16[640,768]{1,0:T(8,128)(2,1)} %shard_map.122.refs_0_., ...), custom_call_target="tpu_custom_call" | custom-call | flops 3221225472 | bytes 2097152 | tf_op jit(solution)/shard_map/pallas_call | solution.py:331
  285.3 9.4 %shard_map.126 = (bf16[128,1536]{1,0:T(8,128)(2,1)}, bf16[128,1536]{1,0:T(8,128)(2,1)}, bf16[128,1536]{1,0:T(8,128)(2,1)}, bf16[128,1536]{1,0:T(8,128)(2,1)}, bf...) custom-call(bf16[640,768]{1,0:T(8,128)(2,1)} %shard_map.122.refs_0_., ...), custom_call_target="tpu_custom_call" | custom-call | flops 4831838208 | bytes 3145728 | tf_op jit(solution)/shard_map/pallas_call | solution.py:331
  300.1 10.0 %shard_map.139 = f32[1,768]{1,0:T(1,128)} custom-call(bf16[128,4096]{1,0:T(8,128)(2,1)} %refs_0_.9, bf16[64,4096]{1,0:T(8,128)(2,1)} %collective-permute-done.54.refs_1_, bf16[64,4096]{1,0:T(8,128)(2,1)} %copy-done.28, bf16[64,4096]{1,0:T(8,128)(2,1)} %collective-permute-done.56.refs_3_, bf16[64,4096]{1,0:T(8,128)(2,1)} %collective-permute-done.57.refs_4_, ...), custom_call_target="tpu_custom_call" | custom-call | flops 4026531840 | bytes 3072 | tf_op jit(solution)/shard_map/pallas_call | solution.py:246
  310.1 13.6 %collective-permute-done.26.ahead_ref = bf16[64,1536]{1,0:T(8,128)(2,1)S(1)} collective-permute-done((bf16[64,1536]{1,0:T(8,128)(2,1)}, bf16[64,1536]{1,0:T(8,128)(2,1)S(1)}, u32[]{:S(2)}, u32[]{:S(2)}) %collective-permute-start.26) | collective-permute-done | bytes 196640 | tf_op jit(solution)/shard_map/ppermute | solution.py:434
  324.9 9.5 %shard_map.130 = (bf16[128,1536]{1,0:T(8,128)(2,1)}, bf16[128,1536]{1,0:T(8,128)(2,1)}, bf16[128,1536]{1,0:T(8,128)(2,1)}, bf16[128,1536]{1,0:T(8,128)(2,1)}, bf...) custom-call(bf16[640,768]{1,0:T(8,128)(2,1)} %shard_map.122.refs_0_., ...), custom_call_target="tpu_custom_call" | custom-call | flops 4831838208 | bytes 3145728 | tf_op jit(solution)/shard_map/pallas_call | solution.py:331
  342.1 14.2 %shard_map.141 = f32[1,768]{1,0:T(1,128)} custom-call(bf16[128,4096]{1,0:T(8,128)(2,1)} %refs_0_.9, bf16[64,4096]{1,0:T(8,128)(2,1)} %collective-permute-done.54.refs_1_, bf16[64,4096]{1,0:T(8,128)(2,1)} %copy-done.28, bf16[64,4096]{1,0:T(8,128)(2,1)} %collective-permute-done.56.refs_3_, bf16[64,4096]{1,0:T(8,128)(2,1)} %collective-permute-done.57.refs_4_, ...), custom_call_target="tpu_custom_call" | custom-call | flops 6442450944 | bytes 3072 | tf_op jit(solution)/shard_map/pallas_call | solution.py:246
  364.0 4.3 %collective-permute-done.29.behind_ref = bf16[128,1536]{1,0:T(8,128)(2,1)S(1)} collective-permute-done((bf16[128,1536]{1,0:T(8,128)(2,1)S(1)}, bf16[128,1536]{1,0:T(8,128)(2,1)S(1)}, u32[]{:S(2)}, u32[]{:S(2)}) %collective-permute-start.29) | collective-permute-done | bytes 393248 | tf_op jit(solution)/shard_map/ppermute | solution.py:434
  372.4 4.4 %collective-permute-done.39.behind_ref = bf16[128,1536]{1,0:T(8,128)(2,1)S(1)} collective-permute-done((bf16[128,1536]{1,0:T(8,128)(2,1)S(1)}, bf16[128,1536]{1,0:T(8,128)(2,1)S(1)}, u32[]{:S(2)}, u32[]{:S(2)}) %collective-permute-start.39) | collective-permute-done | bytes 393248 | tf_op jit(solution)/shard_map/ppermute | solution.py:434
  383.3 7.8 %shard_map.140 = f32[1,768]{1,0:T(1,128)} custom-call(bf16[64,4096]{1,0:T(8,128)(2,1)} %collective-permute-done.62.refs_0_.refs_9_, bf16[64,4096]{1,0:T(8,128)(2,1)} %collective-permute-done.63.refs_1_.refs_10_, bf16[64,4096]{1,0:T(8,128)(2,1)} %collective-permute-done.64.refs_2_.refs_11_, bf16[64,4096]{1,0:T(8,128)(2,1)} %collective-permute-done.65.refs_3_.refs_12_, ...), custom_call_target="tpu_custom_call" | custom-call | flops 2415919104 | bytes 3072 | tf_op jit(solution)/shard_map/pallas_call | solution.py:246
  401.0 19.5 %collective-permute-done.53.refs_8_ = bf16[128,1024]{1,0:T(8,128)(2,1)S(1)} collective-permute-done((bf16[128,1024]{1,0:T(8,128)(2,1)S(1)}, bf16[128,1024]{1,0:T(8,128)(2,1)S(1)}, u32[]{:S(2)}, u32[]{:S(2)}) %collective-permute-start.53) | collective-permute-done | bytes 262176 | tf_op jit(solution)/shard_map/ppermute | solution.py:434
  (242 shorter events, 96.2 us)
Async XLA Ops:
  6.9 29.5 %collective-permute-start = (bf16[64,4096]{1,0:T(8,128)(2,1)S(1)}, bf16[64,4096]{1,0:T(8,128)(2,1)}, u32[]{:S(2)}, u32[]{:S(2)}) collective-permute-start(bf16[64,4096]{1,0:T(8,128)(2,1)S(1)} %get-tuple-element.103), channel_id=1, source_target_pairs={{0,4},{4,8},{8,12},{12,14},{14,10},{10,6},{6,2},{2,0},{1,5},{5,9},... | collective-permute-start | bytes 1572872 | tf_op jit(solution)/shard_map/ppermute | solution.py:434
  8.5 31.5 %collective-permute-start.2 = (bf16[64,4096]{1,0:T(8,128)(2,1)S(1)}, bf16[64,4096]{1,0:T(8,128)(2,1)S(1)}, u32[]{:S(2)}, u32[]{:S(2)}) collective-permute-start(bf16[64,4096]{1,0:T(8,128)(2,1)S(1)} %get-tuple-element.103), channel_id=1, source_target_pairs={{0,2},{4,0},{8,4},{12,8},{14,12},{10,14},{6,10},{2,6},{1,3},{5,1},... | collective-permute-start | bytes 1572872 | tf_op jit(solution)/shard_map/ppermute | solution.py:434
  9.7 28.2 %collective-permute-start.1 = (bf16[64,4096]{1,0:T(8,128)(2,1)S(1)}, bf16[64,4096]{1,0:T(8,128)(2,1)}, u32[]{:S(2)}, u32[]{:S(2)}) collective-permute-start(bf16[64,4096]{1,0:T(8,128)(2,1)S(1)} %get-tuple-element.102), channel_id=1, source_target_pairs={{0,4},{4,8},{8,12},{12,14},{14,10},{10,6},{6,2},{2,0},{1,5},{5,9},... | collective-permute-start | bytes 1572872 | tf_op jit(solution)/shard_map/ppermute | solution.py:434
  10.5 29.5 %collective-permute-start.3 = (bf16[64,4096]{1,0:T(8,128)(2,1)S(1)}, bf16[64,4096]{1,0:T(8,128)(2,1)}, u32[]{:S(2)}, u32[]{:S(2)}) collective-permute-start(bf16[64,4096]{1,0:T(8,128)(2,1)S(1)} %get-tuple-element.102), channel_id=1, source_target_pairs={{0,2},{4,0},{8,4},{12,8},{14,12},{10,14},{6,10},{2,6},{1,3},{5,1},... | collective-permute-start | bytes 1572872 | tf_op jit(solution)/shard_map/ppermute | solution.py:434
  36.3 27.2 %collective-permute-start.44 = (bf16[384,1024]{1,0:T(8,128)(2,1)}, bf16[384,1024]{1,0:T(8,128)(2,1)S(1)}, u32[]{:S(2)}, u32[]{:S(2)}) collective-permute-start(bf16[384,1024]{1,0:T(8,128)(2,1)} %get-tuple-element.82), channel_id=1, source_target_pairs={{0,1},{1,0},{2,3},{3,2},{4,5},{5,4},{6,7},{7,6},{8,9},{9,8},{10,11... | collective-permute-start | bytes 2359304 | tf_op jit(solution)/shard_map/ppermute | solution.py:434
  40.1 23.1 %collective-permute-start.57 = (bf16[64,4096]{1,0:T(8,128)(2,1)}, bf16[64,4096]{1,0:T(8,128)(2,1)}, u32[]{:S(2)}, u32[]{:S(2)}) collective-permute-start(bf16[64,4096]{1,0:T(8,128)(2,1)} %get-tuple-element.100), channel_id=1, source_target_pairs={{0,2},{4,0},{8,4},{12,8},{14,12},{10,14},{6,10},{2,6},{1,3},{5,1},... | collective-permute-start | bytes 1572872 | tf_op jit(solution)/shard_map/ppermute | solution.py:434
  59.1 65.7 %collective-permute-start.14 = (bf16[4096,256]{1,0:T(8,128)(2,1)S(1)}, bf16[4096,256]{1,0:T(8,128)(2,1)}, u32[]{:S(2)}, u32[]{:S(2)}) collective-permute-start(bf16[4096,256]{1,0:T(8,128)(2,1)S(1)} %copy-done.22), channel_id=1, source_target_pairs={{0,1},{1,0},{2,3},{3,2},{4,5},{5,4},{6,7},{7,6},{8,9},{9,8},{10,11... | collective-permute-start | bytes 6291464 | tf_op jit(solution)/shard_map/ppermute | solution.py:434
  60.6 92.1 %collective-permute-start.16 = (bf16[4096,256]{1,0:T(8,128)(2,1)}, bf16[4096,256]{1,0:T(8,128)(2,1)}, u32[]{:S(2)}, u32[]{:S(2)}) collective-permute-start(bf16[4096,256]{1,0:T(8,128)(2,1)} %cut_columns.4), channel_id=1, source_target_pairs={{0,1},{1,0},{2,3},{3,2},{4,5},{5,4},{6,7},{7,6},{8,9},{9,8},{10,11... | collective-permute-start | bytes 6291464 | tf_op jit(solution)/shard_map/ppermute | solution.py:434
  78.0 111.5 %collective-permute-start.19 = (bf16[4096,256]{1,0:T(8,128)(2,1)}, bf16[4096,256]{1,0:T(8,128)(2,1)}, u32[]{:S(2)}, u32[]{:S(2)}) collective-permute-start(bf16[4096,256]{1,0:T(8,128)(2,1)} %cut_columns.5), channel_id=1, source_target_pairs={{0,1},{1,0},{2,3},{3,2},{4,5},{5,4},{6,7},{7,6},{8,9},{9,8},{10,11... | collective-permute-start | bytes 6291464 | tf_op jit(solution)/shard_map/ppermute | solution.py:434
  83.8 22.6 %collective-permute-start.59 = (bf16[64,4096]{1,0:T(8,128)(2,1)}, bf16[64,4096]{1,0:T(8,128)(2,1)}, u32[]{:S(2)}, u32[]{:S(2)}) collective-permute-start(bf16[64,4096]{1,0:T(8,128)(2,1)} %copy-done.28), channel_id=1, source_target_pairs={{0,4},{4,8},{8,12},{12,14},{14,10},{10,6},{6,2},{2,0},{1,5},{5,9},... | collective-permute-start | bytes 1572872 | tf_op jit(solution)/shard_map/ppermute | solution.py:434
  117.5 36.8 %collective-permute-start.10 = (bf16[64,4096]{1,0:T(8,128)(2,1)}, bf16[64,4096]{1,0:T(8,128)(2,1)}, u32[]{:S(2)}, u32[]{:S(2)}) collective-permute-start(bf16[64,4096]{1,0:T(8,128)(2,1)} %collective-permute-done.6.refs_7_), channel_id=1, source_target_pairs={{0,2},{4,0},{8,4},{12,8},{14,12},{10,14},{6,10},{2,6},{1,3},{5,1},... | collective-permute-start | bytes 1572872 | tf_op jit(solution)/shard_map/ppermute | solution.py:434
  123.9 31.0 %collective-permute-start.11 = (bf16[64,4096]{1,0:T(8,128)(2,1)}, bf16[64,4096]{1,0:T(8,128)(2,1)}, u32[]{:S(2)}, u32[]{:S(2)}) collective-permute-start(bf16[64,4096]{1,0:T(8,128)(2,1)} %collective-permute-done.7.refs_8_), channel_id=1, source_target_pairs={{0,2},{4,0},{8,4},{12,8},{14,12},{10,14},{6,10},{2,6},{1,3},{5,1},... | collective-permute-start | bytes 1572872 | tf_op jit(solution)/shard_map/ppermute | solution.py:434
  124.8 122.5 %collective-permute-start.15 = (bf16[4096,256]{1,0:T(8,128)(2,1)}, bf16[4096,256]{1,0:T(8,128)(2,1)}, u32[]{:S(2)}, u32[]{:S(2)}) collective-permute-start(bf16[4096,256]{1,0:T(8,128)(2,1)} %collective-permute-done.14.refs_15_), channel_id=1, source_target_pairs={{0,16},{16,0},{1,17},{17,1},{2,18},{18,2},{3,19},{19,3},{4,20},{20... | collective-permute-start | bytes 6291464 | tf_op jit(solution)/shard_map/ppermute | solution.py:437
  152.7 95.2 %collective-permute-start.17 = (bf16[4096,256]{1,0:T(8,128)(2,1)}, bf16[4096,256]{1,0:T(8,128)(2,1)}, u32[]{:S(2)}, u32[]{:S(2)}) collective-permute-start(bf16[4096,256]{1,0:T(8,128)(2,1)} %collective-permute-done.16.refs_17_), channel_id=1, source_target_pairs={{0,16},{16,0},{1,17},{17,1},{2,18},{18,2},{3,19},{19,3},{4,20},{20... | collective-permute-start | bytes 6291464 | tf_op jit(solution)/shard_map/ppermute | solution.py:437
  154.4 39.0 %collective-permute-start.12 = (bf16[64,4096]{1,0:T(8,128)(2,1)}, bf16[64,4096]{1,0:T(8,128)(2,1)S(1)}, u32[]{:S(2)}, u32[]{:S(2)}) collective-permute-start(bf16[64,4096]{1,0:T(8,128)(2,1)} %copy-done.31), channel_id=1, source_target_pairs={{0,4},{4,8},{8,12},{12,14},{14,10},{10,6},{6,2},{2,0},{1,5},{5,9},... | collective-permute-start | bytes 1572872 | tf_op jit(solution)/shard_map/ppermute | solution.py:434
  154.9 40.0 %collective-permute-start.13 = (bf16[64,4096]{1,0:T(8,128)(2,1)}, bf16[64,4096]{1,0:T(8,128)(2,1)S(1)}, u32[]{:S(2)}, u32[]{:S(2)}) collective-permute-start(bf16[64,4096]{1,0:T(8,128)(2,1)} %collective-permute-done.11.refs_3_.refs_12_), channel_id=1, source_target_pairs={{0,2},{4,0},{8,4},{12,8},{14,12},{10,14},{6,10},{2,6},{1,3},{5,1},... | collective-permute-start | bytes 1572872 | tf_op jit(solution)/shard_map/ppermute | solution.py:434
  189.4 73.4 %collective-permute-start.20 = (bf16[4096,256]{1,0:T(8,128)(2,1)}, bf16[4096,256]{1,0:T(8,128)(2,1)}, u32[]{:S(2)}, u32[]{:S(2)}) collective-permute-start(bf16[4096,256]{1,0:T(8,128)(2,1)} %collective-permute-done.19.refs_15_), channel_id=1, source_target_pairs={{0,16},{16,0},{1,17},{17,1},{2,18},{18,2},{3,19},{19,3},{4,20},{20... | collective-permute-start | bytes 6291464 | tf_op jit(solution)/shard_map/ppermute | solution.py:437
  193.4 29.2 %collective-permute-start.21 = (bf16[384,1536]{1,0:T(8,128)(2,1)}, bf16[384,1536]{1,0:T(8,128)(2,1)}, u32[]{:S(2)}, u32[]{:S(2)}) collective-permute-start(bf16[384,1536]{1,0:T(8,128)(2,1)} %get-tuple-element.50), channel_id=1, source_target_pairs={{0,1},{1,0},{2,3},{3,2},{4,5},{5,4},{6,7},{7,6},{8,9},{9,8},{10,11... | collective-permute-start | bytes 3538952 | tf_op jit(solution)/shard_map/ppermute | solution.py:434
  194.9 52.5 %collective-permute-start.34 = (bf16[384,1536]{1,0:T(8,128)(2,1)}, bf16[384,1536]{1,0:T(8,128)(2,1)}, u32[]{:S(2)}, u32[]{:S(2)}) collective-permute-start(bf16[384,1536]{1,0:T(8,128)(2,1)} %get-tuple-element.66), channel_id=1, source_target_pairs={{0,1},{1,0},{2,3},{3,2},{4,5},{5,4},{6,7},{7,6},{8,9},{9,8},{10,11... | collective-permute-start | bytes 3538952 | tf_op jit(solution)/shard_map/ppermute | solution.py:434
  222.5 50.5 %collective-permute-start.61 = (bf16[64,4096]{1,0:T(8,128)(2,1)}, bf16[64,4096]{1,0:T(8,128)(2,1)S(1)}, u32[]{:S(2)}, u32[]{:S(2)}) collective-permute-start(bf16[64,4096]{1,0:T(8,128)(2,1)} %collective-permute-done.57.refs_4_), channel_id=1, source_target_pairs={{0,2},{4,0},{8,4},{12,8},{14,12},{10,14},{6,10},{2,6},{1,3},{5,1},... | collective-permute-start | bytes 1572872 | tf_op jit(solution)/shard_map/ppermute | solution.py:434
  247.3 27.5 %collective-permute-start.45 = (bf16[384,1024]{1,0:T(8,128)(2,1)S(1)}, bf16[384,1024]{1,0:T(8,128)(2,1)S(1)}, u32[]{:S(2)}, u32[]{:S(2)}) collective-permute-start(bf16[384,1024]{1,0:T(8,128)(2,1)S(1)} %collective-permute-done.44.refs_5_.refs_17_), channel_id=1, source_target_pairs={{0,16},{16,0},{1,17},{17,1},{2,18},{18,2},{3,19},{19,3},{4,20},{20... | collective-permute-start | bytes 2359304 | tf_op jit(solution)/shard_map/ppermute | solution.py:437
  247.4 37.1 %collective-permute-start.22 = (bf16[384,1536]{1,0:T(8,128)(2,1)}, bf16[384,1536]{1,0:T(8,128)(2,1)}, u32[]{:S(2)}, u32[]{:S(2)}) collective-permute-start(bf16[384,1536]{1,0:T(8,128)(2,1)} %collective-permute-done.21.refs_5_.refs_15_), channel_id=1, source_target_pairs={{0,16},{16,0},{1,17},{17,1},{2,18},{18,2},{3,19},{19,3},{4,20},{20... | collective-permute-start | bytes 3538952 | tf_op jit(solution)/shard_map/ppermute | solution.py:437
  247.9 49.0 %collective-permute-start.35 = (bf16[384,1536]{1,0:T(8,128)(2,1)}, bf16[384,1536]{1,0:T(8,128)(2,1)}, u32[]{:S(2)}, u32[]{:S(2)}) collective-permute-start(bf16[384,1536]{1,0:T(8,128)(2,1)} %collective-permute-done.34.refs_5_.refs_16_), channel_id=1, source_target_pairs={{0,16},{16,0},{1,17},{17,1},{2,18},{18,2},{3,19},{19,3},{4,20},{20... | collective-permute-start | bytes 3538952 | tf_op jit(solution)/shard_map/ppermute | solution.py:437
  294.8 43.0 %collective-permute-start.63 = (bf16[64,4096]{1,0:T(8,128)(2,1)}, bf16[64,4096]{1,0:T(8,128)(2,1)}, u32[]{:S(2)}, u32[]{:S(2)}) collective-permute-start(bf16[64,4096]{1,0:T(8,128)(2,1)} %collective-permute-done.59.refs_6_), channel_id=1, source_target_pairs={{0,4},{4,8},{8,12},{12,14},{14,10},{10,6},{6,2},{2,0},{1,5},{5,9},... | collective-permute-start | bytes 1572872 | tf_op jit(solution)/shard_map/ppermute | solution.py:434
  296.0 42.8 %collective-permute-start.64 = (bf16[64,4096]{1,0:T(8,128)(2,1)}, bf16[64,4096]{1,0:T(8,128)(2,1)}, u32[]{:S(2)}, u32[]{:S(2)}) collective-permute-start(bf16[64,4096]{1,0:T(8,128)(2,1)} %collective-permute-done.60.refs_7_), channel_id=1, source_target_pairs={{0,2},{4,0},{8,4},{12,8},{14,12},{10,14},{6,10},{2,6},{1,3},{5,1},... | collective-permute-start | bytes 1572872 | tf_op jit(solution)/shard_map/ppermute | solution.py:434
  296.9 43.1 %collective-permute-start.66 = (bf16[64,4096]{1,0:T(8,128)(2,1)}, bf16[64,4096]{1,0:T(8,128)(2,1)}, u32[]{:S(2)}, u32[]{:S(2)}) collective-permute-start(bf16[64,4096]{1,0:T(8,128)(2,1)} %collective-permute-done.62.refs_0_.refs_9_), channel_id=1, source_target_pairs={{0,4},{4,8},{8,12},{12,14},{14,10},{10,6},{6,2},{2,0},{1,5},{5,9},... | collective-permute-start | bytes 1572872 | tf_op jit(solution)/shard_map/ppermute | solution.py:434
  298.0 42.8 %collective-permute-start.67 = (bf16[64,4096]{1,0:T(8,128)(2,1)}, bf16[64,4096]{1,0:T(8,128)(2,1)}, u32[]{:S(2)}, u32[]{:S(2)}) collective-permute-start(bf16[64,4096]{1,0:T(8,128)(2,1)} %collective-permute-done.65.refs_3_.refs_12_), channel_id=1, source_target_pairs={{0,2},{4,0},{8,4},{12,8},{14,12},{10,14},{6,10},{2,6},{1,3},{5,1},... | collective-permute-start | bytes 1572872 | tf_op jit(solution)/shard_map/ppermute | solution.py:434
  298.9 24.7 %collective-permute-start.26 = (bf16[64,1536]{1,0:T(8,128)(2,1)}, bf16[64,1536]{1,0:T(8,128)(2,1)S(1)}, u32[]{:S(2)}, u32[]{:S(2)}) collective-permute-start(bf16[64,1536]{1,0:T(8,128)(2,1)} %get-tuple-element.58), channel_id=1, source_target_pairs={{0,4},{4,8},{8,12},{12,14},{14,10},{10,6},{6,2},{2,0},{1,5},{5,9},... | collective-permute-start | bytes 589832 | tf_op jit(solution)/shard_map/ppermute | solution.py:434
  368.3 23.1 %collective-permute-start.68 = (f32[1,768]{1,0:T(1,128)S(1)}, f32[1,768]{1,0:T(1,128)S(1)}, u32[]{:S(2)}, u32[]{:S(2)}) collective-permute-start(f32[1,768]{1,0:T(1,128)S(1)} %broadcast_select_fusion.1), channel_id=1, source_target_pairs={{0,1},{1,0},{2,3},{3,2},{4,5},{5,4},{6,7},{7,6},{8,9},{9,8},{10,11... | collective-permute-start | bytes 9224 | tf_op jit(solution)/shard_map/ppermute | solution.py:434
  394.4 26.2 %collective-permute-start.32 = (bf16[128,1536]{1,0:T(8,128)(2,1)S(1)}, bf16[128,1536]{1,0:T(8,128)(2,1)S(1)}, u32[]{:S(2)}, u32[]{:S(2)}) collective-permute-start(bf16[128,1536]{1,0:T(8,128)(2,1)S(1)} %get-tuple-element.64), channel_id=1, source_target_pairs={{0,4},{4,8},{8,12},{12,14},{14,10},{10,6},{6,2},{2,0},{1,5},{5,9},... | collective-permute-start | bytes 1179656 | tf_op jit(solution)/shard_map/ppermute | solution.py:434
  395.3 25.3 %collective-permute-start.33 = (bf16[128,1536]{1,0:T(8,128)(2,1)S(1)}, bf16[128,1536]{1,0:T(8,128)(2,1)S(1)}, u32[]{:S(2)}, u32[]{:S(2)}) collective-permute-start(bf16[128,1536]{1,0:T(8,128)(2,1)S(1)} %get-tuple-element.65), channel_id=1, source_target_pairs={{0,2},{4,0},{8,4},{12,8},{14,12},{10,14},{6,10},{2,6},{1,3},{5,1},... | collective-permute-start | bytes 1179656 | tf_op jit(solution)/shard_map/ppermute | solution.py:434
  397.4 23.1 %collective-permute-start.42 = (bf16[128,1536]{1,0:T(8,128)(2,1)S(1)}, bf16[128,1536]{1,0:T(8,128)(2,1)S(1)}, u32[]{:S(2)}, u32[]{:S(2)}) collective-permute-start(bf16[128,1536]{1,0:T(8,128)(2,1)S(1)} %get-tuple-element.80), channel_id=1, source_target_pairs={{0,4},{4,8},{8,12},{12,14},{14,10},{10,6},{6,2},{2,0},{1,5},{5,9},... | collective-permute-start | bytes 1179656 | tf_op jit(solution)/shard_map/ppermute | solution.py:434
  (76 other events, 1431.3 us)
